TPU v7x, 256 devices: a whole 4x4x8 slice. The times are simulated.
256 devices in a mesh: sec: 16 (over y, x), own: 16 (over z, core).
Axes of the slice: x: 4, y: 4, z: 8, core: 2. Of those that a mesh axis runs over, the one named last changes fastest.
Arguments:
- right_sides: float32 [2, 128, 65536], P(None, None, ('sec', 'own')), may hold values from -6 to 6
- inv_diag: float32 [65536, 256], P(('sec', 'own')), may hold values from -1 to 2, as said below
- factor_tiles: bfloat16 [65536, 4096], P(('sec', 'own')), may hold values from -0.046875 to 0.046875
- structure: int32 [256, 16], P(('sec', 'own')), may hold values 0 or 1
- ancestor: int32 [16, 16], P('sec'), may hold values from 0 to 15, each once within a row
- carried: float32 [128, 65536], P(None, ('sec', 'own')), may hold values from -4 to 4
Outputs:
- solution: float32 [2, 128, 65536], P(None, None, ('sec', 'own'))
- carry_out: float32 [128, 65536], P(None, ('sec', 'own'))
Inputs may be any that keep to these rules, and one draw needn't show every extreme that they name: `inv_diag`: each diagonal block is the identity plus a dense part of moderate size. `ancestor`: each row is a permutation of 0 to 15.
All inputs are finite; a program needn't handle non-finite values. No bound on the sum of `structure` on one device may be relied on, other than what follows from the above.
Results may differ from a plain program's by a relative error of at most 0.0003.
Values sent between devices are 32-bit elements; how exact they have to be, the bound alone decides.
No kernel may reach another device: no remote copies, remote signals or barrier semaphores. Data moves between devices by JAX's collectives and lax.ppermute only.
A program may use at most 64 MiB of HBM per device.

v0:
```python
import functools

import jax
import jax.numpy as jnp
from jax import lax
from jax.experimental import pallas as pl
from jax.experimental.pallas import tpu as pltpu
from jax.sharding import PartitionSpec as P


STREAMS = 2


def split(value):
    high = value.astype(jnp.bfloat16)
    return high, (value - high.astype(jnp.float32)).astype(jnp.bfloat16)


def dot(a, b):
    return jnp.dot(a, b, preferred_element_type=jnp.float32)


def product(table, lhs, factor, place, distance, to_core):
    chips, chip = place
    rows, block = lhs.shape[0] // 2, lhs.shape[1]
    target = ((chip + distance + chips) % chips) * 2 + to_core
    start = pl.multiple_of(table[0, target] * block, block)
    both = dot(lhs, factor[:, pl.ds(start, block)])
    return (both[:rows] + both[rows:]) * table[1, target].astype(jnp.float32)


def position(chips):
    me = lax.axis_index("own")
    chip, core = me // 2, me % 2
    return (chips, chip), core, 1 - 2 * ((chip + core) % 2)


def solve(residual, inverse_high, inverse_low):
    rows = residual.shape[0]
    high, low = split(residual)
    both = dot(jnp.concatenate([high, low], axis=0), inverse_high)
    result = both[:rows] + both[rows:] + dot(high, inverse_low)
    return result, jnp.concatenate(split(result), axis=0)


def parts_of_step(chips, step):
    _, core, ahead = position(chips)
    last = chips // 2 - 1 - step
    up, down = last, -last - 1
    mine = jnp.where(ahead == 1, up, down)
    other = up + down - mine
    for give, distance, first in (
        (True, other, (core + 1 + other) % 2),
        (False, mine, (core + mine) % 2),
    ):
        yield give, 0, distance, (first + 2) % 2
        yield give, 1, distance, (3 - first) % 2


def put_step(table, lhs, factor, chips, step, give, keep, offset):
    rows = keep[0].shape[1]
    place = position(chips)[0]
    for given, index, distance, to_core in parts_of_step(chips, step):
        whole = product(table, lhs, factor, place, distance, to_core)
        for stream, ref in enumerate(give if given else keep):
            ref[offset + index] = whole[stream * rows : (stream + 1) * rows]


def first_kernel(
    chips, streams, ancestor, structure, right_sides, carried, inverse, factor,
    table, factor_here, inverse_high, inverse_low, solved, lhs, *rest,
):
    early, keep = rest[:streams], rest[streams : 2 * streams]
    slots, present, right_here, carried_here, inverse_here, sems = rest[2 * streams :]
    copies = [
        pltpu.make_async_copy(source, target, sems.at[i])
        for i, (source, target) in enumerate(
            (
                (inverse, inverse_here),
                (right_sides.at[0], right_here),
                (carried, carried_here),
                (ancestor, slots),
                (structure, present),
                (factor, factor_here),
            )
        )
    ]
    for copy in copies:
        copy.start()
    for copy in copies[:3]:
        copy.wait()
    inverse_high[...], inverse_low[...] = split(inverse_here[...])
    solved[...], lhs[...] = solve(
        right_here[...] - carried_here[...], inverse_high[...], inverse_low[...]
    )
    copies[3].wait()
    copies[4].wait()
    for slot in range(slots.shape[1]):
        table[0, slots[0, slot]] = slot
        table[1, slots[0, slot]] = present[0, slot]
    copies[5].wait()
    put_step(table, lhs[...], factor_here, chips, 0, early, keep, 0)


def next_kernel(
    chips, tick, first_row, table, right_sides, moving, crossed,
    inverse_high, inverse_low, factor, solved, lhs, early, keep,
):
    here = pl.ds(first_row, solved.shape[0])
    incoming = moving[0] + crossed[...]
    incoming = jnp.where(lax.axis_index("sec") == 0, 0.0, incoming)
    solved[...], lhs[...] = solve(
        right_sides[tick, here] - incoming, inverse_high[...], inverse_low[...]
    )
    put_step(table, lhs[...], factor, chips, 0, [early], [keep], 0)


def late_kernel(chips, streams, table, lhs, factor, *outs):
    give, keep = outs[:streams], outs[streams:]
    value = lhs[...]
    for step in range(1, chips // 2):
        put_step(table, value, factor, chips, step, give, keep, 2 * (step - 1))


VMEM = pl.BlockSpec(memory_space=pltpu.VMEM)
SMEM = pl.BlockSpec(memory_space=pltpu.SMEM)
HBM = pl.BlockSpec(memory_space=pltpu.HBM)
F32 = functools.partial(jax.ShapeDtypeStruct, dtype=jnp.float32)
BF16 = functools.partial(jax.ShapeDtypeStruct, dtype=jnp.bfloat16)


def call(kernel, products, in_specs, outs, limit, scratch=()):
    return pl.pallas_call(
        kernel,
        out_shape=outs,
        in_specs=in_specs,
        out_specs=[SMEM if out.dtype == jnp.int32 else VMEM for out in outs],
        scratch_shapes=list(scratch),
        compiler_params=pltpu.CompilerParams(vmem_limit_bytes=limit << 20),
        cost_estimate=pl.CostEstimate(
            flops=products * 2 * 256 * 256 * 256,
            bytes_accessed=products * 65536 * 2,
            transcendentals=0,
        ),
    )


def first_step(chips, streams, rows, arrays):
    ancestor, _, _, carried, _, factor = arrays
    slots = ancestor.shape[1]
    width, block = carried.shape
    square = (block, block)
    outs = [jax.ShapeDtypeStruct((2, slots), jnp.int32), BF16(factor.shape)]
    outs += [BF16(square)] * 2 + [F32((width, block)), BF16((2 * width, block))]
    outs += [F32((2, rows, block))] * (2 * streams)
    scratch = [
        pltpu.SMEM((1, slots), jnp.int32),
        pltpu.SMEM((1, slots), jnp.int32),
        pltpu.VMEM((width, block), jnp.float32),
        pltpu.VMEM((width, block), jnp.float32),
        pltpu.VMEM(square, jnp.float32),
        pltpu.SemaphoreType.DMA((6,)),
    ]
    kernel = functools.partial(first_kernel, chips, streams)
    out = call(kernel, 6, [HBM] * 6, outs, 4, scratch)(
        *[pltpu.with_memory_space_constraint(array, pltpu.HBM) for array in arrays]
    )
    fixed, (solved, lhs) = out[:4], out[4:6]
    return fixed, solved, lhs, out[6 : 6 + streams], out[6 + streams :]


def next_step(chips, tick, first_row, fixed, right_sides, moving, crossed):
    table, factor, inverse_high, inverse_low = fixed
    rows, block = crossed.shape
    outs = [F32((rows, block)), BF16((2 * rows, block))]
    outs += [F32((2, rows, block))] * 2
    kernel = functools.partial(next_kernel, chips, tick, first_row)
    return call(kernel, 6, [SMEM] + [VMEM] * 6, outs, 4)(
        table, right_sides, moving, crossed, inverse_high, inverse_low, factor
    )


def late_step(chips, streams, fixed, lhs):
    rows, block = lhs.shape[0] // 2 // streams, lhs.shape[1]
    outs = [F32((chips - 2, rows, block))] * (2 * streams)
    kernel = functools.partial(late_kernel, chips, streams)
    out = call(kernel, 12, [SMEM, VMEM, VMEM], outs, 4)(fixed[0], lhs, fixed[1])
    return out[:streams], out[streams:]


def shards(right_sides, inv_diag, factor_tiles, structure, ancestor, carried):
    owners = lax.axis_size("own")
    sections = lax.axis_size("sec")
    chips = owners // 2
    partner = [(i, i ^ 1) for i in range(owners)]

    def next_on_chain(i):
        chip, core = i // 2, i % 2
        ahead = 1 - 2 * ((chip + core) % 2)
        return ((chip + ahead) % chips) * 2 + 1 - core

    def to_next_section(place):
        return [
            (s * owners + i, (s + 1) % sections * owners + place(i))
            for s in range(sections)
            for i in range(owners)
        ]

    chain = [(i, next_on_chain(i)) for i in range(owners)]
    upward = lambda i: (i // 2 + i) % 2 == 0
    onward = to_next_section(lambda i: i if upward(i) else next_on_chain(i))
    first_section = lax.axis_index("sec") == 0

    swap = lambda value: lax.ppermute(value, "own", partner)
    pass_on = lambda value: lax.ppermute(value, "own", chain)
    leave = lambda value: lax.ppermute(value, ("sec", "own"), onward)

    ticks, width, _ = right_sides.shape
    rows = width // STREAMS
    streams = range(STREAMS)
    solved_all = []
    for tick in range(ticks):
        if tick == 0:
            fixed, solved, lhs, gives, keeps = first_step(
                chips,
                STREAMS,
                rows,
                (ancestor, structure, right_sides, carried, inv_diag, factor_tiles),
            )
            solved_all.append(solved)
            later_gives, later_keeps = late_step(chips, STREAMS, fixed, lhs)
        else:
            gives, keeps, later_gives, later_keeps = [], [], [], []
            for stream in streams:
                solved, lhs, give, keep = next_step(
                    chips, tick, stream * rows, fixed, right_sides,
                    moving[stream], crossed[stream],
                )
                solved_all.append(solved)
                gives.append(give)
                keeps.append(keep)
                give, keep = late_step(chips, 1, fixed, lhs)
                later_gives += give
                later_keeps += keep
        moving, crossed = [], []
        for stream in streams:
            taken = swap(gives[stream])
            later = swap(later_gives[stream])
            value = keeps[stream] + taken
            for step in range(chips // 2 - 1):
                value = pass_on(value)
                part = slice(2 * step, 2 * step + 2)
                value = later_keeps[stream][part] + later[part] + value
            value = leave(value)
            moving.append(value)
            crossed.append(swap(value[1]))
    carry = jnp.concatenate([value[0] for value in moving], axis=0)
    carry = jnp.where(first_section, 0.0, carry + jnp.concatenate(crossed, axis=0))
    return jnp.concatenate(solved_all, axis=0).reshape(right_sides.shape), carry


def solution(mesh):
    in_specs = (
        P(None, None, ("sec", "own")),
        P(("sec", "own"), None),
        P(("sec", "own"), None),
        P(("sec", "own"), None),
        P("sec", None),
        P(None, ("sec", "own")),
    )
    out_specs = (P(None, None, ("sec", "own")), P(None, ("sec", "own")))
    return jax.shard_map(
        shards,
        mesh=mesh,
        in_specs=in_specs,
        out_specs=out_specs,
        check_vma=False,
    )
```

profile of v0, /device:TPU:1, one launch (start us, length us, event | category | flops | bytes accessed | tf_op | source)
XLA Modules:
  0.0 76.7 jit_solution(3189201193034008291)
XLA Ops:
  0.6 2.6 %shard_map.77 = (s32[2,16]{1,0:T(2,128)S(1)}, bf16[256,4096]{1,0:T(8,128)(2,1)S(1)}, bf16[256,256]{1,0:T(8,128)(2,1)S(1)}, bf16[256,256]{1,0:T(8,128)(2,1)S(1)},...) custom-call(s32[1,16]{1,0:T(1,128)} %ancestor.1, ...), custom_call_target="tpu_custom_call" | custom-call | flops 201326592 | bytes 786432 | tf_op jit(solution)/shard_map/pallas_call | solution.py:165
  3.2 1.2 %shard_map.78 = (f32[6,64,256]{2,1,0:T(8,128)S(1)}, f32[6,64,256]{2,1,0:T(8,128)S(1)}, f32[6,64,256]{2,1,0:T(8,128)S(1)}, f32[6,64,256]{2,1,0:T(8,128)S(1)}) custom-call(s32[2,16]{1,0:T(2,128)S(1)} %get-tuple-element.29.table, bf16[256,256]{1,0:T(8,128)(2,1)S(1)} %get-tuple-element.30.lhs, bf16[256,4096]{1,0:T(8,128)(2,1)S(1)} %get-tuple-element.31.factor), custom_call_target="tpu_custom_call" | custom-call | flops 402653184 | bytes 1572864 | tf_op jit(solution)/shard_map/pallas_call | solution.py:187
  4.4 0.0 copy-start
  4.4 3.3 %collective-permute-start.7 = (f32[6,64,256]{2,1,0:T(8,128)S(1)}, f32[6,64,256]{2,1,0:T(8,128)S(1)}, u32[]{:S(2)}, u32[]{:S(2)}) collective-permute-start(f32[6,64,256]{2,1,0:T(8,128)S(1)} %get-tuple-element.40), channel_id=1, source_target_pairs={{0,1},{1,0},{2,3},{3,2},{4,5},{5,4},{6,7},{7,6},{8,9},{9,8},{10,11... | collective-permute-start | bytes 1179656 | tf_op jit(solution)/shard_map/ppermute | solution.py:214
  7.7 0.1 collective-permute-start.8
  7.8 0.4 collective-permute-start
  8.2 0.1 collective-permute-start.1
  8.3 0.9 %collective-permute-done.8 = f32[2,64,256]{2,1,0:T(8,128)S(1)} collective-permute-done((f32[2,64,256]{2,1,0:T(8,128)S(1)}, f32[2,64,256]{2,1,0:T(8,128)S(1)}, u32[]{:S(2)}, u32[]{:S(2)}) %collective-permute-start.8) | collective-permute-done | bytes 131104 | tf_op jit(solution)/shard_map/ppermute | solution.py:214
  9.3 4.2 %collective-permute-start.9 = (f32[2,64,256]{2,1,0:T(8,128)S(1)}, f32[2,64,256]{2,1,0:T(8,128)S(1)}, u32[]{:S(2)}, u32[]{:S(2)}) collective-permute-start(f32[2,64,256]{2,1,0:T(8,128)S(1)} %add.97), channel_id=1, source_target_pairs={{0,3},{1,14},{2,1},{3,4},{4,7},{5,2},{6,5},{7,8},{8,11},{9,6},{10,... | collective-permute-start | bytes 393224 | tf_op jit(solution)/shard_map/ppermute | solution.py:215
  13.5 0.0 collective-permute-done.1
  13.5 0.8 %collective-permute-start.2 = (f32[2,64,256]{2,1,0:T(8,128)S(1)}, f32[2,64,256]{2,1,0:T(8,128)S(1)}, u32[]{:S(2)}, u32[]{:S(2)}) collective-permute-start(f32[2,64,256]{2,1,0:T(8,128)S(1)} %add.90), channel_id=1, source_target_pairs={{0,3},{1,14},{2,1},{3,4},{4,7},{5,2},{6,5},{7,8},{8,11},{9,6},{10,... | collective-permute-start | bytes 393224 | tf_op jit(solution)/shard_map/ppermute | solution.py:215
  14.3 1.1 %collective-permute-done.9 = f32[2,64,256]{2,1,0:T(8,128)S(1)} collective-permute-done((f32[2,64,256]{2,1,0:T(8,128)S(1)}, f32[2,64,256]{2,1,0:T(8,128)S(1)}, u32[]{:S(2)}, u32[]{:S(2)}) %collective-permute-start.9) | collective-permute-done | bytes 131104 | tf_op jit(solution)/shard_map/ppermute | solution.py:215
  15.4 0.0 collective-permute-done.7
  15.4 3.7 %collective-permute-start.10 = (f32[2,64,256]{2,1,0:T(8,128)S(1)}, f32[2,64,256]{2,1,0:T(8,128)S(1)}, u32[]{:S(2)}, u32[]{:S(2)}) collective-permute-start(f32[2,64,256]{2,1,0:T(8,128)S(1)} %fusion.6), channel_id=1, source_target_pairs={{0,3},{1,14},{2,1},{3,4},{4,7},{5,2},{6,5},{7,8},{8,11},{9,6},{10,... | collective-permute-start | bytes 393224 | tf_op jit(solution)/shard_map/ppermute | solution.py:215
  19.2 0.0 collective-permute-done.2
  19.2 0.0 collective-permute-done
  19.2 1.4 %collective-permute-start.3 = (f32[2,64,256]{2,1,0:T(8,128)S(1)}, f32[2,64,256]{2,1,0:T(8,128)S(1)}, u32[]{:S(2)}, u32[]{:S(2)}) collective-permute-start(f32[2,64,256]{2,1,0:T(8,128)S(1)} %fusion.9), channel_id=1, source_target_pairs={{0,3},{1,14},{2,1},{3,4},{4,7},{5,2},{6,5},{7,8},{8,11},{9,6},{10,... | collective-permute-start | bytes 393224 | tf_op jit(solution)/shard_map/ppermute | solution.py:215
  20.6 0.5 collective-permute-done.10
  21.2 3.7 %collective-permute-start.11 = (f32[2,64,256]{2,1,0:T(8,128)S(1)}, f32[2,64,256]{2,1,0:T(8,128)S(1)}, u32[]{:S(2)}, u32[]{:S(2)}) collective-permute-start(f32[2,64,256]{2,1,0:T(8,128)S(1)} %fusion.7), channel_id=1, source_target_pairs={{0,3},{1,14},{2,1},{3,4},{4,7},{5,2},{6,5},{7,8},{8,11},{9,6},{10,... | collective-permute-start | bytes 393224 | tf_op jit(solution)/shard_map/ppermute | solution.py:215
  24.9 0.0 collective-permute-done.3
  24.9 1.4 %collective-permute-start.4 = (f32[2,64,256]{2,1,0:T(8,128)S(1)}, f32[2,64,256]{2,1,0:T(8,128)S(1)}, u32[]{:S(2)}, u32[]{:S(2)}) collective-permute-start(f32[2,64,256]{2,1,0:T(8,128)S(1)} %fusion.10), channel_id=1, source_target_pairs={{0,3},{1,14},{2,1},{3,4},{4,7},{5,2},{6,5},{7,8},{8,11},{9,6},{10,... | collective-permute-start | bytes 393224 | tf_op jit(solution)/shard_map/ppermute | solution.py:215
  26.3 0.5 collective-permute-done.11
  26.9 4.7 %collective-permute-start.12 = (f32[2,64,256]{2,1,0:T(8,128)S(1)}, f32[2,64,256]{2,1,0:T(8,128)S(1)}, u32[]{:S(2)}, u32[]{:S(2)}) collective-permute-start(f32[2,64,256]{2,1,0:T(8,128)S(1)} %fusion.8), channel_id=1, source_target_pairs={{0,16},{1,30},{2,17},{3,19},{4,20},{5,18},{6,21},{7,23},{8,24},{9,... | collective-permute-start | bytes 393224 | tf_op jit(solution)/shard_map/ppermute | solution.py:216
  31.5 0.0 collective-permute-done.4
  31.6 1.4 %collective-permute-start.5 = (f32[2,64,256]{2,1,0:T(8,128)S(1)}, f32[2,64,256]{2,1,0:T(8,128)S(1)}, u32[]{:S(2)}, u32[]{:S(2)}) collective-permute-start(f32[2,64,256]{2,1,0:T(8,128)S(1)} %fusion.11), channel_id=1, source_target_pairs={{0,16},{1,30},{2,17},{3,19},{4,20},{5,18},{6,21},{7,23},{8,24},{9,... | collective-permute-start | bytes 393224 | tf_op jit(solution)/shard_map/ppermute | solution.py:216
  32.9 2.7 %collective-permute-done.12.moving = f32[2,64,256]{2,1,0:T(8,128)S(1)} collective-permute-done((f32[2,64,256]{2,1,0:T(8,128)S(1)}, f32[2,64,256]{2,1,0:T(8,128)S(1)}, u32[]{:S(2)}, u32[]{:S(2)}) %collective-permute-start.12) | collective-permute-done | bytes 131104 | tf_op jit(solution)/shard_map/ppermute | solution.py:216
  35.7 1.8 %collective-permute-start.13 = (f32[64,256]{1,0:T(8,128)S(1)}, f32[64,256]{1,0:T(8,128)S(1)}, u32[]{:S(2)}, u32[]{:S(2)}) collective-permute-start(f32[64,256]{1,0:T(8,128)S(1)} %slice_bitcast_fusion.4), channel_id=1, source_target_pairs={{0,1},{1,0},{2,3},{3,2},{4,5},{5,4},{6,7},{7,6},{8,9},{9,8},{10,11... | collective-permute-start | bytes 196616 | tf_op jit(solution)/shard_map/ppermute | solution.py:214
  37.5 0.9 %collective-permute-done.13.crossed = f32[64,256]{1,0:T(8,128)S(1)} collective-permute-done((f32[64,256]{1,0:T(8,128)S(1)}, f32[64,256]{1,0:T(8,128)S(1)}, u32[]{:S(2)}, u32[]{:S(2)}) %collective-permute-start.13) | collective-permute-done | bytes 65568 | tf_op jit(solution)/shard_map/ppermute | solution.py:214
  38.4 1.0 %shard_map.80 = (f32[64,256]{1,0:T(8,128)S(1)}, bf16[128,256]{1,0:T(8,128)(2,1)S(1)}, f32[2,64,256]{2,1,0:T(8,128)S(1)}, f32[2,64,256]{2,1,0:T(8,128)S(1)}) custom-call(s32[2,16]{1,0:T(2,128)S(1)} %get-tuple-element.29.table, f32[2,128,256]{2,1,0:T(8,128)S(1)} %copy-done, f32[2,64,256]{2,1,0:T(8,128)S(1)} %collective-permute-done.12.moving, ...), custom_call_target="tpu_custom_call" | custom-call | flops 201326592 | bytes 786432 | tf_op jit(solution)/shard_map/pallas_call | solution.py:178
  39.4 1.0 %shard_map.82 = (f32[6,64,256]{2,1,0:T(8,128)S(1)}, f32[6,64,256]{2,1,0:T(8,128)S(1)}) custom-call(s32[2,16]{1,0:T(2,128)S(1)} %get-tuple-element.29.table, bf16[128,256]{1,0:T(8,128)(2,1)S(1)} %get-tuple-element.49.lhs, bf16[256,4096]{1,0:T(8,128)(2,1)S(1)} %get-tuple-element.31.factor), custom_call_target="tpu_custom_call" | custom-call | flops 402653184 | bytes 1572864 | tf_op jit(solution)/shard_map/pallas_call | solution.py:187
  40.3 0.4 collective-permute-start.20
  40.8 0.0 collective-permute-done.5.moving
  40.8 0.2 collective-permute-start.6
  41.0 0.4 collective-permute-start.21
  41.4 0.8 %collective-permute-done.6.crossed = f32[64,256]{1,0:T(8,128)S(1)} collective-permute-done((f32[64,256]{1,0:T(8,128)S(1)}, f32[64,256]{1,0:T(8,128)S(1)}, u32[]{:S(2)}, u32[]{:S(2)}) %collective-permute-start.6) | collective-permute-done | bytes 65568 | tf_op jit(solution)/shard_map/ppermute | solution.py:214
  42.2 1.0 %shard_map.79 = (f32[64,256]{1,0:T(8,128)S(1)}, bf16[128,256]{1,0:T(8,128)(2,1)S(1)}, f32[2,64,256]{2,1,0:T(8,128)S(1)}, f32[2,64,256]{2,1,0:T(8,128)S(1)}) custom-call(s32[2,16]{1,0:T(2,128)S(1)} %get-tuple-element.29.table, f32[2,128,256]{2,1,0:T(8,128)S(1)} %copy-done, f32[2,64,256]{2,1,0:T(8,128)S(1)} %collective-permute-done.5.moving, ...), custom_call_target="tpu_custom_call" | custom-call | flops 201326592 | bytes 786432 | tf_op jit(solution)/shard_map/pallas_call | solution.py:178
  43.2 1.0 %shard_map.81 = (f32[6,64,256]{2,1,0:T(8,128)S(1)}, f32[6,64,256]{2,1,0:T(8,128)S(1)}) custom-call(s32[2,16]{1,0:T(2,128)S(1)} %get-tuple-element.29.table, bf16[128,256]{1,0:T(8,128)(2,1)S(1)} %get-tuple-element.44.lhs, bf16[256,4096]{1,0:T(8,128)(2,1)S(1)} %get-tuple-element.31.factor), custom_call_target="tpu_custom_call" | custom-call | flops 402653184 | bytes 1572864 | tf_op jit(solution)/shard_map/pallas_call | solution.py:187
  44.2 0.5 collective-permute-start.14
  44.6 0.1 collective-permute-start.15
  44.8 0.0 collective-permute-done.21
  44.8 3.4 %collective-permute-start.22 = (f32[2,64,256]{2,1,0:T(8,128)S(1)}, f32[2,64,256]{2,1,0:T(8,128)S(1)}, u32[]{:S(2)}, u32[]{:S(2)}) collective-permute-start(f32[2,64,256]{2,1,0:T(8,128)S(1)} %add.111), channel_id=1, source_target_pairs={{0,3},{1,14},{2,1},{3,4},{4,7},{5,2},{6,5},{7,8},{8,11},{9,6},{10,... | collective-permute-start | bytes 393224 | tf_op jit(solution)/shard_map/ppermute | solution.py:215
  48.2 0.0 collective-permute-done.15
  48.2 1.4 %collective-permute-start.16 = (f32[2,64,256]{2,1,0:T(8,128)S(1)}, f32[2,64,256]{2,1,0:T(8,128)S(1)}, u32[]{:S(2)}, u32[]{:S(2)}) collective-permute-start(f32[2,64,256]{2,1,0:T(8,128)S(1)} %add.104), channel_id=1, source_target_pairs={{0,3},{1,14},{2,1},{3,4},{4,7},{5,2},{6,5},{7,8},{8,11},{9,6},{10,... | collective-permute-start | bytes 393224 | tf_op jit(solution)/shard_map/ppermute | solution.py:215
  49.6 0.6 collective-permute-done.22
  50.2 0.0 collective-permute-done.20
  50.2 3.7 %collective-permute-start.23 = (f32[2,64,256]{2,1,0:T(8,128)S(1)}, f32[2,64,256]{2,1,0:T(8,128)S(1)}, u32[]{:S(2)}, u32[]{:S(2)}) collective-permute-start(f32[2,64,256]{2,1,0:T(8,128)S(1)} %fusion), channel_id=1, source_target_pairs={{0,3},{1,14},{2,1},{3,4},{4,7},{5,2},{6,5},{7,8},{8,11},{9,6},{10,... | collective-permute-start | bytes 393224 | tf_op jit(solution)/shard_map/ppermute | solution.py:215
  53.9 0.0 collective-permute-done.16
  53.9 0.0 collective-permute-done.14
  54.0 1.4 %collective-permute-start.17 = (f32[2,64,256]{2,1,0:T(8,128)S(1)}, f32[2,64,256]{2,1,0:T(8,128)S(1)}, u32[]{:S(2)}, u32[]{:S(2)}) collective-permute-start(f32[2,64,256]{2,1,0:T(8,128)S(1)} %fusion.3), channel_id=1, source_target_pairs={{0,3},{1,14},{2,1},{3,4},{4,7},{5,2},{6,5},{7,8},{8,11},{9,6},{10,... | collective-permute-start | bytes 393224 | tf_op jit(solution)/shard_map/ppermute | solution.py:215
  55.3 0.5 collective-permute-done.23
  55.9 3.7 %collective-permute-start.24 = (f32[2,64,256]{2,1,0:T(8,128)S(1)}, f32[2,64,256]{2,1,0:T(8,128)S(1)}, u32[]{:S(2)}, u32[]{:S(2)}) collective-permute-start(f32[2,64,256]{2,1,0:T(8,128)S(1)} %fusion.1), channel_id=1, source_target_pairs={{0,3},{1,14},{2,1},{3,4},{4,7},{5,2},{6,5},{7,8},{8,11},{9,6},{10,... | collective-permute-start | bytes 393224 | tf_op jit(solution)/shard_map/ppermute | solution.py:215
  59.6 0.0 collective-permute-done.17
  59.7 1.4 %collective-permute-start.18 = (f32[2,64,256]{2,1,0:T(8,128)S(1)}, f32[2,64,256]{2,1,0:T(8,128)S(1)}, u32[]{:S(2)}, u32[]{:S(2)}) collective-permute-start(f32[2,64,256]{2,1,0:T(8,128)S(1)} %fusion.4), channel_id=1, source_target_pairs={{0,3},{1,14},{2,1},{3,4},{4,7},{5,2},{6,5},{7,8},{8,11},{9,6},{10,... | collective-permute-start | bytes 393224 | tf_op jit(solution)/shard_map/ppermute | solution.py:215
  61.0 0.5 collective-permute-done.24
  61.6 1.3 %collective-permute-start.25 = (f32[2,64,256]{2,1,0:T(8,128)S(1)}, f32[2,64,256]{2,1,0:T(8,128)S(1)}, u32[]{:S(2)}, u32[]{:S(2)}) collective-permute-start(f32[2,64,256]{2,1,0:T(8,128)S(1)} %fusion.2), channel_id=1, source_target_pairs={{0,16},{1,30},{2,17},{3,19},{4,20},{5,18},{6,21},{7,23},{8,24},{9,... | collective-permute-start | bytes 393224 | tf_op jit(solution)/shard_map/ppermute | solution.py:216
  62.9 1.2 %collective-permute-done.18 = f32[2,64,256]{2,1,0:T(8,128)S(1)} collective-permute-done((f32[2,64,256]{2,1,0:T(8,128)S(1)}, f32[2,64,256]{2,1,0:T(8,128)S(1)}, u32[]{:S(2)}, u32[]{:S(2)}) %collective-permute-start.18) | collective-permute-done | bytes 131104 | tf_op jit(solution)/shard_map/ppermute | solution.py:215
  64.2 0.2 collective-permute-start.19
  64.4 6.0 %collective-permute-done.25 = f32[2,64,256]{2,1,0:T(8,128)S(1)} collective-permute-done((f32[2,64,256]{2,1,0:T(8,128)S(1)}, f32[2,64,256]{2,1,0:T(8,128)S(1)}, u32[]{:S(2)}, u32[]{:S(2)}) %collective-permute-start.25) | collective-permute-done | bytes 131104 | tf_op jit(solution)/shard_map/ppermute | solution.py:216
  70.4 3.3 %collective-permute-start.27 = (f32[64,256]{1,0:T(8,128)S(1)}, f32[64,256]{1,0:T(8,128)S(1)}, u32[]{:S(2)}, u32[]{:S(2)}) collective-permute-start(f32[64,256]{1,0:T(8,128)S(1)} %get-tuple-element.56), channel_id=1, source_target_pairs={{0,1},{1,0},{2,3},{3,2},{4,5},{5,4},{6,7},{7,6},{8,9},{9,8},{10,11... | collective-permute-start | bytes 196616 | tf_op jit(solution)/shard_map/ppermute | solution.py:214
  73.7 0.0 collective-permute-done.19
  73.7 1.4 %collective-permute-start.26 = (f32[64,256]{1,0:T(8,128)S(1)}, f32[64,256]{1,0:T(8,128)S(1)}, u32[]{:S(2)}, u32[]{:S(2)}) collective-permute-start(f32[64,256]{1,0:T(8,128)S(1)} %get-tuple-element.54), channel_id=1, source_target_pairs={{0,1},{1,0},{2,3},{3,2},{4,5},{5,4},{6,7},{7,6},{8,9},{9,8},{10,11... | collective-permute-start | bytes 196616 | tf_op jit(solution)/shard_map/ppermute | solution.py:214
  75.1 0.7 pad_maximum_fusion
  75.9 0.2 collective-permute-done.26
  76.0 0.7 fusion.12
  (22 shorter events, 0.4 us)
Async XLA Ops:
  4.4 34.0 %copy-start = (f32[2,128,256]{2,1,0:T(8,128)S(1)}, f32[2,128,256]{2,1,0:T(8,128)}, u32[]{:S(2)}) copy-start(f32[2,128,256]{2,1,0:T(8,128)} %right_sides.5) | copy-start | bytes 786436
  4.4 11.0 %collective-permute-start.7 = (f32[6,64,256]{2,1,0:T(8,128)S(1)}, f32[6,64,256]{2,1,0:T(8,128)S(1)}, u32[]{:S(2)}, u32[]{:S(2)}) collective-permute-start(f32[6,64,256]{2,1,0:T(8,128)S(1)} %get-tuple-element.40), channel_id=1, source_target_pairs={{0,1},{1,0},{2,3},{3,2},{4,5},{5,4},{6,7},{7,6},{8,9},{9,8},{10,11... | collective-permute-start | bytes 1179656 | tf_op jit(solution)/shard_map/ppermute | solution.py:214
  7.7 1.5 %collective-permute-start.8 = (f32[2,64,256]{2,1,0:T(8,128)S(1)}, f32[2,64,256]{2,1,0:T(8,128)S(1)}, u32[]{:S(2)}, u32[]{:S(2)}) collective-permute-start(f32[2,64,256]{2,1,0:T(8,128)S(1)} %get-tuple-element.42), channel_id=1, source_target_pairs={{0,1},{1,0},{2,3},{3,2},{4,5},{5,4},{6,7},{7,6},{8,9},{9,8},{10,11... | collective-permute-start | bytes 393224 | tf_op jit(solution)/shard_map/ppermute | solution.py:214
  7.8 11.4 %collective-permute-start = (f32[6,64,256]{2,1,0:T(8,128)S(1)}, f32[6,64,256]{2,1,0:T(8,128)S(1)}, u32[]{:S(2)}, u32[]{:S(2)}) collective-permute-start(f32[6,64,256]{2,1,0:T(8,128)S(1)} %get-tuple-element.33), channel_id=1, source_target_pairs={{0,1},{1,0},{2,3},{3,2},{4,5},{5,4},{6,7},{7,6},{8,9},{9,8},{10,11... | collective-permute-start | bytes 1179656 | tf_op jit(solution)/shard_map/ppermute | solution.py:214
  8.2 5.3 %collective-permute-start.1 = (f32[2,64,256]{2,1,0:T(8,128)S(1)}, f32[2,64,256]{2,1,0:T(8,128)S(1)}, u32[]{:S(2)}, u32[]{:S(2)}) collective-permute-start(f32[2,64,256]{2,1,0:T(8,128)S(1)} %get-tuple-element.35), channel_id=1, source_target_pairs={{0,1},{1,0},{2,3},{3,2},{4,5},{5,4},{6,7},{7,6},{8,9},{9,8},{10,11... | collective-permute-start | bytes 393224 | tf_op jit(solution)/shard_map/ppermute | solution.py:214
  9.3 6.2 %collective-permute-start.9 = (f32[2,64,256]{2,1,0:T(8,128)S(1)}, f32[2,64,256]{2,1,0:T(8,128)S(1)}, u32[]{:S(2)}, u32[]{:S(2)}) collective-permute-start(f32[2,64,256]{2,1,0:T(8,128)S(1)} %add.97), channel_id=1, source_target_pairs={{0,3},{1,14},{2,1},{3,4},{4,7},{5,2},{6,5},{7,8},{8,11},{9,6},{10,... | collective-permute-start | bytes 393224 | tf_op jit(solution)/shard_map/ppermute | solution.py:215
  13.5 5.7 %collective-permute-start.2 = (f32[2,64,256]{2,1,0:T(8,128)S(1)}, f32[2,64,256]{2,1,0:T(8,128)S(1)}, u32[]{:S(2)}, u32[]{:S(2)}) collective-permute-start(f32[2,64,256]{2,1,0:T(8,128)S(1)} %add.90), channel_id=1, source_target_pairs={{0,3},{1,14},{2,1},{3,4},{4,7},{5,2},{6,5},{7,8},{8,11},{9,6},{10,... | collective-permute-start | bytes 393224 | tf_op jit(solution)/shard_map/ppermute | solution.py:215
  15.4 5.7 %collective-permute-start.10 = (f32[2,64,256]{2,1,0:T(8,128)S(1)}, f32[2,64,256]{2,1,0:T(8,128)S(1)}, u32[]{:S(2)}, u32[]{:S(2)}) collective-permute-start(f32[2,64,256]{2,1,0:T(8,128)S(1)} %fusion.6), channel_id=1, source_target_pairs={{0,3},{1,14},{2,1},{3,4},{4,7},{5,2},{6,5},{7,8},{8,11},{9,6},{10,... | collective-permute-start | bytes 393224 | tf_op jit(solution)/shard_map/ppermute | solution.py:215
  19.2 5.7 %collective-permute-start.3 = (f32[2,64,256]{2,1,0:T(8,128)S(1)}, f32[2,64,256]{2,1,0:T(8,128)S(1)}, u32[]{:S(2)}, u32[]{:S(2)}) collective-permute-start(f32[2,64,256]{2,1,0:T(8,128)S(1)} %fusion.9), channel_id=1, source_target_pairs={{0,3},{1,14},{2,1},{3,4},{4,7},{5,2},{6,5},{7,8},{8,11},{9,6},{10,... | collective-permute-start | bytes 393224 | tf_op jit(solution)/shard_map/ppermute | solution.py:215
  21.2 5.7 %collective-permute-start.11 = (f32[2,64,256]{2,1,0:T(8,128)S(1)}, f32[2,64,256]{2,1,0:T(8,128)S(1)}, u32[]{:S(2)}, u32[]{:S(2)}) collective-permute-start(f32[2,64,256]{2,1,0:T(8,128)S(1)} %fusion.7), channel_id=1, source_target_pairs={{0,3},{1,14},{2,1},{3,4},{4,7},{5,2},{6,5},{7,8},{8,11},{9,6},{10,... | collective-permute-start | bytes 393224 | tf_op jit(solution)/shard_map/ppermute | solution.py:215
  24.9 6.6 %collective-permute-start.4 = (f32[2,64,256]{2,1,0:T(8,128)S(1)}, f32[2,64,256]{2,1,0:T(8,128)S(1)}, u32[]{:S(2)}, u32[]{:S(2)}) collective-permute-start(f32[2,64,256]{2,1,0:T(8,128)S(1)} %fusion.10), channel_id=1, source_target_pairs={{0,3},{1,14},{2,1},{3,4},{4,7},{5,2},{6,5},{7,8},{8,11},{9,6},{10,... | collective-permute-start | bytes 393224 | tf_op jit(solution)/shard_map/ppermute | solution.py:215
  26.9 8.8 %collective-permute-start.12 = (f32[2,64,256]{2,1,0:T(8,128)S(1)}, f32[2,64,256]{2,1,0:T(8,128)S(1)}, u32[]{:S(2)}, u32[]{:S(2)}) collective-permute-start(f32[2,64,256]{2,1,0:T(8,128)S(1)} %fusion.8), channel_id=1, source_target_pairs={{0,16},{1,30},{2,17},{3,19},{4,20},{5,18},{6,21},{7,23},{8,24},{9,... | collective-permute-start | bytes 393224 | tf_op jit(solution)/shard_map/ppermute | solution.py:216
  31.6 9.2 %collective-permute-start.5 = (f32[2,64,256]{2,1,0:T(8,128)S(1)}, f32[2,64,256]{2,1,0:T(8,128)S(1)}, u32[]{:S(2)}, u32[]{:S(2)}) collective-permute-start(f32[2,64,256]{2,1,0:T(8,128)S(1)} %fusion.11), channel_id=1, source_target_pairs={{0,16},{1,30},{2,17},{3,19},{4,20},{5,18},{6,21},{7,23},{8,24},{9,... | collective-permute-start | bytes 393224 | tf_op jit(solution)/shard_map/ppermute | solution.py:216
  35.7 2.7 %collective-permute-start.13 = (f32[64,256]{1,0:T(8,128)S(1)}, f32[64,256]{1,0:T(8,128)S(1)}, u32[]{:S(2)}, u32[]{:S(2)}) collective-permute-start(f32[64,256]{1,0:T(8,128)S(1)} %slice_bitcast_fusion.4), channel_id=1, source_target_pairs={{0,1},{1,0},{2,3},{3,2},{4,5},{5,4},{6,7},{7,6},{8,9},{9,8},{10,11... | collective-permute-start | bytes 196616 | tf_op jit(solution)/shard_map/ppermute | solution.py:214
  40.3 9.8 %collective-permute-start.20 = (f32[6,64,256]{2,1,0:T(8,128)S(1)}, f32[6,64,256]{2,1,0:T(8,128)S(1)}, u32[]{:S(2)}, u32[]{:S(2)}) collective-permute-start(f32[6,64,256]{2,1,0:T(8,128)S(1)} %get-tuple-element.51), channel_id=1, source_target_pairs={{0,1},{1,0},{2,3},{3,2},{4,5},{5,4},{6,7},{7,6},{8,9},{9,8},{10,11... | collective-permute-start | bytes 1179656 | tf_op jit(solution)/shard_map/ppermute | solution.py:214
  40.8 1.4 %collective-permute-start.6 = (f32[64,256]{1,0:T(8,128)S(1)}, f32[64,256]{1,0:T(8,128)S(1)}, u32[]{:S(2)}, u32[]{:S(2)}) collective-permute-start(f32[64,256]{1,0:T(8,128)S(1)} %slice_bitcast_fusion.5), channel_id=1, source_target_pairs={{0,1},{1,0},{2,3},{3,2},{4,5},{5,4},{6,7},{7,6},{8,9},{9,8},{10,11... | collective-permute-start | bytes 196616 | tf_op jit(solution)/shard_map/ppermute | solution.py:214
  41.0 3.8 %collective-permute-start.21 = (f32[2,64,256]{2,1,0:T(8,128)S(1)}, f32[2,64,256]{2,1,0:T(8,128)S(1)}, u32[]{:S(2)}, u32[]{:S(2)}) collective-permute-start(f32[2,64,256]{2,1,0:T(8,128)S(1)} %get-tuple-element.53), channel_id=1, source_target_pairs={{0,1},{1,0},{2,3},{3,2},{4,5},{5,4},{6,7},{7,6},{8,9},{9,8},{10,11... | collective-permute-start | bytes 393224 | tf_op jit(solution)/shard_map/ppermute | solution.py:214
  44.2 9.7 %collective-permute-start.14 = (f32[6,64,256]{2,1,0:T(8,128)S(1)}, f32[6,64,256]{2,1,0:T(8,128)S(1)}, u32[]{:S(2)}, u32[]{:S(2)}) collective-permute-start(f32[6,64,256]{2,1,0:T(8,128)S(1)} %get-tuple-element.46), channel_id=1, source_target_pairs={{0,1},{1,0},{2,3},{3,2},{4,5},{5,4},{6,7},{7,6},{8,9},{9,8},{10,11... | collective-permute-start | bytes 1179656 | tf_op jit(solution)/shard_map/ppermute | solution.py:214
  44.6 3.6 %collective-permute-start.15 = (f32[2,64,256]{2,1,0:T(8,128)S(1)}, f32[2,64,256]{2,1,0:T(8,128)S(1)}, u32[]{:S(2)}, u32[]{:S(2)}) collective-permute-start(f32[2,64,256]{2,1,0:T(8,128)S(1)} %get-tuple-element.48), channel_id=1, source_target_pairs={{0,1},{1,0},{2,3},{3,2},{4,5},{5,4},{6,7},{7,6},{8,9},{9,8},{10,11... | collective-permute-start | bytes 393224 | tf_op jit(solution)/shard_map/ppermute | solution.py:214
  44.8 5.3 %collective-permute-start.22 = (f32[2,64,256]{2,1,0:T(8,128)S(1)}, f32[2,64,256]{2,1,0:T(8,128)S(1)}, u32[]{:S(2)}, u32[]{:S(2)}) collective-permute-start(f32[2,64,256]{2,1,0:T(8,128)S(1)} %add.111), channel_id=1, source_target_pairs={{0,3},{1,14},{2,1},{3,4},{4,7},{5,2},{6,5},{7,8},{8,11},{9,6},{10,... | collective-permute-start | bytes 393224 | tf_op jit(solution)/shard_map/ppermute | solution.py:215
  48.2 5.7 %collective-permute-start.16 = (f32[2,64,256]{2,1,0:T(8,128)S(1)}, f32[2,64,256]{2,1,0:T(8,128)S(1)}, u32[]{:S(2)}, u32[]{:S(2)}) collective-permute-start(f32[2,64,256]{2,1,0:T(8,128)S(1)} %add.104), channel_id=1, source_target_pairs={{0,3},{1,14},{2,1},{3,4},{4,7},{5,2},{6,5},{7,8},{8,11},{9,6},{10,... | collective-permute-start | bytes 393224 | tf_op jit(solution)/shard_map/ppermute | solution.py:215
  50.2 5.7 %collective-permute-start.23 = (f32[2,64,256]{2,1,0:T(8,128)S(1)}, f32[2,64,256]{2,1,0:T(8,128)S(1)}, u32[]{:S(2)}, u32[]{:S(2)}) collective-permute-start(f32[2,64,256]{2,1,0:T(8,128)S(1)} %fusion), channel_id=1, source_target_pairs={{0,3},{1,14},{2,1},{3,4},{4,7},{5,2},{6,5},{7,8},{8,11},{9,6},{10,... | collective-permute-start | bytes 393224 | tf_op jit(solution)/shard_map/ppermute | solution.py:215
  54.0 5.7 %collective-permute-start.17 = (f32[2,64,256]{2,1,0:T(8,128)S(1)}, f32[2,64,256]{2,1,0:T(8,128)S(1)}, u32[]{:S(2)}, u32[]{:S(2)}) collective-permute-start(f32[2,64,256]{2,1,0:T(8,128)S(1)} %fusion.3), channel_id=1, source_target_pairs={{0,3},{1,14},{2,1},{3,4},{4,7},{5,2},{6,5},{7,8},{8,11},{9,6},{10,... | collective-permute-start | bytes 393224 | tf_op jit(solution)/shard_map/ppermute | solution.py:215
  55.9 5.7 %collective-permute-start.24 = (f32[2,64,256]{2,1,0:T(8,128)S(1)}, f32[2,64,256]{2,1,0:T(8,128)S(1)}, u32[]{:S(2)}, u32[]{:S(2)}) collective-permute-start(f32[2,64,256]{2,1,0:T(8,128)S(1)} %fusion.1), channel_id=1, source_target_pairs={{0,3},{1,14},{2,1},{3,4},{4,7},{5,2},{6,5},{7,8},{8,11},{9,6},{10,... | collective-permute-start | bytes 393224 | tf_op jit(solution)/shard_map/ppermute | solution.py:215
  59.7 4.5 %collective-permute-start.18 = (f32[2,64,256]{2,1,0:T(8,128)S(1)}, f32[2,64,256]{2,1,0:T(8,128)S(1)}, u32[]{:S(2)}, u32[]{:S(2)}) collective-permute-start(f32[2,64,256]{2,1,0:T(8,128)S(1)} %fusion.4), channel_id=1, source_target_pairs={{0,3},{1,14},{2,1},{3,4},{4,7},{5,2},{6,5},{7,8},{8,11},{9,6},{10,... | collective-permute-start | bytes 393224 | tf_op jit(solution)/shard_map/ppermute | solution.py:215
  61.6 8.8 %collective-permute-start.25 = (f32[2,64,256]{2,1,0:T(8,128)S(1)}, f32[2,64,256]{2,1,0:T(8,128)S(1)}, u32[]{:S(2)}, u32[]{:S(2)}) collective-permute-start(f32[2,64,256]{2,1,0:T(8,128)S(1)} %fusion.2), channel_id=1, source_target_pairs={{0,16},{1,30},{2,17},{3,19},{4,20},{5,18},{6,21},{7,23},{8,24},{9,... | collective-permute-start | bytes 393224 | tf_op jit(solution)/shard_map/ppermute | solution.py:216
  64.2 9.6 %collective-permute-start.19 = (f32[2,64,256]{2,1,0:T(8,128)S(1)}, f32[2,64,256]{2,1,0:T(8,128)S(1)}, u32[]{:S(2)}, u32[]{:S(2)}) collective-permute-start(f32[2,64,256]{2,1,0:T(8,128)S(1)} %fusion.5), channel_id=1, source_target_pairs={{0,16},{1,30},{2,17},{3,19},{4,20},{5,18},{6,21},{7,23},{8,24},{9,... | collective-permute-start | bytes 393224 | tf_op jit(solution)/shard_map/ppermute | solution.py:216
  70.4 5.4 %collective-permute-start.27 = (f32[64,256]{1,0:T(8,128)S(1)}, f32[64,256]{1,0:T(8,128)S(1)}, u32[]{:S(2)}, u32[]{:S(2)}) collective-permute-start(f32[64,256]{1,0:T(8,128)S(1)} %get-tuple-element.56), channel_id=1, source_target_pairs={{0,1},{1,0},{2,3},{3,2},{4,5},{5,4},{6,7},{7,6},{8,9},{9,8},{10,11... | collective-permute-start | bytes 196616 | tf_op jit(solution)/shard_map/ppermute | solution.py:214
  73.7 2.3 %collective-permute-start.26 = (f32[64,256]{1,0:T(8,128)S(1)}, f32[64,256]{1,0:T(8,128)S(1)}, u32[]{:S(2)}, u32[]{:S(2)}) collective-permute-start(f32[64,256]{1,0:T(8,128)S(1)} %get-tuple-element.54), channel_id=1, source_target_pairs={{0,1},{1,0},{2,3},{3,2},{4,5},{5,4},{6,7},{7,6},{8,9},{9,8},{10,11... | collective-permute-start | bytes 196616 | tf_op jit(solution)/shard_map/ppermute | solution.py:214
where the time goes:
time: 76.8 us; the launch traced here: 76.7 us
  starting transfers between devices  49.8 us (65%)
  waiting for transfers between devices  16.7 us (22%)
  Pallas kernels  7.62 us (10%)
  other arithmetic  1.78 us (2%)
  between operations  0.79 us (1%)
    ppermute x12, starting transfers between devices, shards(): pass_on = lambda value: lax.ppermute(value, 'own', chain)  30.2 us
    ppermute x12, starting transfers between devices, shards(): swap = lambda value: lax.ppermute(value, 'own', partner)  12.1 us
    ppermute x4, waiting for transfers between devices, shards(): leave = lambda value: lax.ppermute(value, ('sec', 'own'), onward)  8.77 us
    ppermute x4, starting transfers between devices, shards(): leave = lambda value: lax.ppermute(value, ('sec', 'own'), onward)  7.57 us
    ppermute x12, waiting for transfers between devices, shards(): pass_on = lambda value: lax.ppermute(value, 'own', chain)  5.01 us
    pallas_call x3, Pallas kernels, late_step(): out = call(kernel, 12, [SMEM, VMEM, VMEM], outs, 4)(fixed[0], lhs, fixed[1])  3.11 us
    ppermute x12, waiting for transfers between devices, shards(): swap = lambda value: lax.ppermute(value, 'own', partner)  2.88 us
    pallas_call x1, Pallas kernels, first_step(): call(kernel, 6, [HBM] * 6, outs, 4, scratch)  2.58 us
  transfers between devices with their start and end apart: 28, of which 13 were waited for; matrix products, arithmetic and copies ran while one was open for 1% of the time, Pallas kernels for 5%

commit v1 on v0

v1 whole, which is shorter than its diff:
```python
import functools

import jax
import jax.numpy as jnp
from jax import lax
from jax.experimental import pallas as pl
from jax.experimental.pallas import tpu as pltpu
from jax.sharding import PartitionSpec as P


STREAMS = 2


def split(value):
    high = value.astype(jnp.bfloat16)
    return high, (value - high.astype(jnp.float32)).astype(jnp.bfloat16)


def dot(a, b):
    return jnp.dot(a, b, preferred_element_type=jnp.float32)


def blocks_of(chips, core, chip, names):
    ahead = 1 - 2 * ((chip + core) % 2)
    for name in names:
        if name == "far":
            yield chips // 2, core
        elif name == "own":
            yield 0, 1 - core
        else:
            first = (core + name) % 2
            yield name * ahead, first
            yield name * ahead, 1 - first


EARLY = (3, "far", "own")
LATE = (2, 1)


def put(table, lhs, factor, chips, names, gives, keeps):
    rows, block = gives[0].shape[1:]
    me = lax.axis_index("own")
    chip, core = me // 2, me % 2
    for refs, who in ((gives, 1 - core), (keeps, core)):
        for place, (distance, to_core) in enumerate(blocks_of(chips, who, chip, names)):
            target = (chip + distance + chips) % chips * 2 + to_core
            start = pl.multiple_of(table[0, target] * block, block)
            both = dot(lhs, factor[:, pl.ds(start, block)])
            scale = table[1, target].astype(jnp.float32)
            for stream, ref in enumerate(refs):
                low = slice((2 * stream + 1) * rows, (2 * stream + 2) * rows)
                high = slice(2 * stream * rows, (2 * stream + 1) * rows)
                ref[place] = (both[high] + both[low]) * scale


def solve(residual, inverse_high, inverse_low, streams):
    width = residual.shape[0]
    rows = width // streams
    high, low = split(residual)
    both = dot(jnp.concatenate([high, low], axis=0), inverse_high)
    result = both[:width] + both[width:] + dot(high, inverse_low)
    high, low = split(result)
    parts = []
    for stream in range(streams):
        here = slice(stream * rows, (stream + 1) * rows)
        parts += [high[here], low[here]]
    return result, jnp.concatenate(parts, axis=0)


def first_kernel(
    chips, streams, ancestor, structure, right_sides, carried, inverse, factor,
    table, factor_here, inverse_high, inverse_low, solved, lhs, *rest,
):
    gives, keeps = rest[:streams], rest[streams : 2 * streams]
    slots, present, right_here, carried_here, inverse_here, sems = rest[2 * streams :]
    chunk = factor.shape[0] // 4
    pairs = [
        (inverse, inverse_here),
        (right_sides.at[0], right_here),
        (carried, carried_here),
        (ancestor, slots),
        (structure, present),
    ]
    for i in range(4):
        here = pl.ds(i * chunk, chunk)
        pairs.append((factor.at[here], factor_here.at[here]))
    copies = [
        pltpu.make_async_copy(source, target, sems.at[i])
        for i, (source, target) in enumerate(pairs)
    ]
    for copy in copies:
        copy.start()
    for copy in copies[:3]:
        copy.wait()
    inverse_high[...], inverse_low[...] = split(inverse_here[...])
    solved[...], lhs[...] = solve(
        right_here[...] - carried_here[...], inverse_high[...], inverse_low[...], streams
    )
    copies[3].wait()
    copies[4].wait()
    for slot in range(slots.shape[1]):
        table[0, slots[0, slot]] = slot
        table[1, slots[0, slot]] = present[0, slot]
    for copy in copies[5:]:
        copy.wait()
    put(table, lhs[...], factor_here, chips, EARLY, gives, keeps)


def next_kernel(
    chips, tick, first_row, table, right_sides, moving, crossed,
    inverse_high, inverse_low, factor, solved, lhs, give, keep,
):
    here = pl.ds(first_row, solved.shape[0])
    incoming = moving[0] + crossed[...]
    incoming = jnp.where(lax.axis_index("sec") == 0, 0.0, incoming)
    solved[...], lhs[...] = solve(
        right_sides[tick, here] - incoming, inverse_high[...], inverse_low[...], 1
    )
    put(table, lhs[...], factor, chips, EARLY, [give], [keep])


def late_kernel(chips, streams, table, factor, *rest):
    parts, outs = rest[: -2 * streams], rest[-2 * streams :]
    lhs = jnp.concatenate([part[...] for part in parts], axis=0)
    put(table, lhs, factor, chips, LATE, outs[:streams], outs[streams:])


VMEM = pl.BlockSpec(memory_space=pltpu.VMEM)
SMEM = pl.BlockSpec(memory_space=pltpu.SMEM)
HBM = pl.BlockSpec(memory_space=pltpu.HBM)
F32 = functools.partial(jax.ShapeDtypeStruct, dtype=jnp.float32)
BF16 = functools.partial(jax.ShapeDtypeStruct, dtype=jnp.bfloat16)


def call(kernel, products, in_specs, outs, limit, scratch=()):
    return pl.pallas_call(
        kernel,
        out_shape=outs,
        in_specs=in_specs,
        out_specs=[SMEM if out.dtype == jnp.int32 else VMEM for out in outs],
        scratch_shapes=list(scratch),
        compiler_params=pltpu.CompilerParams(vmem_limit_bytes=limit << 20),
        cost_estimate=pl.CostEstimate(
            flops=products * 2 * 256 * 256 * 256,
            bytes_accessed=products * 65536 * 2,
            transcendentals=0,
        ),
    )


def first_step(chips, streams, rows, arrays):
    ancestor, _, _, carried, _, factor = arrays
    slots = ancestor.shape[1]
    width, block = carried.shape
    square = (block, block)
    outs = [jax.ShapeDtypeStruct((2, slots), jnp.int32), BF16(factor.shape)]
    outs += [BF16(square)] * 2 + [F32((width, block)), BF16((2 * width, block))]
    outs += [F32((4, rows, block))] * (2 * streams)
    scratch = [
        pltpu.SMEM((1, slots), jnp.int32),
        pltpu.SMEM((1, slots), jnp.int32),
        pltpu.VMEM((width, block), jnp.float32),
        pltpu.VMEM((width, block), jnp.float32),
        pltpu.VMEM(square, jnp.float32),
        pltpu.SemaphoreType.DMA((9,)),
    ]
    kernel = functools.partial(first_kernel, chips, streams)
    out = call(kernel, 6, [HBM] * 6, outs, 4, scratch)(
        *[pltpu.with_memory_space_constraint(array, pltpu.HBM) for array in arrays]
    )
    fixed, (solved, lhs) = out[:4], out[4:6]
    return fixed, solved, lhs, out[6 : 6 + streams], out[6 + streams :]


def next_step(chips, tick, first_row, fixed, right_sides, moving, crossed):
    table, factor, inverse_high, inverse_low = fixed
    rows, block = crossed.shape
    outs = [F32((rows, block)), BF16((2 * rows, block))]
    outs += [F32((4, rows, block))] * 2
    kernel = functools.partial(next_kernel, chips, tick, first_row)
    return call(kernel, 6, [SMEM] + [VMEM] * 6, outs, 4)(
        table, right_sides, moving, crossed, inverse_high, inverse_low, factor
    )


def late_step(chips, streams, fixed, parts):
    block = parts[0].shape[1]
    rows = sum(part.shape[0] for part in parts) // 2 // streams
    outs = [F32((4, rows, block))] * (2 * streams)
    kernel = functools.partial(late_kernel, chips, streams)
    out = call(kernel, 16, [SMEM] + [VMEM] * (1 + len(parts)), outs, 4)(
        fixed[0], fixed[1], *parts
    )
    return out[:streams], out[streams:]


def shards(right_sides, inv_diag, factor_tiles, structure, ancestor, carried):
    owners = lax.axis_size("own")
    sections = lax.axis_size("sec")
    chips = owners // 2
    partner = [(i, i ^ 1) for i in range(owners)]

    def next_on_chain(i):
        chip, core = i // 2, i % 2
        ahead = 1 - 2 * ((chip + core) % 2)
        return ((chip + ahead) % chips) * 2 + 1 - core

    def to_next_section(place):
        return [
            (s * owners + i, (s + 1) % sections * owners + place(i))
            for s in range(sections)
            for i in range(owners)
        ]

    chain = [(i, next_on_chain(i)) for i in range(owners)]
    slanted = to_next_section(next_on_chain)
    first_section = lax.axis_index("sec") == 0

    def on_chain(chips_on):
        pairs = []
        for i in range(owners):
            ahead = 1 - 2 * ((i // 2 + i) % 2)
            pairs.append((i, (i // 2 + chips_on * ahead) % chips * 2 + 1 - i % 2))
        return pairs

    own_permute = lambda value, pairs: lax.ppermute(value, "own", pairs)
    swap = lambda value: own_permute(value, partner)

    ticks, width, _ = right_sides.shape
    rows = width // STREAMS
    streams = range(STREAMS)
    solved_all = []
    for tick in range(ticks):
        if tick == 0:
            fixed, solved, lhs, gives, keeps = first_step(
                chips,
                STREAMS,
                rows,
                (ancestor, structure, right_sides, carried, inv_diag, factor_tiles),
            )
            solved_all.append(solved)
            parts = [lhs]
        else:
            gives, keeps, parts = [], [], []
            for stream in streams:
                solved, lhs, give, keep = next_step(
                    chips, tick, stream * rows, fixed, right_sides,
                    moving[stream], crossed[stream],
                )
                solved_all.append(solved)
                gives.append(give)
                keeps.append(keep)
                parts.append(lhs)
        later_gives, later_keeps = late_step(chips, STREAMS, fixed, parts)
        sums = []
        for stream in streams:
            sums.append(keeps[stream] + swap(gives[stream]))
        far = jnp.concatenate([value[2] for value in sums], axis=0)
        own = jnp.concatenate([value[3] for value in sums], axis=0)
        far = own_permute(far, on_chain(chips // 2 - 1))
        own = own_permute(own, on_chain(-1))
        joining = jnp.stack([far, own])
        joining = lax.optimization_barrier(
            [joining[:, stream * rows : (stream + 1) * rows] for stream in streams]
        )
        moving, crossed = [], []
        for stream in streams:
            later = later_keeps[stream] + swap(later_gives[stream])
            value = own_permute(sums[stream][:2], chain)
            value = later[:2] + value
            value = own_permute(value, chain)
            value = later[2:] + joining[stream] + value
            value = lax.ppermute(value, ("sec", "own"), slanted)
            moving.append(value)
            crossed.append(swap(value[1]))
    carry = jnp.concatenate([value[0] for value in moving], axis=0)
    carry = jnp.where(first_section, 0.0, carry + jnp.concatenate(crossed, axis=0))
    return jnp.concatenate(solved_all, axis=0).reshape(right_sides.shape), carry


def solution(mesh):
    in_specs = (
        P(None, None, ("sec", "own")),
        P(("sec", "own"), None),
        P(("sec", "own"), None),
        P(("sec", "own"), None),
        P("sec", None),
        P(None, ("sec", "own")),
    )
    out_specs = (P(None, None, ("sec", "own")), P(None, ("sec", "own")))
    return jax.shard_map(
        shards,
        mesh=mesh,
        in_specs=in_specs,
        out_specs=out_specs,
        check_vma=False,
    )
```

time: 76.8 us -> 78.4 us (1.021)
  waiting for transfers between devices: 16.7 us -> 27.2 us
  starting transfers between devices: 49.8 us -> 39.6 us
  other arithmetic: 1.78 us -> 2.9 us
    ppermute x28, waiting for transfers between devices: 16.7 us -> 27.2 us  [the longest x24 15.2 us: shards(): own_permute = lambda value, pairs: lax.ppermute(value, 'own', pairs)]
    ppermute x28, starting transfers between devices: 49.8 us -> 39.6 us  [the longest x24 33.4 us: shards(): own_permute = lambda value, pairs: lax.ppermute(value, 'own', pairs)]
    pallas_call x3 -> x2, Pallas kernels: 3.11 us -> 2.06 us  [late_step(): call(kernel, 16, [SMEM] + [VMEM] * (1 + len(parts)), outs, 4)]
    add x16, other arithmetic: 0.38 us -> 1.42 us  [the longest x4 1.09 us: shards(): sums.append(keeps[stream] + swap(gives[stream]))]
    pallas_call x2, Pallas kernels: 1.93 us -> 2.73 us  [next_step(): call(kernel, 6, [SMEM] + [VMEM] * 6, outs, 4)]
  transfers between devices with their start and end apart: 28 -> 28, of which waited for: 13 -> 13; matrix products, arithmetic and copies ran while one was open for 1% -> 3% of each run, Pallas kernels for 5% -> 6%
where the time goes in v1:
time: 78.4 us; the launch traced here: 78.3 us
  starting transfers between devices  39.6 us (51%)
  waiting for transfers between devices  27.2 us (35%)
  Pallas kernels  7.55 us (10%)
  other arithmetic  2.9 us (4%)
  between operations  0.94 us (1%)
    ppermute x24, starting transfers between devices, shards(): own_permute = lambda value, pairs: lax.ppermute(value, 'own', pairs)  33.4 us
    ppermute x24, waiting for transfers between devices, shards(): own_permute = lambda value, pairs: lax.ppermute(value, 'own', pairs)  15.2 us
    ppermute x4, waiting for transfers between devices, shards(): value = lax.ppermute(value, ('sec', 'own'), slanted)  12 us
    ppermute x4, starting transfers between devices, shards(): value = lax.ppermute(value, ('sec', 'own'), slanted)  6.26 us
    pallas_call x1, Pallas kernels, first_step(): call(kernel, 6, [HBM] * 6, outs, 4, scratch)  2.76 us
    pallas_call x2, Pallas kernels, next_step(): call(kernel, 6, [SMEM] + [VMEM] * 6, outs, 4)  2.73 us
    pallas_call x2, Pallas kernels, late_step(): call(kernel, 16, [SMEM] + [VMEM] * (1 + len(parts)), outs, 4)  2.06 us
  transfers between devices with their start and end apart: 28, of which 13 were waited for; matrix products, arithmetic and copies ran while one was open for 3% of the time, Pallas kernels for 6%

profile of v1, /device:TPU:1, one launch (start us, length us, event | category | flops | bytes accessed | tf_op | source)
XLA Modules:
  0.0 78.3 jit_solution(17363722417122014509)
XLA Ops:
  0.6 2.8 %shard_map.77 = (s32[2,16]{1,0:T(2,128)S(1)}, bf16[256,4096]{1,0:T(8,128)(2,1)S(1)}, bf16[256,256]{1,0:T(8,128)(2,1)S(1)}, bf16[256,256]{1,0:T(8,128)(2,1)S(1)},...) custom-call(s32[1,16]{1,0:T(1,128)} %ancestor.1, ...), custom_call_target="tpu_custom_call" | custom-call | flops 201326592 | bytes 786432 | tf_op jit(solution)/shard_map/pallas_call | solution.py:168
  3.4 3.3 %collective-permute-start.1 = (f32[4,64,256]{2,1,0:T(8,128)S(1)}, f32[4,64,256]{2,1,0:T(8,128)S(1)}, u32[]{:S(2)}, u32[]{:S(2)}) collective-permute-start(f32[4,64,256]{2,1,0:T(8,128)S(1)} %get-tuple-element.39), channel_id=1, source_target_pairs={{0,1},{1,0},{2,3},{3,2},{4,5},{5,4},{6,7},{7,6},{8,9},{9,8},{10,11... | collective-permute-start | bytes 786440 | tf_op jit(solution)/shard_map/ppermute | solution.py:226
  6.7 0.1 collective-permute-start.2
  6.8 1.0 %shard_map.78 = (f32[4,64,256]{2,1,0:T(8,128)S(1)}, f32[4,64,256]{2,1,0:T(8,128)S(1)}, f32[4,64,256]{2,1,0:T(8,128)S(1)}, f32[4,64,256]{2,1,0:T(8,128)S(1)}) custom-call(s32[2,16]{1,0:T(2,128)S(1)} %get-tuple-element.33.table, bf16[256,4096]{1,0:T(8,128)(2,1)S(1)} %get-tuple-element.34.factor, bf16[256,256]{1,0:T(8,128)(2,1)S(1)} %get-tuple-element.35.rest_0_), custom_call_target="tpu_custom_call" | custom-call | flops 536870912 | bytes 2097152 | tf_op jit(solution)/shard_map/pallas_call | solution.py:191
  7.8 0.5 collective-permute-start
  8.3 0.1 collective-permute-start.9
  8.4 0.0 collective-permute-done.1
  8.5 0.0 collective-permute-done.2
  8.6 5.1 %collective-permute-start.3 = (f32[128,256]{1,0:T(8,128)S(1)}, f32[128,256]{1,0:T(8,128)S(1)}, u32[]{:S(2)}, u32[]{:S(2)}) collective-permute-start(f32[128,256]{1,0:T(8,128)S(1)} %pad_maximum_fusion.3), channel_id=1, source_target_pairs={{0,7},{1,10},{2,13},{3,8},{4,11},{5,14},{6,1},{7,12},{8,15},{9,2},... | collective-permute-start | bytes 393224 | tf_op jit(solution)/shard_map/ppermute | solution.py:226
  13.7 0.8 %collective-permute-start.4 = (f32[128,256]{1,0:T(8,128)S(1)}, f32[128,256]{1,0:T(8,128)S(1)}, u32[]{:S(2)}, u32[]{:S(2)}) collective-permute-start(f32[128,256]{1,0:T(8,128)S(1)} %pad_maximum_fusion.4), channel_id=1, source_target_pairs={{0,15},{1,2},{2,5},{3,0},{4,3},{5,6},{6,9},{7,4},{8,7},{9,10},{10,... | collective-permute-start | bytes 393224 | tf_op jit(solution)/shard_map/ppermute | solution.py:226
  14.5 2.3 %collective-permute-start.5 = (f32[2,64,256]{2,1,0:T(8,128)S(1)}, f32[2,64,256]{2,1,0:T(8,128)S(1)}, u32[]{:S(2)}, u32[]{:S(2)}) collective-permute-start(f32[2,64,256]{2,1,0:T(8,128)S(1)} %slice.128), channel_id=1, source_target_pairs={{0,3},{1,14},{2,1},{3,4},{4,7},{5,2},{6,5},{7,8},{8,11},{9,6},{10,... | collective-permute-start | bytes 393224 | tf_op jit(solution)/shard_map/ppermute | solution.py:226
  16.8 0.0 copy-start
  16.8 0.0 collective-permute-done
  16.9 0.1 collective-permute-start.10
  17.0 0.0 collective-permute-done.9
  17.0 2.4 %collective-permute-done.3 = f32[128,256]{1,0:T(8,128)S(1)} collective-permute-done((f32[128,256]{1,0:T(8,128)S(1)}, f32[128,256]{1,0:T(8,128)S(1)}, u32[]{:S(2)}, u32[]{:S(2)}) %collective-permute-start.3) | collective-permute-done | bytes 131104 | tf_op jit(solution)/shard_map/ppermute | solution.py:226
  19.4 1.9 %collective-permute-done.4 = f32[128,256]{1,0:T(8,128)S(1)} collective-permute-done((f32[128,256]{1,0:T(8,128)S(1)}, f32[128,256]{1,0:T(8,128)S(1)}, u32[]{:S(2)}, u32[]{:S(2)}) %collective-permute-start.4) | collective-permute-done | bytes 131104 | tf_op jit(solution)/shard_map/ppermute | solution.py:226
  21.3 0.1 collective-permute-done.5
  21.4 3.2 %collective-permute-start.6 = (f32[2,64,256]{2,1,0:T(8,128)S(1)}, f32[2,64,256]{2,1,0:T(8,128)S(1)}, u32[]{:S(2)}, u32[]{:S(2)}) collective-permute-start(f32[2,64,256]{2,1,0:T(8,128)S(1)} %slice_add_fusion.6), channel_id=1, source_target_pairs={{0,3},{1,14},{2,1},{3,4},{4,7},{5,2},{6,5},{7,8},{8,11},{9,6},{10,... | collective-permute-start | bytes 393224 | tf_op jit(solution)/shard_map/ppermute | solution.py:226
  24.6 0.0 collective-permute-done.10
  24.6 1.4 %collective-permute-start.11 = (f32[2,64,256]{2,1,0:T(8,128)S(1)}, f32[2,64,256]{2,1,0:T(8,128)S(1)}, u32[]{:S(2)}, u32[]{:S(2)}) collective-permute-start(f32[2,64,256]{2,1,0:T(8,128)S(1)} %slice_add_fusion.4), channel_id=1, source_target_pairs={{0,3},{1,14},{2,1},{3,4},{4,7},{5,2},{6,5},{7,8},{8,11},{9,6},{10,... | collective-permute-start | bytes 393224 | tf_op jit(solution)/shard_map/ppermute | solution.py:226
  26.0 0.5 collective-permute-done.6
  26.6 4.7 %collective-permute-start.7 = (f32[2,64,256]{2,1,0:T(8,128)S(1)}, f32[2,64,256]{2,1,0:T(8,128)S(1)}, u32[]{:S(2)}, u32[]{:S(2)}) collective-permute-start(f32[2,64,256]{2,1,0:T(8,128)S(1)} %fusion.5), channel_id=1, source_target_pairs={{0,19},{1,30},{2,17},{3,20},{4,23},{5,18},{6,21},{7,24},{8,27},{9,... | collective-permute-start | bytes 393224 | tf_op jit(solution)/shard_map/ppermute | solution.py:273
  31.2 0.0 collective-permute-done.11
  31.3 1.4 %collective-permute-start.12 = (f32[2,64,256]{2,1,0:T(8,128)S(1)}, f32[2,64,256]{2,1,0:T(8,128)S(1)}, u32[]{:S(2)}, u32[]{:S(2)}) collective-permute-start(f32[2,64,256]{2,1,0:T(8,128)S(1)} %fusion.4), channel_id=1, source_target_pairs={{0,19},{1,30},{2,17},{3,20},{4,23},{5,18},{6,21},{7,24},{8,27},{9,... | collective-permute-start | bytes 393224 | tf_op jit(solution)/shard_map/ppermute | solution.py:273
  32.6 3.5 %collective-permute-done.7.moving = f32[2,64,256]{2,1,0:T(8,128)S(1)} collective-permute-done((f32[2,64,256]{2,1,0:T(8,128)S(1)}, f32[2,64,256]{2,1,0:T(8,128)S(1)}, u32[]{:S(2)}, u32[]{:S(2)}) %collective-permute-start.7) | collective-permute-done | bytes 131104 | tf_op jit(solution)/shard_map/ppermute | solution.py:273
  36.1 1.2 %collective-permute-start.8 = (f32[64,256]{1,0:T(8,128)S(1)}, f32[64,256]{1,0:T(8,128)S(1)}, u32[]{:S(2)}, u32[]{:S(2)}) collective-permute-start(f32[64,256]{1,0:T(8,128)S(1)} %slice_bitcast_fusion.9), channel_id=1, source_target_pairs={{0,1},{1,0},{2,3},{3,2},{4,5},{5,4},{6,7},{7,6},{8,9},{9,8},{10,11... | collective-permute-start | bytes 196616 | tf_op jit(solution)/shard_map/ppermute | solution.py:226
  37.4 0.9 %collective-permute-done.8.crossed = f32[64,256]{1,0:T(8,128)S(1)} collective-permute-done((f32[64,256]{1,0:T(8,128)S(1)}, f32[64,256]{1,0:T(8,128)S(1)}, u32[]{:S(2)}, u32[]{:S(2)}) %collective-permute-start.8) | collective-permute-done | bytes 65568 | tf_op jit(solution)/shard_map/ppermute | solution.py:226
  38.3 1.7 %shard_map.79 = (f32[64,256]{1,0:T(8,128)S(1)}, bf16[128,256]{1,0:T(8,128)(2,1)S(1)}, f32[4,64,256]{2,1,0:T(8,128)}, f32[4,64,256]{2,1,0:T(8,128)S(1)}) custom-call(s32[2,16]{1,0:T(2,128)S(1)} %get-tuple-element.33.table, f32[2,128,256]{2,1,0:T(8,128)S(1)} %copy-done, f32[2,64,256]{2,1,0:T(8,128)S(1)} %collective-permute-done.7.moving, ...), custom_call_target="tpu_custom_call" | custom-call | flops 201326592 | bytes 786432 | tf_op jit(solution)/shard_map/pallas_call | solution.py:181
  40.0 0.4 collective-permute-start.15
  40.3 0.0 collective-permute-done.12.moving
  40.3 0.2 collective-permute-start.13
  40.6 1.3 %collective-permute-done.13.crossed = f32[64,256]{1,0:T(8,128)S(1)} collective-permute-done((f32[64,256]{1,0:T(8,128)S(1)}, f32[64,256]{1,0:T(8,128)S(1)}, u32[]{:S(2)}, u32[]{:S(2)}) %collective-permute-start.13) | collective-permute-done | bytes 65568 | tf_op jit(solution)/shard_map/ppermute | solution.py:226
  41.8 1.0 %shard_map.80 = (f32[64,256]{1,0:T(8,128)S(1)}, bf16[128,256]{1,0:T(8,128)(2,1)S(1)}, f32[4,64,256]{2,1,0:T(8,128)S(1)}, f32[4,64,256]{2,1,0:T(8,128)S(1)}) custom-call(s32[2,16]{1,0:T(2,128)S(1)} %get-tuple-element.33.table, f32[2,128,256]{2,1,0:T(8,128)S(1)} %copy-done, f32[2,64,256]{2,1,0:T(8,128)S(1)} %collective-permute-done.12.moving, ...), custom_call_target="tpu_custom_call" | custom-call | flops 201326592 | bytes 786432 | tf_op jit(solution)/shard_map/pallas_call | solution.py:181
  42.9 0.6 collective-permute-start.16
  43.5 1.0 %shard_map.81 = (f32[4,64,256]{2,1,0:T(8,128)S(1)}, f32[4,64,256]{2,1,0:T(8,128)S(1)}, f32[4,64,256]{2,1,0:T(8,128)S(1)}, f32[4,64,256]{2,1,0:T(8,128)S(1)}) custom-call(s32[2,16]{1,0:T(2,128)S(1)} %get-tuple-element.33.table, bf16[256,4096]{1,0:T(8,128)(2,1)S(1)} %get-tuple-element.34.factor, bf16[128,256]{1,0:T(8,128)(2,1)S(1)} %get-tuple-element.50.rest_0_, ...), custom_call_target="tpu_custom_call" | custom-call | flops 536870912 | bytes 2097152 | tf_op jit(solution)/shard_map/pallas_call | solution.py:191
  44.5 0.2 collective-permute-start.14
  44.8 0.4 collective-permute-start.22
  45.1 0.0 collective-permute-done.15
  45.1 1.0 %add.74 = f32[4,64,256]{2,1,0:T(8,128)S(1)} add(f32[4,64,256]{2,1,0:T(8,128)S(1)} %get-tuple-element.54, f32[4,64,256]{2,1,0:T(8,128)} %collective-permute-done.15) | non-fusion elementwise | flops 65536 | bytes 786432 | tf_op jit(solution)/shard_map/add | solution.py:257
  46.2 3.8 %collective-permute-start.19 = (f32[2,64,256]{2,1,0:T(8,128)S(1)}, f32[2,64,256]{2,1,0:T(8,128)S(1)}, u32[]{:S(2)}, u32[]{:S(2)}) collective-permute-start(f32[2,64,256]{2,1,0:T(8,128)S(1)} %slice.142), channel_id=1, source_target_pairs={{0,3},{1,14},{2,1},{3,4},{4,7},{5,2},{6,5},{7,8},{8,11},{9,6},{10,... | collective-permute-start | bytes 393224 | tf_op jit(solution)/shard_map/ppermute | solution.py:226
  49.9 0.0 collective-permute-done.16
  50.0 2.1 %collective-permute-start.17 = (f32[128,256]{1,0:T(8,128)S(1)}, f32[128,256]{1,0:T(8,128)S(1)}, u32[]{:S(2)}, u32[]{:S(2)}) collective-permute-start(f32[128,256]{1,0:T(8,128)S(1)} %pad_maximum_fusion.5), channel_id=1, source_target_pairs={{0,7},{1,10},{2,13},{3,8},{4,11},{5,14},{6,1},{7,12},{8,15},{9,2},... | collective-permute-start | bytes 393224 | tf_op jit(solution)/shard_map/ppermute | solution.py:226
  52.2 0.1 collective-permute-start.18
  52.3 0.0 collective-permute-done.14
  52.3 2.9 %collective-permute-start.23 = (f32[2,64,256]{2,1,0:T(8,128)S(1)}, f32[2,64,256]{2,1,0:T(8,128)S(1)}, u32[]{:S(2)}, u32[]{:S(2)}) collective-permute-start(f32[2,64,256]{2,1,0:T(8,128)S(1)} %slice.146), channel_id=1, source_target_pairs={{0,3},{1,14},{2,1},{3,4},{4,7},{5,2},{6,5},{7,8},{8,11},{9,6},{10,... | collective-permute-start | bytes 393224 | tf_op jit(solution)/shard_map/ppermute | solution.py:226
  55.3 0.0 collective-permute-done.22
  55.3 0.0 collective-permute-done.19
  55.3 0.3 collective-permute-start.20
  55.6 2.7 %collective-permute-done.17 = f32[128,256]{1,0:T(8,128)S(1)} collective-permute-done((f32[128,256]{1,0:T(8,128)S(1)}, f32[128,256]{1,0:T(8,128)S(1)}, u32[]{:S(2)}, u32[]{:S(2)}) %collective-permute-start.17) | collective-permute-done | bytes 131104 | tf_op jit(solution)/shard_map/ppermute | solution.py:226
  58.4 2.6 %collective-permute-done.18 = f32[128,256]{1,0:T(8,128)S(1)} collective-permute-done((f32[128,256]{1,0:T(8,128)S(1)}, f32[128,256]{1,0:T(8,128)S(1)}, u32[]{:S(2)}, u32[]{:S(2)}) %collective-permute-start.18) | collective-permute-done | bytes 131104 | tf_op jit(solution)/shard_map/ppermute | solution.py:226
  61.0 0.0 collective-permute-done.23
  61.0 2.0 %collective-permute-start.24 = (f32[2,64,256]{2,1,0:T(8,128)S(1)}, f32[2,64,256]{2,1,0:T(8,128)S(1)}, u32[]{:S(2)}, u32[]{:S(2)}) collective-permute-start(f32[2,64,256]{2,1,0:T(8,128)S(1)} %slice_add_fusion), channel_id=1, source_target_pairs={{0,3},{1,14},{2,1},{3,4},{4,7},{5,2},{6,5},{7,8},{8,11},{9,6},{10,... | collective-permute-start | bytes 393224 | tf_op jit(solution)/shard_map/ppermute | solution.py:226
  63.0 0.0 collective-permute-done.20
  63.1 0.1 collective-permute-start.21
  63.1 2.6 %collective-permute-done.24 = f32[2,64,256]{2,1,0:T(8,128)S(1)} collective-permute-done((f32[2,64,256]{2,1,0:T(8,128)S(1)}, f32[2,64,256]{2,1,0:T(8,128)S(1)}, u32[]{:S(2)}, u32[]{:S(2)}) %collective-permute-start.24) | collective-permute-done | bytes 131104 | tf_op jit(solution)/shard_map/ppermute | solution.py:226
  65.8 0.1 collective-permute-start.25
  66.0 7.1 %collective-permute-done.21 = f32[2,64,256]{2,1,0:T(8,128)S(1)} collective-permute-done((f32[2,64,256]{2,1,0:T(8,128)S(1)}, f32[2,64,256]{2,1,0:T(8,128)S(1)}, u32[]{:S(2)}, u32[]{:S(2)}) %collective-permute-start.21) | collective-permute-done | bytes 131104 | tf_op jit(solution)/shard_map/ppermute | solution.py:273
  73.0 0.5 collective-permute-start.26
  73.6 1.4 %collective-permute-done.25 = f32[2,64,256]{2,1,0:T(8,128)S(1)} collective-permute-done((f32[2,64,256]{2,1,0:T(8,128)S(1)}, f32[2,64,256]{2,1,0:T(8,128)S(1)}, u32[]{:S(2)}, u32[]{:S(2)}) %collective-permute-start.25) | collective-permute-done | bytes 131104 | tf_op jit(solution)/shard_map/ppermute | solution.py:273
  75.0 1.7 %collective-permute-start.27 = (f32[64,256]{1,0:T(8,128)S(1)}, f32[64,256]{1,0:T(8,128)S(1)}, u32[]{:S(2)}, u32[]{:S(2)}) collective-permute-start(f32[64,256]{1,0:T(8,128)S(1)} %get-tuple-element.76), channel_id=1, source_target_pairs={{0,1},{1,0},{2,3},{3,2},{4,5},{5,4},{6,7},{7,6},{8,9},{9,8},{10,11... | collective-permute-start | bytes 196616 | tf_op jit(solution)/shard_map/ppermute | solution.py:226
  76.7 0.7 pad_maximum_fusion
  77.4 0.2 collective-permute-done.27
  77.6 0.7 fusion.6
  (35 shorter events, 0.6 us)
Async XLA Ops:
  3.4 5.0 %collective-permute-start.1 = (f32[4,64,256]{2,1,0:T(8,128)S(1)}, f32[4,64,256]{2,1,0:T(8,128)S(1)}, u32[]{:S(2)}, u32[]{:S(2)}) collective-permute-start(f32[4,64,256]{2,1,0:T(8,128)S(1)} %get-tuple-element.39), channel_id=1, source_target_pairs={{0,1},{1,0},{2,3},{3,2},{4,5},{5,4},{6,7},{7,6},{8,9},{9,8},{10,11... | collective-permute-start | bytes 786440 | tf_op jit(solution)/shard_map/ppermute | solution.py:226
  6.7 1.8 %collective-permute-start.2 = (f32[4,64,256]{2,1,0:T(8,128)S(1)}, f32[4,64,256]{2,1,0:T(8,128)S(1)}, u32[]{:S(2)}, u32[]{:S(2)}) collective-permute-start(f32[4,64,256]{2,1,0:T(8,128)S(1)} %get-tuple-element.41), channel_id=1, source_target_pairs={{0,1},{1,0},{2,3},{3,2},{4,5},{5,4},{6,7},{7,6},{8,9},{9,8},{10,11... | collective-permute-start | bytes 786440 | tf_op jit(solution)/shard_map/ppermute | solution.py:226
  7.8 9.0 %collective-permute-start = (f32[4,64,256]{2,1,0:T(8,128)S(1)}, f32[4,64,256]{2,1,0:T(8,128)S(1)}, u32[]{:S(2)}, u32[]{:S(2)}) collective-permute-start(f32[4,64,256]{2,1,0:T(8,128)S(1)} %get-tuple-element.37), channel_id=1, source_target_pairs={{0,1},{1,0},{2,3},{3,2},{4,5},{5,4},{6,7},{7,6},{8,9},{9,8},{10,11... | collective-permute-start | bytes 786440 | tf_op jit(solution)/shard_map/ppermute | solution.py:226
  8.3 8.7 %collective-permute-start.9 = (f32[4,64,256]{2,1,0:T(8,128)S(1)}, f32[4,64,256]{2,1,0:T(8,128)S(1)}, u32[]{:S(2)}, u32[]{:S(2)}) collective-permute-start(f32[4,64,256]{2,1,0:T(8,128)S(1)} %get-tuple-element.47), channel_id=1, source_target_pairs={{0,1},{1,0},{2,3},{3,2},{4,5},{5,4},{6,7},{7,6},{8,9},{9,8},{10,11... | collective-permute-start | bytes 786440 | tf_op jit(solution)/shard_map/ppermute | solution.py:226
  8.6 10.8 %collective-permute-start.3 = (f32[128,256]{1,0:T(8,128)S(1)}, f32[128,256]{1,0:T(8,128)S(1)}, u32[]{:S(2)}, u32[]{:S(2)}) collective-permute-start(f32[128,256]{1,0:T(8,128)S(1)} %pad_maximum_fusion.3), channel_id=1, source_target_pairs={{0,7},{1,10},{2,13},{3,8},{4,11},{5,14},{6,1},{7,12},{8,15},{9,2},... | collective-permute-start | bytes 393224 | tf_op jit(solution)/shard_map/ppermute | solution.py:226
  13.7 7.6 %collective-permute-start.4 = (f32[128,256]{1,0:T(8,128)S(1)}, f32[128,256]{1,0:T(8,128)S(1)}, u32[]{:S(2)}, u32[]{:S(2)}) collective-permute-start(f32[128,256]{1,0:T(8,128)S(1)} %pad_maximum_fusion.4), channel_id=1, source_target_pairs={{0,15},{1,2},{2,5},{3,0},{4,3},{5,6},{6,9},{7,4},{8,7},{9,10},{10,... | collective-permute-start | bytes 393224 | tf_op jit(solution)/shard_map/ppermute | solution.py:226
  14.5 6.9 %collective-permute-start.5 = (f32[2,64,256]{2,1,0:T(8,128)S(1)}, f32[2,64,256]{2,1,0:T(8,128)S(1)}, u32[]{:S(2)}, u32[]{:S(2)}) collective-permute-start(f32[2,64,256]{2,1,0:T(8,128)S(1)} %slice.128), channel_id=1, source_target_pairs={{0,3},{1,14},{2,1},{3,4},{4,7},{5,2},{6,5},{7,8},{8,11},{9,6},{10,... | collective-permute-start | bytes 393224 | tf_op jit(solution)/shard_map/ppermute | solution.py:226
  16.8 21.4 %copy-start = (f32[2,128,256]{2,1,0:T(8,128)S(1)}, f32[2,128,256]{2,1,0:T(8,128)}, u32[]{:S(2)}) copy-start(f32[2,128,256]{2,1,0:T(8,128)} %right_sides.5) | copy-start | bytes 786436
  16.9 7.7 %collective-permute-start.10 = (f32[2,64,256]{2,1,0:T(8,128)S(1)}, f32[2,64,256]{2,1,0:T(8,128)S(1)}, u32[]{:S(2)}, u32[]{:S(2)}) collective-permute-start(f32[2,64,256]{2,1,0:T(8,128)S(1)} %slice.132), channel_id=1, source_target_pairs={{0,3},{1,14},{2,1},{3,4},{4,7},{5,2},{6,5},{7,8},{8,11},{9,6},{10,... | collective-permute-start | bytes 393224 | tf_op jit(solution)/shard_map/ppermute | solution.py:226
  21.4 5.1 %collective-permute-start.6 = (f32[2,64,256]{2,1,0:T(8,128)S(1)}, f32[2,64,256]{2,1,0:T(8,128)S(1)}, u32[]{:S(2)}, u32[]{:S(2)}) collective-permute-start(f32[2,64,256]{2,1,0:T(8,128)S(1)} %slice_add_fusion.6), channel_id=1, source_target_pairs={{0,3},{1,14},{2,1},{3,4},{4,7},{5,2},{6,5},{7,8},{8,11},{9,6},{10,... | collective-permute-start | bytes 393224 | tf_op jit(solution)/shard_map/ppermute | solution.py:226
  24.6 6.6 %collective-permute-start.11 = (f32[2,64,256]{2,1,0:T(8,128)S(1)}, f32[2,64,256]{2,1,0:T(8,128)S(1)}, u32[]{:S(2)}, u32[]{:S(2)}) collective-permute-start(f32[2,64,256]{2,1,0:T(8,128)S(1)} %slice_add_fusion.4), channel_id=1, source_target_pairs={{0,3},{1,14},{2,1},{3,4},{4,7},{5,2},{6,5},{7,8},{8,11},{9,6},{10,... | collective-permute-start | bytes 393224 | tf_op jit(solution)/shard_map/ppermute | solution.py:226
  26.6 9.5 %collective-permute-start.7 = (f32[2,64,256]{2,1,0:T(8,128)S(1)}, f32[2,64,256]{2,1,0:T(8,128)S(1)}, u32[]{:S(2)}, u32[]{:S(2)}) collective-permute-start(f32[2,64,256]{2,1,0:T(8,128)S(1)} %fusion.5), channel_id=1, source_target_pairs={{0,19},{1,30},{2,17},{3,20},{4,23},{5,18},{6,21},{7,24},{8,27},{9,... | collective-permute-start | bytes 393224 | tf_op jit(solution)/shard_map/ppermute | solution.py:273
  31.3 9.0 %collective-permute-start.12 = (f32[2,64,256]{2,1,0:T(8,128)S(1)}, f32[2,64,256]{2,1,0:T(8,128)S(1)}, u32[]{:S(2)}, u32[]{:S(2)}) collective-permute-start(f32[2,64,256]{2,1,0:T(8,128)S(1)} %fusion.4), channel_id=1, source_target_pairs={{0,19},{1,30},{2,17},{3,20},{4,23},{5,18},{6,21},{7,24},{8,27},{9,... | collective-permute-start | bytes 393224 | tf_op jit(solution)/shard_map/ppermute | solution.py:273
  36.1 2.2 %collective-permute-start.8 = (f32[64,256]{1,0:T(8,128)S(1)}, f32[64,256]{1,0:T(8,128)S(1)}, u32[]{:S(2)}, u32[]{:S(2)}) collective-permute-start(f32[64,256]{1,0:T(8,128)S(1)} %slice_bitcast_fusion.9), channel_id=1, source_target_pairs={{0,1},{1,0},{2,3},{3,2},{4,5},{5,4},{6,7},{7,6},{8,9},{9,8},{10,11... | collective-permute-start | bytes 196616 | tf_op jit(solution)/shard_map/ppermute | solution.py:226
  40.0 5.2 %collective-permute-start.15 = (f32[4,64,256]{2,1,0:T(8,128)}, f32[4,64,256]{2,1,0:T(8,128)}, u32[]{:S(2)}, u32[]{:S(2)}) collective-permute-start(f32[4,64,256]{2,1,0:T(8,128)} %get-tuple-element.55), channel_id=1, source_target_pairs={{0,1},{1,0},{2,3},{3,2},{4,5},{5,4},{6,7},{7,6},{8,9},{9,8},{10,11... | collective-permute-start | bytes 786440 | tf_op jit(solution)/shard_map/ppermute | solution.py:226
  40.3 1.5 %collective-permute-start.13 = (f32[64,256]{1,0:T(8,128)S(1)}, f32[64,256]{1,0:T(8,128)S(1)}, u32[]{:S(2)}, u32[]{:S(2)}) collective-permute-start(f32[64,256]{1,0:T(8,128)S(1)} %slice_bitcast_fusion.8), channel_id=1, source_target_pairs={{0,1},{1,0},{2,3},{3,2},{4,5},{5,4},{6,7},{7,6},{8,9},{9,8},{10,11... | collective-permute-start | bytes 196616 | tf_op jit(solution)/shard_map/ppermute | solution.py:226
  42.9 7.0 %collective-permute-start.16 = (f32[4,64,256]{2,1,0:T(8,128)S(1)}, f32[4,64,256]{2,1,0:T(8,128)S(1)}, u32[]{:S(2)}, u32[]{:S(2)}) collective-permute-start(f32[4,64,256]{2,1,0:T(8,128)S(1)} %get-tuple-element.57), channel_id=1, source_target_pairs={{0,1},{1,0},{2,3},{3,2},{4,5},{5,4},{6,7},{7,6},{8,9},{9,8},{10,11... | collective-permute-start | bytes 786440 | tf_op jit(solution)/shard_map/ppermute | solution.py:226
  44.5 7.7 %collective-permute-start.14 = (f32[4,64,256]{2,1,0:T(8,128)S(1)}, f32[4,64,256]{2,1,0:T(8,128)S(1)}, u32[]{:S(2)}, u32[]{:S(2)}) collective-permute-start(f32[4,64,256]{2,1,0:T(8,128)S(1)} %get-tuple-element.53), channel_id=1, source_target_pairs={{0,1},{1,0},{2,3},{3,2},{4,5},{5,4},{6,7},{7,6},{8,9},{9,8},{10,11... | collective-permute-start | bytes 786440 | tf_op jit(solution)/shard_map/ppermute | solution.py:226
  44.8 10.5 %collective-permute-start.22 = (f32[4,64,256]{2,1,0:T(8,128)S(1)}, f32[4,64,256]{2,1,0:T(8,128)S(1)}, u32[]{:S(2)}, u32[]{:S(2)}) collective-permute-start(f32[4,64,256]{2,1,0:T(8,128)S(1)} %get-tuple-element.60), channel_id=1, source_target_pairs={{0,1},{1,0},{2,3},{3,2},{4,5},{5,4},{6,7},{7,6},{8,9},{9,8},{10,11... | collective-permute-start | bytes 786440 | tf_op jit(solution)/shard_map/ppermute | solution.py:226
  46.2 9.2 %collective-permute-start.19 = (f32[2,64,256]{2,1,0:T(8,128)S(1)}, f32[2,64,256]{2,1,0:T(8,128)S(1)}, u32[]{:S(2)}, u32[]{:S(2)}) collective-permute-start(f32[2,64,256]{2,1,0:T(8,128)S(1)} %slice.142), channel_id=1, source_target_pairs={{0,3},{1,14},{2,1},{3,4},{4,7},{5,2},{6,5},{7,8},{8,11},{9,6},{10,... | collective-permute-start | bytes 393224 | tf_op jit(solution)/shard_map/ppermute | solution.py:226
  50.0 8.3 %collective-permute-start.17 = (f32[128,256]{1,0:T(8,128)S(1)}, f32[128,256]{1,0:T(8,128)S(1)}, u32[]{:S(2)}, u32[]{:S(2)}) collective-permute-start(f32[128,256]{1,0:T(8,128)S(1)} %pad_maximum_fusion.5), channel_id=1, source_target_pairs={{0,7},{1,10},{2,13},{3,8},{4,11},{5,14},{6,1},{7,12},{8,15},{9,2},... | collective-permute-start | bytes 393224 | tf_op jit(solution)/shard_map/ppermute | solution.py:226
  52.2 8.8 %collective-permute-start.18 = (f32[128,256]{1,0:T(8,128)S(1)}, f32[128,256]{1,0:T(8,128)S(1)}, u32[]{:S(2)}, u32[]{:S(2)}) collective-permute-start(f32[128,256]{1,0:T(8,128)S(1)} %pad_maximum_fusion.6), channel_id=1, source_target_pairs={{0,15},{1,2},{2,5},{3,0},{4,3},{5,6},{6,9},{7,4},{8,7},{9,10},{10,... | collective-permute-start | bytes 393224 | tf_op jit(solution)/shard_map/ppermute | solution.py:226
  52.3 8.7 %collective-permute-start.23 = (f32[2,64,256]{2,1,0:T(8,128)S(1)}, f32[2,64,256]{2,1,0:T(8,128)S(1)}, u32[]{:S(2)}, u32[]{:S(2)}) collective-permute-start(f32[2,64,256]{2,1,0:T(8,128)S(1)} %slice.146), channel_id=1, source_target_pairs={{0,3},{1,14},{2,1},{3,4},{4,7},{5,2},{6,5},{7,8},{8,11},{9,6},{10,... | collective-permute-start | bytes 393224 | tf_op jit(solution)/shard_map/ppermute | solution.py:226
  55.3 7.7 %collective-permute-start.20 = (f32[2,64,256]{2,1,0:T(8,128)S(1)}, f32[2,64,256]{2,1,0:T(8,128)S(1)}, u32[]{:S(2)}, u32[]{:S(2)}) collective-permute-start(f32[2,64,256]{2,1,0:T(8,128)S(1)} %slice_add_fusion.2), channel_id=1, source_target_pairs={{0,3},{1,14},{2,1},{3,4},{4,7},{5,2},{6,5},{7,8},{8,11},{9,6},{10,... | collective-permute-start | bytes 393224 | tf_op jit(solution)/shard_map/ppermute | solution.py:226
  61.0 4.8 %collective-permute-start.24 = (f32[2,64,256]{2,1,0:T(8,128)S(1)}, f32[2,64,256]{2,1,0:T(8,128)S(1)}, u32[]{:S(2)}, u32[]{:S(2)}) collective-permute-start(f32[2,64,256]{2,1,0:T(8,128)S(1)} %slice_add_fusion), channel_id=1, source_target_pairs={{0,3},{1,14},{2,1},{3,4},{4,7},{5,2},{6,5},{7,8},{8,11},{9,6},{10,... | collective-permute-start | bytes 393224 | tf_op jit(solution)/shard_map/ppermute | solution.py:226
  63.1 10.0 %collective-permute-start.21 = (f32[2,64,256]{2,1,0:T(8,128)S(1)}, f32[2,64,256]{2,1,0:T(8,128)S(1)}, u32[]{:S(2)}, u32[]{:S(2)}) collective-permute-start(f32[2,64,256]{2,1,0:T(8,128)S(1)} %fusion.3), channel_id=1, source_target_pairs={{0,19},{1,30},{2,17},{3,20},{4,23},{5,18},{6,21},{7,24},{8,27},{9,... | collective-permute-start | bytes 393224 | tf_op jit(solution)/shard_map/ppermute | solution.py:273
  65.8 9.2 %collective-permute-start.25 = (f32[2,64,256]{2,1,0:T(8,128)S(1)}, f32[2,64,256]{2,1,0:T(8,128)S(1)}, u32[]{:S(2)}, u32[]{:S(2)}) collective-permute-start(f32[2,64,256]{2,1,0:T(8,128)S(1)} %fusion.2), channel_id=1, source_target_pairs={{0,19},{1,30},{2,17},{3,20},{4,23},{5,18},{6,21},{7,24},{8,27},{9,... | collective-permute-start | bytes 393224 | tf_op jit(solution)/shard_map/ppermute | solution.py:273
  73.0 4.4 %collective-permute-start.26 = (f32[64,256]{1,0:T(8,128)S(1)}, f32[64,256]{1,0:T(8,128)S(1)}, u32[]{:S(2)}, u32[]{:S(2)}) collective-permute-start(f32[64,256]{1,0:T(8,128)S(1)} %get-tuple-element.74), channel_id=1, source_target_pairs={{0,1},{1,0},{2,3},{3,2},{4,5},{5,4},{6,7},{7,6},{8,9},{9,8},{10,11... | collective-permute-start | bytes 196616 | tf_op jit(solution)/shard_map/ppermute | solution.py:226
  75.0 2.6 %collective-permute-start.27 = (f32[64,256]{1,0:T(8,128)S(1)}, f32[64,256]{1,0:T(8,128)S(1)}, u32[]{:S(2)}, u32[]{:S(2)}) collective-permute-start(f32[64,256]{1,0:T(8,128)S(1)} %get-tuple-element.76), channel_id=1, source_target_pairs={{0,1},{1,0},{2,3},{3,2},{4,5},{5,4},{6,7},{7,6},{8,9},{9,8},{10,11... | collective-permute-start | bytes 196616 | tf_op jit(solution)/shard_map/ppermute | solution.py:226

commit v2 on v1

--- a/solution.py
+++ b/solution.py
@@ -21,19 +21,17 @@
 
 
 def blocks_of(chips, core, chip, names):
-    ahead = 1 - 2 * ((chip + core) % 2)
+    downward = (chip + core) % 2
     for name in names:
-        if name == "far":
-            yield chips // 2, core
-        elif name == "own":
-            yield 0, 1 - core
+        if name == "side":
+            first, distance = core, chips // 2 * (1 - downward)
         else:
-            first = (core + name) % 2
-            yield name * ahead, first
-            yield name * ahead, 1 - first
-
-
-EARLY = (3, "far", "own")
+            first, distance = (core + name) % 2, name * (1 - 2 * downward)
+        yield distance, first
+        yield distance, 1 - first
+
+
+EARLY = (3, "side")
 LATE = (2, 1)
 
 
@@ -216,13 +214,12 @@
     slanted = to_next_section(next_on_chain)
     first_section = lax.axis_index("sec") == 0
 
-    def on_chain(chips_on):
-        pairs = []
-        for i in range(owners):
-            ahead = 1 - 2 * ((i // 2 + i) % 2)
-            pairs.append((i, (i // 2 + chips_on * ahead) % chips * 2 + 1 - i % 2))
-        return pairs
-
+    def to_side(i):
+        chip, core = i // 2, i % 2
+        chips_on = 1 if (chip + core) % 2 else chips // 2 - 1
+        return (chip + chips_on) % chips * 2 + 1 - core
+
+    beside = [(i, to_side(i)) for i in range(owners)]
     own_permute = lambda value, pairs: lax.ppermute(value, "own", pairs)
     swap = lambda value: own_permute(value, partner)
 
@@ -255,13 +252,10 @@
         sums = []
         for stream in streams:
             sums.append(keeps[stream] + swap(gives[stream]))
-        far = jnp.concatenate([value[2] for value in sums], axis=0)
-        own = jnp.concatenate([value[3] for value in sums], axis=0)
-        far = own_permute(far, on_chain(chips // 2 - 1))
-        own = own_permute(own, on_chain(-1))
-        joining = jnp.stack([far, own])
+        side = jnp.concatenate([value[2:] for value in sums], axis=1)
+        side = own_permute(side, beside)
         joining = lax.optimization_barrier(
-            [joining[:, stream * rows : (stream + 1) * rows] for stream in streams]
+            [side[:, stream * rows : (stream + 1) * rows] for stream in streams]
         )
         moving, crossed = [], []
         for stream in streams:

time: 78.4 us -> 83 us (1.059)
  starting transfers between devices: 39.6 us -> 42.9 us
  waiting for transfers between devices: 27.2 us -> 28.5 us
    ppermute x24 -> x22, starting transfers between devices: 33.4 us -> 36.4 us  [shards(): own_permute = lambda value, pairs: lax.ppermute(value, 'own', pairs)]
    ppermute x24 -> x22, waiting for transfers between devices: 15.2 us -> 17.8 us  [shards(): own_permute = lambda value, pairs: lax.ppermute(value, 'own', pairs)]
    ppermute x4, waiting for transfers between devices: 12 us -> 10.7 us  [shards(): value = lax.ppermute(value, ('sec', 'own'), slanted)]
  transfers between devices with their start and end apart: 28 -> 26, of which waited for: 13 -> 8; matrix products, arithmetic and copies ran while one was open for 3% -> 3% of each run, Pallas kernels for 6% -> 6%
where the time goes in v2:
time: 83 us; the launch traced here: 82.8 us
  starting transfers between devices  42.9 us (52%)
  waiting for transfers between devices  28.5 us (34%)
  Pallas kernels  7.54 us (9%)
  other arithmetic  2.86 us (3%)
  between operations  0.87 us (1%)
    ppermute x22, starting transfers between devices, shards(): own_permute = lambda value, pairs: lax.ppermute(value, 'own', pairs)  36.4 us
    ppermute x22, waiting for transfers between devices, shards(): own_permute = lambda value, pairs: lax.ppermute(value, 'own', pairs)  17.8 us
    ppermute x4, waiting for transfers between devices, shards(): value = lax.ppermute(value, ('sec', 'own'), slanted)  10.7 us
    ppermute x4, starting transfers between devices, shards(): value = lax.ppermute(value, ('sec', 'own'), slanted)  6.59 us
    pallas_call x1, Pallas kernels, first_step(): call(kernel, 6, [HBM] * 6, outs, 4, scratch)  2.75 us
    pallas_call x2, Pallas kernels, next_step(): call(kernel, 6, [SMEM] + [VMEM] * 6, outs, 4)  2.73 us
    pallas_call x2, Pallas kernels, late_step(): call(kernel, 16, [SMEM] + [VMEM] * (1 + len(parts)), outs, 4)  2.05 us
  transfers between devices with their start and end apart: 26, of which 8 were waited for; matrix products, arithmetic and copies ran while one was open for 3% of the time, Pallas kernels for 6%

profile of v2, /device:TPU:1, one launch (start us, length us, event | category | flops | bytes accessed | tf_op | source)
XLA Modules:
  0.0 82.8 jit_solution(920099829130929583)
XLA Ops:
  0.6 2.8 %shard_map.77 = (s32[2,16]{1,0:T(2,128)S(1)}, bf16[256,4096]{1,0:T(8,128)(2,1)S(1)}, bf16[256,256]{1,0:T(8,128)(2,1)S(1)}, bf16[256,256]{1,0:T(8,128)(2,1)S(1)},...) custom-call(s32[1,16]{1,0:T(1,128)} %ancestor.1, ...), custom_call_target="tpu_custom_call" | custom-call | flops 201326592 | bytes 786432 | tf_op jit(solution)/shard_map/pallas_call | solution.py:166
  3.4 3.3 %collective-permute-start.1 = (f32[4,64,256]{2,1,0:T(8,128)S(1)}, f32[4,64,256]{2,1,0:T(8,128)S(1)}, u32[]{:S(2)}, u32[]{:S(2)}) collective-permute-start(f32[4,64,256]{2,1,0:T(8,128)S(1)} %get-tuple-element.39), channel_id=1, source_target_pairs={{0,1},{1,0},{2,3},{3,2},{4,5},{5,4},{6,7},{7,6},{8,9},{9,8},{10,11... | collective-permute-start | bytes 786440 | tf_op jit(solution)/shard_map/ppermute | solution.py:223
  6.7 0.1 collective-permute-start.2
  6.8 1.0 %shard_map.78 = (f32[4,64,256]{2,1,0:T(8,128)S(1)}, f32[4,64,256]{2,1,0:T(8,128)S(1)}, f32[4,64,256]{2,1,0:T(8,128)S(1)}, f32[4,64,256]{2,1,0:T(8,128)S(1)}) custom-call(s32[2,16]{1,0:T(2,128)S(1)} %get-tuple-element.33.table, bf16[256,4096]{1,0:T(8,128)(2,1)S(1)} %get-tuple-element.34.factor, bf16[256,256]{1,0:T(8,128)(2,1)S(1)} %get-tuple-element.35.rest_0_), custom_call_target="tpu_custom_call" | custom-call | flops 536870912 | bytes 2097152 | tf_op jit(solution)/shard_map/pallas_call | solution.py:189
  7.8 0.5 collective-permute-start
  8.3 0.1 collective-permute-start.8
  8.4 0.0 collective-permute-done.1
  8.5 4.2 %collective-permute-start.4 = (f32[2,64,256]{2,1,0:T(8,128)S(1)}, f32[2,64,256]{2,1,0:T(8,128)S(1)}, u32[]{:S(2)}, u32[]{:S(2)}) collective-permute-start(f32[2,64,256]{2,1,0:T(8,128)S(1)} %get-tuple-element.68), channel_id=1, source_target_pairs={{0,3},{1,14},{2,1},{3,4},{4,7},{5,2},{6,5},{7,8},{8,11},{9,6},{10,... | collective-permute-start | bytes 393224 | tf_op jit(solution)/shard_map/ppermute | solution.py:223
  12.7 0.0 collective-permute-done.2
  12.8 0.8 collective-permute-start.9
  13.6 0.0 copy-start
  13.6 1.1 %collective-permute-start.3 = (f32[2,128,256]{2,1,0:T(8,128)S(1)}, f32[2,128,256]{2,1,0:T(8,128)S(1)}, u32[]{:S(2)}, u32[]{:S(2)}) collective-permute-start(f32[2,128,256]{2,1,0:T(8,128)S(1)} %pad_maximum_fusion), channel_id=1, source_target_pairs={{0,7},{1,2},{2,5},{3,8},{4,11},{5,6},{6,9},{7,12},{8,15},{9,10},{1... | collective-permute-start | bytes 786440 | tf_op jit(solution)/shard_map/ppermute | solution.py:223
  14.7 0.0 collective-permute-done
  14.8 0.0 collective-permute-done.8
  14.8 0.0 collective-permute-done.4
  14.8 3.6 %collective-permute-start.5 = (f32[2,64,256]{2,1,0:T(8,128)S(1)}, f32[2,64,256]{2,1,0:T(8,128)S(1)}, u32[]{:S(2)}, u32[]{:S(2)}) collective-permute-start(f32[2,64,256]{2,1,0:T(8,128)S(1)} %slice_add_fusion.6), channel_id=1, source_target_pairs={{0,3},{1,14},{2,1},{3,4},{4,7},{5,2},{6,5},{7,8},{8,11},{9,6},{10,... | collective-permute-start | bytes 393224 | tf_op jit(solution)/shard_map/ppermute | solution.py:223
  18.4 0.0 collective-permute-done.9
  18.4 1.4 %collective-permute-start.10 = (f32[2,64,256]{2,1,0:T(8,128)S(1)}, f32[2,64,256]{2,1,0:T(8,128)S(1)}, u32[]{:S(2)}, u32[]{:S(2)}) collective-permute-start(f32[2,64,256]{2,1,0:T(8,128)S(1)} %slice_add_fusion.4), channel_id=1, source_target_pairs={{0,3},{1,14},{2,1},{3,4},{4,7},{5,2},{6,5},{7,8},{8,11},{9,6},{10,... | collective-permute-start | bytes 393224 | tf_op jit(solution)/shard_map/ppermute | solution.py:223
  19.8 7.0 %collective-permute-done.3 = f32[2,128,256]{2,1,0:T(8,128)S(1)} collective-permute-done((f32[2,128,256]{2,1,0:T(8,128)S(1)}, f32[2,128,256]{2,1,0:T(8,128)S(1)}, u32[]{:S(2)}, u32[]{:S(2)}) %collective-permute-start.3) | collective-permute-done | bytes 262176 | tf_op jit(solution)/shard_map/ppermute | solution.py:223
  26.8 0.0 collective-permute-done.5
  26.9 3.1 %collective-permute-start.6 = (f32[2,64,256]{2,1,0:T(8,128)S(1)}, f32[2,64,256]{2,1,0:T(8,128)S(1)}, u32[]{:S(2)}, u32[]{:S(2)}) collective-permute-start(f32[2,64,256]{2,1,0:T(8,128)S(1)} %fusion.3), channel_id=1, source_target_pairs={{0,19},{1,30},{2,17},{3,20},{4,23},{5,18},{6,21},{7,24},{8,27},{9,... | collective-permute-start | bytes 393224 | tf_op jit(solution)/shard_map/ppermute | solution.py:267
  30.0 0.0 collective-permute-done.10
  30.0 0.1 collective-permute-start.11
  30.2 5.4 %collective-permute-done.6.moving = f32[2,64,256]{2,1,0:T(8,128)S(1)} collective-permute-done((f32[2,64,256]{2,1,0:T(8,128)S(1)}, f32[2,64,256]{2,1,0:T(8,128)S(1)}, u32[]{:S(2)}, u32[]{:S(2)}) %collective-permute-start.6) | collective-permute-done | bytes 131104 | tf_op jit(solution)/shard_map/ppermute | solution.py:267
  35.6 5.6 %collective-permute-start.7 = (f32[64,256]{1,0:T(8,128)S(1)}, f32[64,256]{1,0:T(8,128)S(1)}, u32[]{:S(2)}, u32[]{:S(2)}) collective-permute-start(f32[64,256]{1,0:T(8,128)S(1)} %slice_bitcast_fusion.5), channel_id=1, source_target_pairs={{0,1},{1,0},{2,3},{3,2},{4,5},{5,4},{6,7},{7,6},{8,9},{9,8},{10,11... | collective-permute-start | bytes 196616 | tf_op jit(solution)/shard_map/ppermute | solution.py:223
  41.2 0.9 %collective-permute-done.7.crossed = f32[64,256]{1,0:T(8,128)S(1)} collective-permute-done((f32[64,256]{1,0:T(8,128)S(1)}, f32[64,256]{1,0:T(8,128)S(1)}, u32[]{:S(2)}, u32[]{:S(2)}) %collective-permute-start.7) | collective-permute-done | bytes 65568 | tf_op jit(solution)/shard_map/ppermute | solution.py:223
  42.1 0.0 copy-done
  42.1 1.7 %shard_map.79 = (f32[64,256]{1,0:T(8,128)S(1)}, bf16[128,256]{1,0:T(8,128)(2,1)S(1)}, f32[4,64,256]{2,1,0:T(8,128)}, f32[4,64,256]{2,1,0:T(8,128)S(1)}) custom-call(s32[2,16]{1,0:T(2,128)S(1)} %get-tuple-element.33.table, f32[2,128,256]{2,1,0:T(8,128)S(1)} %copy-done, f32[2,64,256]{2,1,0:T(8,128)S(1)} %collective-permute-done.6.moving, ...), custom_call_target="tpu_custom_call" | custom-call | flops 201326592 | bytes 786432 | tf_op jit(solution)/shard_map/pallas_call | solution.py:179
  43.7 0.4 collective-permute-start.14
  44.1 0.0 collective-permute-done.11.moving
  44.1 0.2 collective-permute-start.12
  44.4 1.3 %collective-permute-done.12.crossed = f32[64,256]{1,0:T(8,128)S(1)} collective-permute-done((f32[64,256]{1,0:T(8,128)S(1)}, f32[64,256]{1,0:T(8,128)S(1)}, u32[]{:S(2)}, u32[]{:S(2)}) %collective-permute-start.12) | collective-permute-done | bytes 65568 | tf_op jit(solution)/shard_map/ppermute | solution.py:223
  45.6 1.0 %shard_map.80 = (f32[64,256]{1,0:T(8,128)S(1)}, bf16[128,256]{1,0:T(8,128)(2,1)S(1)}, f32[4,64,256]{2,1,0:T(8,128)S(1)}, f32[4,64,256]{2,1,0:T(8,128)S(1)}) custom-call(s32[2,16]{1,0:T(2,128)S(1)} %get-tuple-element.33.table, f32[2,128,256]{2,1,0:T(8,128)S(1)} %copy-done, f32[2,64,256]{2,1,0:T(8,128)S(1)} %collective-permute-done.11.moving, ...), custom_call_target="tpu_custom_call" | custom-call | flops 201326592 | bytes 786432 | tf_op jit(solution)/shard_map/pallas_call | solution.py:179
  46.7 0.6 collective-permute-start.15
  47.3 1.0 %shard_map.81 = (f32[4,64,256]{2,1,0:T(8,128)S(1)}, f32[4,64,256]{2,1,0:T(8,128)S(1)}, f32[4,64,256]{2,1,0:T(8,128)S(1)}, f32[4,64,256]{2,1,0:T(8,128)S(1)}) custom-call(s32[2,16]{1,0:T(2,128)S(1)} %get-tuple-element.33.table, bf16[256,4096]{1,0:T(8,128)(2,1)S(1)} %get-tuple-element.34.factor, bf16[128,256]{1,0:T(8,128)(2,1)S(1)} %get-tuple-element.50.rest_0_, ...), custom_call_target="tpu_custom_call" | custom-call | flops 536870912 | bytes 2097152 | tf_op jit(solution)/shard_map/pallas_call | solution.py:189
  48.3 0.2 collective-permute-start.13
  48.6 0.4 collective-permute-start.20
  48.9 0.0 collective-permute-done.14
  48.9 1.0 %add.74 = f32[4,64,256]{2,1,0:T(8,128)S(1)} add(f32[4,64,256]{2,1,0:T(8,128)S(1)} %get-tuple-element.54, f32[4,64,256]{2,1,0:T(8,128)} %collective-permute-done.14) | non-fusion elementwise | flops 65536 | bytes 786432 | tf_op jit(solution)/shard_map/add | solution.py:254
  50.0 0.4 collective-permute-start.17
  50.4 0.0 collective-permute-done.15
  50.5 0.4 collective-permute-start.21
  50.9 1.5 %collective-permute-start.16 = (f32[2,128,256]{2,1,0:T(8,128)S(1)}, f32[2,128,256]{2,1,0:T(8,128)S(1)}, u32[]{:S(2)}, u32[]{:S(2)}) collective-permute-start(f32[2,128,256]{2,1,0:T(8,128)S(1)} %pad_maximum_fusion.2), channel_id=1, source_target_pairs={{0,7},{1,2},{2,5},{3,8},{4,11},{5,6},{6,9},{7,12},{8,15},{9,10},{1... | collective-permute-start | bytes 786440 | tf_op jit(solution)/shard_map/ppermute | solution.py:223
  52.4 0.0 collective-permute-done.13
  52.4 0.0 collective-permute-done.20
  52.5 2.2 %collective-permute-done.17 = f32[2,64,256]{2,1,0:T(8,128)S(1)} collective-permute-done((f32[2,64,256]{2,1,0:T(8,128)S(1)}, f32[2,64,256]{2,1,0:T(8,128)S(1)}, u32[]{:S(2)}, u32[]{:S(2)}) %collective-permute-start.17) | collective-permute-done | bytes 131104 | tf_op jit(solution)/shard_map/ppermute | solution.py:223
  54.7 1.4 %collective-permute-start.18 = (f32[2,64,256]{2,1,0:T(8,128)S(1)}, f32[2,64,256]{2,1,0:T(8,128)S(1)}, u32[]{:S(2)}, u32[]{:S(2)}) collective-permute-start(f32[2,64,256]{2,1,0:T(8,128)S(1)} %slice_add_fusion.2), channel_id=1, source_target_pairs={{0,3},{1,14},{2,1},{3,4},{4,7},{5,2},{6,5},{7,8},{8,11},{9,6},{10,... | collective-permute-start | bytes 393224 | tf_op jit(solution)/shard_map/ppermute | solution.py:223
  56.1 0.0 collective-permute-done.21
  56.1 1.4 %collective-permute-start.22 = (f32[2,64,256]{2,1,0:T(8,128)S(1)}, f32[2,64,256]{2,1,0:T(8,128)S(1)}, u32[]{:S(2)}, u32[]{:S(2)}) collective-permute-start(f32[2,64,256]{2,1,0:T(8,128)S(1)} %slice_add_fusion), channel_id=1, source_target_pairs={{0,3},{1,14},{2,1},{3,4},{4,7},{5,2},{6,5},{7,8},{8,11},{9,6},{10,... | collective-permute-start | bytes 393224 | tf_op jit(solution)/shard_map/ppermute | solution.py:223
  57.5 6.2 %collective-permute-done.16 = f32[2,128,256]{2,1,0:T(8,128)S(1)} collective-permute-done((f32[2,128,256]{2,1,0:T(8,128)S(1)}, f32[2,128,256]{2,1,0:T(8,128)S(1)}, u32[]{:S(2)}, u32[]{:S(2)}) %collective-permute-start.16) | collective-permute-done | bytes 262176 | tf_op jit(solution)/shard_map/ppermute | solution.py:223
  63.7 0.0 collective-permute-done.18
  63.7 0.1 collective-permute-start.19
  63.8 0.0 collective-permute-done.22
  63.9 3.2 %collective-permute-start.23 = (f32[2,64,256]{2,1,0:T(8,128)S(1)}, f32[2,64,256]{2,1,0:T(8,128)S(1)}, u32[]{:S(2)}, u32[]{:S(2)}) collective-permute-start(f32[2,64,256]{2,1,0:T(8,128)S(1)} %fusion), channel_id=1, source_target_pairs={{0,19},{1,30},{2,17},{3,20},{4,23},{5,18},{6,21},{7,24},{8,27},{9,... | collective-permute-start | bytes 393224 | tf_op jit(solution)/shard_map/ppermute | solution.py:267
  67.1 5.3 %collective-permute-done.19 = f32[2,64,256]{2,1,0:T(8,128)S(1)} collective-permute-done((f32[2,64,256]{2,1,0:T(8,128)S(1)}, f32[2,64,256]{2,1,0:T(8,128)S(1)}, u32[]{:S(2)}, u32[]{:S(2)}) %collective-permute-start.19) | collective-permute-done | bytes 131104 | tf_op jit(solution)/shard_map/ppermute | solution.py:267
  72.4 7.4 %collective-permute-start.24 = (f32[64,256]{1,0:T(8,128)S(1)}, f32[64,256]{1,0:T(8,128)S(1)}, u32[]{:S(2)}, u32[]{:S(2)}) collective-permute-start(f32[64,256]{1,0:T(8,128)S(1)} %get-tuple-element.74), channel_id=1, source_target_pairs={{0,1},{1,0},{2,3},{3,2},{4,5},{5,4},{6,7},{7,6},{8,9},{9,8},{10,11... | collective-permute-start | bytes 196616 | tf_op jit(solution)/shard_map/ppermute | solution.py:223
  79.9 0.0 collective-permute-done.23
  79.9 1.4 %collective-permute-start.25 = (f32[64,256]{1,0:T(8,128)S(1)}, f32[64,256]{1,0:T(8,128)S(1)}, u32[]{:S(2)}, u32[]{:S(2)}) collective-permute-start(f32[64,256]{1,0:T(8,128)S(1)} %get-tuple-element.76), channel_id=1, source_target_pairs={{0,1},{1,0},{2,3},{3,2},{4,5},{5,4},{6,7},{7,6},{8,9},{9,8},{10,11... | collective-permute-start | bytes 196616 | tf_op jit(solution)/shard_map/ppermute | solution.py:223
  81.3 0.7 pad_maximum_fusion.1
  82.0 0.0 collective-permute-done.24
  82.0 0.2 collective-permute-done.25
  82.2 0.7 fusion.4
  (27 shorter events, 0.6 us)
Async XLA Ops:
  3.4 5.0 %collective-permute-start.1 = (f32[4,64,256]{2,1,0:T(8,128)S(1)}, f32[4,64,256]{2,1,0:T(8,128)S(1)}, u32[]{:S(2)}, u32[]{:S(2)}) collective-permute-start(f32[4,64,256]{2,1,0:T(8,128)S(1)} %get-tuple-element.39), channel_id=1, source_target_pairs={{0,1},{1,0},{2,3},{3,2},{4,5},{5,4},{6,7},{7,6},{8,9},{9,8},{10,11... | collective-permute-start | bytes 786440 | tf_op jit(solution)/shard_map/ppermute | solution.py:223
  6.7 6.0 %collective-permute-start.2 = (f32[4,64,256]{2,1,0:T(8,128)S(1)}, f32[4,64,256]{2,1,0:T(8,128)S(1)}, u32[]{:S(2)}, u32[]{:S(2)}) collective-permute-start(f32[4,64,256]{2,1,0:T(8,128)S(1)} %get-tuple-element.41), channel_id=1, source_target_pairs={{0,1},{1,0},{2,3},{3,2},{4,5},{5,4},{6,7},{7,6},{8,9},{9,8},{10,11... | collective-permute-start | bytes 786440 | tf_op jit(solution)/shard_map/ppermute | solution.py:223
  7.8 6.9 %collective-permute-start = (f32[4,64,256]{2,1,0:T(8,128)S(1)}, f32[4,64,256]{2,1,0:T(8,128)S(1)}, u32[]{:S(2)}, u32[]{:S(2)}) collective-permute-start(f32[4,64,256]{2,1,0:T(8,128)S(1)} %get-tuple-element.37), channel_id=1, source_target_pairs={{0,1},{1,0},{2,3},{3,2},{4,5},{5,4},{6,7},{7,6},{8,9},{9,8},{10,11... | collective-permute-start | bytes 786440 | tf_op jit(solution)/shard_map/ppermute | solution.py:223
  8.3 6.5 %collective-permute-start.8 = (f32[4,64,256]{2,1,0:T(8,128)S(1)}, f32[4,64,256]{2,1,0:T(8,128)S(1)}, u32[]{:S(2)}, u32[]{:S(2)}) collective-permute-start(f32[4,64,256]{2,1,0:T(8,128)S(1)} %get-tuple-element.47), channel_id=1, source_target_pairs={{0,1},{1,0},{2,3},{3,2},{4,5},{5,4},{6,7},{7,6},{8,9},{9,8},{10,11... | collective-permute-start | bytes 786440 | tf_op jit(solution)/shard_map/ppermute | solution.py:223
  8.5 6.3 %collective-permute-start.4 = (f32[2,64,256]{2,1,0:T(8,128)S(1)}, f32[2,64,256]{2,1,0:T(8,128)S(1)}, u32[]{:S(2)}, u32[]{:S(2)}) collective-permute-start(f32[2,64,256]{2,1,0:T(8,128)S(1)} %get-tuple-element.68), channel_id=1, source_target_pairs={{0,3},{1,14},{2,1},{3,4},{4,7},{5,2},{6,5},{7,8},{8,11},{9,6},{10,... | collective-permute-start | bytes 393224 | tf_op jit(solution)/shard_map/ppermute | solution.py:223
  12.8 5.6 %collective-permute-start.9 = (f32[2,64,256]{2,1,0:T(8,128)S(1)}, f32[2,64,256]{2,1,0:T(8,128)S(1)}, u32[]{:S(2)}, u32[]{:S(2)}) collective-permute-start(f32[2,64,256]{2,1,0:T(8,128)S(1)} %get-tuple-element.73), channel_id=1, source_target_pairs={{0,3},{1,14},{2,1},{3,4},{4,7},{5,2},{6,5},{7,8},{8,11},{9,6},{10,... | collective-permute-start | bytes 393224 | tf_op jit(solution)/shard_map/ppermute | solution.py:223
  13.6 28.5 %copy-start = (f32[2,128,256]{2,1,0:T(8,128)S(1)}, f32[2,128,256]{2,1,0:T(8,128)}, u32[]{:S(2)}) copy-start(f32[2,128,256]{2,1,0:T(8,128)} %right_sides.5) | copy-start | bytes 786436
  13.6 13.2 %collective-permute-start.3 = (f32[2,128,256]{2,1,0:T(8,128)S(1)}, f32[2,128,256]{2,1,0:T(8,128)S(1)}, u32[]{:S(2)}, u32[]{:S(2)}) collective-permute-start(f32[2,128,256]{2,1,0:T(8,128)S(1)} %pad_maximum_fusion), channel_id=1, source_target_pairs={{0,7},{1,2},{2,5},{3,8},{4,11},{5,6},{6,9},{7,12},{8,15},{9,10},{1... | collective-permute-start | bytes 786440 | tf_op jit(solution)/shard_map/ppermute | solution.py:223
  14.8 12.0 %collective-permute-start.5 = (f32[2,64,256]{2,1,0:T(8,128)S(1)}, f32[2,64,256]{2,1,0:T(8,128)S(1)}, u32[]{:S(2)}, u32[]{:S(2)}) collective-permute-start(f32[2,64,256]{2,1,0:T(8,128)S(1)} %slice_add_fusion.6), channel_id=1, source_target_pairs={{0,3},{1,14},{2,1},{3,4},{4,7},{5,2},{6,5},{7,8},{8,11},{9,6},{10,... | collective-permute-start | bytes 393224 | tf_op jit(solution)/shard_map/ppermute | solution.py:223
  18.4 11.6 %collective-permute-start.10 = (f32[2,64,256]{2,1,0:T(8,128)S(1)}, f32[2,64,256]{2,1,0:T(8,128)S(1)}, u32[]{:S(2)}, u32[]{:S(2)}) collective-permute-start(f32[2,64,256]{2,1,0:T(8,128)S(1)} %slice_add_fusion.4), channel_id=1, source_target_pairs={{0,3},{1,14},{2,1},{3,4},{4,7},{5,2},{6,5},{7,8},{8,11},{9,6},{10,... | collective-permute-start | bytes 393224 | tf_op jit(solution)/shard_map/ppermute | solution.py:223
  26.9 8.7 %collective-permute-start.6 = (f32[2,64,256]{2,1,0:T(8,128)S(1)}, f32[2,64,256]{2,1,0:T(8,128)S(1)}, u32[]{:S(2)}, u32[]{:S(2)}) collective-permute-start(f32[2,64,256]{2,1,0:T(8,128)S(1)} %fusion.3), channel_id=1, source_target_pairs={{0,19},{1,30},{2,17},{3,20},{4,23},{5,18},{6,21},{7,24},{8,27},{9,... | collective-permute-start | bytes 393224 | tf_op jit(solution)/shard_map/ppermute | solution.py:267
  30.0 14.1 %collective-permute-start.11 = (f32[2,64,256]{2,1,0:T(8,128)S(1)}, f32[2,64,256]{2,1,0:T(8,128)S(1)}, u32[]{:S(2)}, u32[]{:S(2)}) collective-permute-start(f32[2,64,256]{2,1,0:T(8,128)S(1)} %fusion.2), channel_id=1, source_target_pairs={{0,19},{1,30},{2,17},{3,20},{4,23},{5,18},{6,21},{7,24},{8,27},{9,... | collective-permute-start | bytes 393224 | tf_op jit(solution)/shard_map/ppermute | solution.py:267
  35.6 6.5 %collective-permute-start.7 = (f32[64,256]{1,0:T(8,128)S(1)}, f32[64,256]{1,0:T(8,128)S(1)}, u32[]{:S(2)}, u32[]{:S(2)}) collective-permute-start(f32[64,256]{1,0:T(8,128)S(1)} %slice_bitcast_fusion.5), channel_id=1, source_target_pairs={{0,1},{1,0},{2,3},{3,2},{4,5},{5,4},{6,7},{7,6},{8,9},{9,8},{10,11... | collective-permute-start | bytes 196616 | tf_op jit(solution)/shard_map/ppermute | solution.py:223
  43.7 5.2 %collective-permute-start.14 = (f32[4,64,256]{2,1,0:T(8,128)}, f32[4,64,256]{2,1,0:T(8,128)}, u32[]{:S(2)}, u32[]{:S(2)}) collective-permute-start(f32[4,64,256]{2,1,0:T(8,128)} %get-tuple-element.55), channel_id=1, source_target_pairs={{0,1},{1,0},{2,3},{3,2},{4,5},{5,4},{6,7},{7,6},{8,9},{9,8},{10,11... | collective-permute-start | bytes 786440 | tf_op jit(solution)/shard_map/ppermute | solution.py:223
  44.1 1.5 %collective-permute-start.12 = (f32[64,256]{1,0:T(8,128)S(1)}, f32[64,256]{1,0:T(8,128)S(1)}, u32[]{:S(2)}, u32[]{:S(2)}) collective-permute-start(f32[64,256]{1,0:T(8,128)S(1)} %slice_bitcast_fusion.4), channel_id=1, source_target_pairs={{0,1},{1,0},{2,3},{3,2},{4,5},{5,4},{6,7},{7,6},{8,9},{9,8},{10,11... | collective-permute-start | bytes 196616 | tf_op jit(solution)/shard_map/ppermute | solution.py:223
  46.7 3.7 %collective-permute-start.15 = (f32[4,64,256]{2,1,0:T(8,128)S(1)}, f32[4,64,256]{2,1,0:T(8,128)S(1)}, u32[]{:S(2)}, u32[]{:S(2)}) collective-permute-start(f32[4,64,256]{2,1,0:T(8,128)S(1)} %get-tuple-element.57), channel_id=1, source_target_pairs={{0,1},{1,0},{2,3},{3,2},{4,5},{5,4},{6,7},{7,6},{8,9},{9,8},{10,11... | collective-permute-start | bytes 786440 | tf_op jit(solution)/shard_map/ppermute | solution.py:223
  48.3 4.1 %collective-permute-start.13 = (f32[4,64,256]{2,1,0:T(8,128)S(1)}, f32[4,64,256]{2,1,0:T(8,128)S(1)}, u32[]{:S(2)}, u32[]{:S(2)}) collective-permute-start(f32[4,64,256]{2,1,0:T(8,128)S(1)} %get-tuple-element.53), channel_id=1, source_target_pairs={{0,1},{1,0},{2,3},{3,2},{4,5},{5,4},{6,7},{7,6},{8,9},{9,8},{10,11... | collective-permute-start | bytes 786440 | tf_op jit(solution)/shard_map/ppermute | solution.py:223
  48.6 3.9 %collective-permute-start.20 = (f32[4,64,256]{2,1,0:T(8,128)S(1)}, f32[4,64,256]{2,1,0:T(8,128)S(1)}, u32[]{:S(2)}, u32[]{:S(2)}) collective-permute-start(f32[4,64,256]{2,1,0:T(8,128)S(1)} %get-tuple-element.60), channel_id=1, source_target_pairs={{0,1},{1,0},{2,3},{3,2},{4,5},{5,4},{6,7},{7,6},{8,9},{9,8},{10,11... | collective-permute-start | bytes 786440 | tf_op jit(solution)/shard_map/ppermute | solution.py:223
  50.0 4.8 %collective-permute-start.17 = (f32[2,64,256]{2,1,0:T(8,128)S(1)}, f32[2,64,256]{2,1,0:T(8,128)S(1)}, u32[]{:S(2)}, u32[]{:S(2)}) collective-permute-start(f32[2,64,256]{2,1,0:T(8,128)S(1)} %get-tuple-element.62), channel_id=1, source_target_pairs={{0,3},{1,14},{2,1},{3,4},{4,7},{5,2},{6,5},{7,8},{8,11},{9,6},{10,... | collective-permute-start | bytes 393224 | tf_op jit(solution)/shard_map/ppermute | solution.py:223
  50.5 5.7 %collective-permute-start.21 = (f32[2,64,256]{2,1,0:T(8,128)S(1)}, f32[2,64,256]{2,1,0:T(8,128)S(1)}, u32[]{:S(2)}, u32[]{:S(2)}) collective-permute-start(f32[2,64,256]{2,1,0:T(8,128)S(1)} %get-tuple-element.67), channel_id=1, source_target_pairs={{0,3},{1,14},{2,1},{3,4},{4,7},{5,2},{6,5},{7,8},{8,11},{9,6},{10,... | collective-permute-start | bytes 393224 | tf_op jit(solution)/shard_map/ppermute | solution.py:223
  50.9 12.8 %collective-permute-start.16 = (f32[2,128,256]{2,1,0:T(8,128)S(1)}, f32[2,128,256]{2,1,0:T(8,128)S(1)}, u32[]{:S(2)}, u32[]{:S(2)}) collective-permute-start(f32[2,128,256]{2,1,0:T(8,128)S(1)} %pad_maximum_fusion.2), channel_id=1, source_target_pairs={{0,7},{1,2},{2,5},{3,8},{4,11},{5,6},{6,9},{7,12},{8,15},{9,10},{1... | collective-permute-start | bytes 786440 | tf_op jit(solution)/shard_map/ppermute | solution.py:223
  54.7 8.9 %collective-permute-start.18 = (f32[2,64,256]{2,1,0:T(8,128)S(1)}, f32[2,64,256]{2,1,0:T(8,128)S(1)}, u32[]{:S(2)}, u32[]{:S(2)}) collective-permute-start(f32[2,64,256]{2,1,0:T(8,128)S(1)} %slice_add_fusion.2), channel_id=1, source_target_pairs={{0,3},{1,14},{2,1},{3,4},{4,7},{5,2},{6,5},{7,8},{8,11},{9,6},{10,... | collective-permute-start | bytes 393224 | tf_op jit(solution)/shard_map/ppermute | solution.py:223
  56.1 7.7 %collective-permute-start.22 = (f32[2,64,256]{2,1,0:T(8,128)S(1)}, f32[2,64,256]{2,1,0:T(8,128)S(1)}, u32[]{:S(2)}, u32[]{:S(2)}) collective-permute-start(f32[2,64,256]{2,1,0:T(8,128)S(1)} %slice_add_fusion), channel_id=1, source_target_pairs={{0,3},{1,14},{2,1},{3,4},{4,7},{5,2},{6,5},{7,8},{8,11},{9,6},{10,... | collective-permute-start | bytes 393224 | tf_op jit(solution)/shard_map/ppermute | solution.py:223
  63.7 8.7 %collective-permute-start.19 = (f32[2,64,256]{2,1,0:T(8,128)S(1)}, f32[2,64,256]{2,1,0:T(8,128)S(1)}, u32[]{:S(2)}, u32[]{:S(2)}) collective-permute-start(f32[2,64,256]{2,1,0:T(8,128)S(1)} %fusion.1), channel_id=1, source_target_pairs={{0,19},{1,30},{2,17},{3,20},{4,23},{5,18},{6,21},{7,24},{8,27},{9,... | collective-permute-start | bytes 393224 | tf_op jit(solution)/shard_map/ppermute | solution.py:267
  63.9 16.0 %collective-permute-start.23 = (f32[2,64,256]{2,1,0:T(8,128)S(1)}, f32[2,64,256]{2,1,0:T(8,128)S(1)}, u32[]{:S(2)}, u32[]{:S(2)}) collective-permute-start(f32[2,64,256]{2,1,0:T(8,128)S(1)} %fusion), channel_id=1, source_target_pairs={{0,19},{1,30},{2,17},{3,20},{4,23},{5,18},{6,21},{7,24},{8,27},{9,... | collective-permute-start | bytes 393224 | tf_op jit(solution)/shard_map/ppermute | solution.py:267
  72.4 9.6 %collective-permute-start.24 = (f32[64,256]{1,0:T(8,128)S(1)}, f32[64,256]{1,0:T(8,128)S(1)}, u32[]{:S(2)}, u32[]{:S(2)}) collective-permute-start(f32[64,256]{1,0:T(8,128)S(1)} %get-tuple-element.74), channel_id=1, source_target_pairs={{0,1},{1,0},{2,3},{3,2},{4,5},{5,4},{6,7},{7,6},{8,9},{9,8},{10,11... | collective-permute-start | bytes 196616 | tf_op jit(solution)/shard_map/ppermute | solution.py:223
  79.9 2.3 %collective-permute-start.25 = (f32[64,256]{1,0:T(8,128)S(1)}, f32[64,256]{1,0:T(8,128)S(1)}, u32[]{:S(2)}, u32[]{:S(2)}) collective-permute-start(f32[64,256]{1,0:T(8,128)S(1)} %get-tuple-element.76), channel_id=1, source_target_pairs={{0,1},{1,0},{2,3},{3,2},{4,5},{5,4},{6,7},{7,6},{8,9},{9,8},{10,11... | collective-permute-start | bytes 196616 | tf_op jit(solution)/shard_map/ppermute | solution.py:223

commit v3 on v1

--- a/solution.py
+++ b/solution.py
@@ -33,7 +33,8 @@
             yield name * ahead, 1 - first
 
 
-EARLY = (3, "far", "own")
+EARLY = (3,)
+SIDE = ("far", "own")
 LATE = (2, 1)
 
 
@@ -71,8 +72,8 @@
     chips, streams, ancestor, structure, right_sides, carried, inverse, factor,
     table, factor_here, inverse_high, inverse_low, solved, lhs, *rest,
 ):
-    gives, keeps = rest[:streams], rest[streams : 2 * streams]
-    slots, present, right_here, carried_here, inverse_here, sems = rest[2 * streams :]
+    outs = [rest[i * streams : (i + 1) * streams] for i in range(4)]
+    slots, present, right_here, carried_here, inverse_here, sems = rest[4 * streams :]
     chunk = factor.shape[0] // 4
     pairs = [
         (inverse, inverse_here),
@@ -103,12 +104,13 @@
         table[1, slots[0, slot]] = present[0, slot]
     for copy in copies[5:]:
         copy.wait()
-    put(table, lhs[...], factor_here, chips, EARLY, gives, keeps)
+    put(table, lhs[...], factor_here, chips, EARLY, *outs[:2])
+    put(table, lhs[...], factor_here, chips, SIDE, *outs[2:])
 
 
 def next_kernel(
     chips, tick, first_row, table, right_sides, moving, crossed,
-    inverse_high, inverse_low, factor, solved, lhs, give, keep,
+    inverse_high, inverse_low, factor, solved, lhs, *outs,
 ):
     here = pl.ds(first_row, solved.shape[0])
     incoming = moving[0] + crossed[...]
@@ -116,7 +118,9 @@
     solved[...], lhs[...] = solve(
         right_sides[tick, here] - incoming, inverse_high[...], inverse_low[...], 1
     )
-    put(table, lhs[...], factor, chips, EARLY, [give], [keep])
+    outs = [[out] for out in outs]
+    put(table, lhs[...], factor, chips, EARLY, *outs[:2])
+    put(table, lhs[...], factor, chips, SIDE, *outs[2:])
 
 
 def late_kernel(chips, streams, table, factor, *rest):
@@ -155,7 +159,7 @@
     square = (block, block)
     outs = [jax.ShapeDtypeStruct((2, slots), jnp.int32), BF16(factor.shape)]
     outs += [BF16(square)] * 2 + [F32((width, block)), BF16((2 * width, block))]
-    outs += [F32((4, rows, block))] * (2 * streams)
+    outs += [F32((2, rows, block))] * (4 * streams)
     scratch = [
         pltpu.SMEM((1, slots), jnp.int32),
         pltpu.SMEM((1, slots), jnp.int32),
@@ -169,14 +173,14 @@
         *[pltpu.with_memory_space_constraint(array, pltpu.HBM) for array in arrays]
     )
     fixed, (solved, lhs) = out[:4], out[4:6]
-    return fixed, solved, lhs, out[6 : 6 + streams], out[6 + streams :]
+    return fixed, solved, lhs, [out[i::streams] for i in range(6, 6 + streams)]
 
 
 def next_step(chips, tick, first_row, fixed, right_sides, moving, crossed):
     table, factor, inverse_high, inverse_low = fixed
     rows, block = crossed.shape
     outs = [F32((rows, block)), BF16((2 * rows, block))]
-    outs += [F32((4, rows, block))] * 2
+    outs += [F32((2, rows, block))] * 4
     kernel = functools.partial(next_kernel, chips, tick, first_row)
     return call(kernel, 6, [SMEM] + [VMEM] * 6, outs, 4)(
         table, right_sides, moving, crossed, inverse_high, inverse_low, factor
@@ -232,7 +236,7 @@
     solved_all = []
     for tick in range(ticks):
         if tick == 0:
-            fixed, solved, lhs, gives, keeps = first_step(
+            fixed, solved, lhs, outs = first_step(
                 chips,
                 STREAMS,
                 rows,
@@ -241,22 +245,23 @@
             solved_all.append(solved)
             parts = [lhs]
         else:
-            gives, keeps, parts = [], [], []
+            outs, parts = [], []
             for stream in streams:
-                solved, lhs, give, keep = next_step(
+                solved, lhs, *out = next_step(
                     chips, tick, stream * rows, fixed, right_sides,
                     moving[stream], crossed[stream],
                 )
                 solved_all.append(solved)
-                gives.append(give)
-                keeps.append(keep)
+                outs.append(out)
                 parts.append(lhs)
         later_gives, later_keeps = late_step(chips, STREAMS, fixed, parts)
-        sums = []
+        sums, sides = [], []
         for stream in streams:
-            sums.append(keeps[stream] + swap(gives[stream]))
-        far = jnp.concatenate([value[2] for value in sums], axis=0)
-        own = jnp.concatenate([value[3] for value in sums], axis=0)
+            give, keep, side_give, side_keep = outs[stream]
+            sums.append(keep + swap(give))
+            sides.append(side_keep + swap(side_give))
+        far = jnp.concatenate([value[0] for value in sides], axis=0)
+        own = jnp.concatenate([value[1] for value in sides], axis=0)
         far = own_permute(far, on_chain(chips // 2 - 1))
         own = own_permute(own, on_chain(-1))
         joining = jnp.stack([far, own])
@@ -266,7 +271,7 @@
         moving, crossed = [], []
         for stream in streams:
             later = later_keeps[stream] + swap(later_gives[stream])
-            value = own_permute(sums[stream][:2], chain)
+            value = own_permute(sums[stream], chain)
             value = later[:2] + value
             value = own_permute(value, chain)
             value = later[2:] + joining[stream] + value

time: 78.4 us -> 78.5 us (level)
  starting transfers between devices: 39.6 us -> 50.2 us
  waiting for transfers between devices: 27.2 us -> 18.4 us
  other arithmetic: 2.9 us -> 1.95 us
    ppermute x24 -> x28, waiting for transfers between devices: 15.2 us -> 5.49 us  [shards(): own_permute = lambda value, pairs: lax.ppermute(value, 'own', pairs)]
    ppermute x24 -> x28, starting transfers between devices: 33.4 us -> 42.5 us  [shards(): own_permute = lambda value, pairs: lax.ppermute(value, 'own', pairs)]
    ppermute x4, starting transfers between devices: 6.26 us -> 7.73 us  [shards(): value = lax.ppermute(value, ('sec', 'own'), slanted)]
    ppermute x4, waiting for transfers between devices: 12 us -> 12.9 us  [shards(): value = lax.ppermute(value, ('sec', 'own'), slanted)]
    add x4 -> x8, other arithmetic: 1.09 us -> 0.15 us  [the longest x4 0.08 us: shards(): sides.append(side_keep + swap(side_give))]
  transfers between devices with their start and end apart: 28 -> 32, of which waited for: 13 -> 10; matrix products, arithmetic and copies ran while one was open for 3% -> 2% of each run, Pallas kernels for 6% -> 5%
where the time goes in v3:
time: 78.5 us; the launch traced here: 78.4 us
  starting transfers between devices  50.2 us (64%)
  waiting for transfers between devices  18.4 us (23%)
  Pallas kernels  6.85 us (9%)
  other arithmetic  1.95 us (2%)
  between operations  0.94 us (1%)
    ppermute x28, starting transfers between devices, shards(): own_permute = lambda value, pairs: lax.ppermute(value, 'own', pairs)  42.5 us
    ppermute x4, waiting for transfers between devices, shards(): value = lax.ppermute(value, ('sec', 'own'), slanted)  12.9 us
    ppermute x4, starting transfers between devices, shards(): value = lax.ppermute(value, ('sec', 'own'), slanted)  7.73 us
    ppermute x28, waiting for transfers between devices, shards(): own_permute = lambda value, pairs: lax.ppermute(value, 'own', pairs)  5.49 us
    pallas_call x1, Pallas kernels, first_step(): call(kernel, 6, [HBM] * 6, outs, 4, scratch)  2.69 us
    pallas_call x2, Pallas kernels, next_step(): call(kernel, 6, [SMEM] + [VMEM] * 6, outs, 4)  2.11 us
    pallas_call x2, Pallas kernels, late_step(): call(kernel, 16, [SMEM] + [VMEM] * (1 + len(parts)), outs, 4)  2.05 us
  transfers between devices with their start and end apart: 32, of which 10 were waited for; matrix products, arithmetic and copies ran while one was open for 2% of the time, Pallas kernels for 5%

profile of v3, /device:TPU:1, one launch (start us, length us, event | category | flops | bytes accessed | tf_op | source)
XLA Modules:
  0.0 78.4 jit_solution(8672336804560582052)
XLA Ops:
  0.6 2.7 %shard_map.77 = (s32[2,16]{1,0:T(2,128)S(1)}, bf16[256,4096]{1,0:T(8,128)(2,1)S(1)}, bf16[256,256]{1,0:T(8,128)(2,1)S(1)}, bf16[256,256]{1,0:T(8,128)(2,1)S(1)},...) custom-call(s32[1,16]{1,0:T(1,128)} %ancestor.1, ...), custom_call_target="tpu_custom_call" | custom-call | flops 201326592 | bytes 786432 | tf_op jit(solution)/shard_map/pallas_call | solution.py:172
  3.3 3.3 %collective-permute-start.1 = (f32[2,64,256]{2,1,0:T(8,128)S(1)}, f32[2,64,256]{2,1,0:T(8,128)S(1)}, u32[]{:S(2)}, u32[]{:S(2)}) collective-permute-start(f32[2,64,256]{2,1,0:T(8,128)S(1)} %get-tuple-element.47), channel_id=1, source_target_pairs={{0,1},{1,0},{2,3},{3,2},{4,5},{5,4},{6,7},{7,6},{8,9},{9,8},{10,11... | collective-permute-start | bytes 393224 | tf_op jit(solution)/shard_map/ppermute | solution.py:230
  6.6 0.1 collective-permute-start.2
  6.7 0.4 collective-permute-start.5
  7.1 0.1 collective-permute-start.11
  7.2 1.0 %shard_map.78 = (f32[4,64,256]{2,1,0:T(8,128)S(1)}, f32[4,64,256]{2,1,0:T(8,128)S(1)}, f32[4,64,256]{2,1,0:T(8,128)S(1)}, f32[4,64,256]{2,1,0:T(8,128)S(1)}) custom-call(s32[2,16]{1,0:T(2,128)S(1)} %get-tuple-element.41.table, bf16[256,4096]{1,0:T(8,128)(2,1)S(1)} %get-tuple-element.42.factor, bf16[256,256]{1,0:T(8,128)(2,1)S(1)} %get-tuple-element.43.rest_0_), custom_call_target="tpu_custom_call" | custom-call | flops 536870912 | bytes 2097152 | tf_op jit(solution)/shard_map/pallas_call | solution.py:195
  8.3 0.5 collective-permute-start.10
  8.8 0.0 collective-permute-done.1
  8.8 0.0 collective-permute-done.2
  8.9 4.8 %collective-permute-start.3 = (f32[128,256]{1,0:T(8,128)S(1)}, f32[128,256]{1,0:T(8,128)S(1)}, u32[]{:S(2)}, u32[]{:S(2)}) collective-permute-start(f32[128,256]{1,0:T(8,128)S(1)} %pad_maximum_fusion.3), channel_id=1, source_target_pairs={{0,7},{1,10},{2,13},{3,8},{4,11},{5,14},{6,1},{7,12},{8,15},{9,2},... | collective-permute-start | bytes 393224 | tf_op jit(solution)/shard_map/ppermute | solution.py:230
  13.7 1.1 %collective-permute-start.4 = (f32[128,256]{1,0:T(8,128)S(1)}, f32[128,256]{1,0:T(8,128)S(1)}, u32[]{:S(2)}, u32[]{:S(2)}) collective-permute-start(f32[128,256]{1,0:T(8,128)S(1)} %pad_maximum_fusion.4), channel_id=1, source_target_pairs={{0,15},{1,2},{2,5},{3,0},{4,3},{5,6},{6,9},{7,4},{8,7},{9,10},{10,... | collective-permute-start | bytes 393224 | tf_op jit(solution)/shard_map/ppermute | solution.py:230
  14.8 0.0 collective-permute-done.11
  14.9 2.0 %collective-permute-start.12 = (f32[2,64,256]{2,1,0:T(8,128)S(1)}, f32[2,64,256]{2,1,0:T(8,128)S(1)}, u32[]{:S(2)}, u32[]{:S(2)}) collective-permute-start(f32[2,64,256]{2,1,0:T(8,128)S(1)} %add.84), channel_id=1, source_target_pairs={{0,3},{1,14},{2,1},{3,4},{4,7},{5,2},{6,5},{7,8},{8,11},{9,6},{10,... | collective-permute-start | bytes 393224 | tf_op jit(solution)/shard_map/ppermute | solution.py:230
  16.8 0.0 collective-permute-done.5
  16.8 0.0 collective-permute-start
  16.9 2.8 %collective-permute-done.3 = f32[128,256]{1,0:T(8,128)S(1)} collective-permute-done((f32[128,256]{1,0:T(8,128)S(1)}, f32[128,256]{1,0:T(8,128)S(1)}, u32[]{:S(2)}, u32[]{:S(2)}) %collective-permute-start.3) | collective-permute-done | bytes 131104 | tf_op jit(solution)/shard_map/ppermute | solution.py:230
  19.7 1.1 %collective-permute-start.6 = (f32[2,64,256]{2,1,0:T(8,128)S(1)}, f32[2,64,256]{2,1,0:T(8,128)S(1)}, u32[]{:S(2)}, u32[]{:S(2)}) collective-permute-start(f32[2,64,256]{2,1,0:T(8,128)S(1)} %add.79), channel_id=1, source_target_pairs={{0,3},{1,14},{2,1},{3,4},{4,7},{5,2},{6,5},{7,8},{8,11},{9,6},{10,... | collective-permute-start | bytes 393224 | tf_op jit(solution)/shard_map/ppermute | solution.py:230
  20.8 0.2 collective-permute-done.4
  21.0 0.0 collective-permute-done.10
  21.0 0.3 collective-permute-done.12
  21.4 3.4 %collective-permute-start.13 = (f32[2,64,256]{2,1,0:T(8,128)S(1)}, f32[2,64,256]{2,1,0:T(8,128)S(1)}, u32[]{:S(2)}, u32[]{:S(2)}) collective-permute-start(f32[2,64,256]{2,1,0:T(8,128)S(1)} %slice_add_fusion.4), channel_id=1, source_target_pairs={{0,3},{1,14},{2,1},{3,4},{4,7},{5,2},{6,5},{7,8},{8,11},{9,6},{10,... | collective-permute-start | bytes 393224 | tf_op jit(solution)/shard_map/ppermute | solution.py:230
  24.8 0.0 collective-permute-done
  24.9 0.0 collective-permute-done.6
  24.9 1.6 %collective-permute-start.7 = (f32[2,64,256]{2,1,0:T(8,128)S(1)}, f32[2,64,256]{2,1,0:T(8,128)S(1)}, u32[]{:S(2)}, u32[]{:S(2)}) collective-permute-start(f32[2,64,256]{2,1,0:T(8,128)S(1)} %slice_add_fusion.6), channel_id=1, source_target_pairs={{0,3},{1,14},{2,1},{3,4},{4,7},{5,2},{6,5},{7,8},{8,11},{9,6},{10,... | collective-permute-start | bytes 393224 | tf_op jit(solution)/shard_map/ppermute | solution.py:230
  26.5 0.3 collective-permute-done.13
  26.8 4.7 %collective-permute-start.14 = (f32[2,64,256]{2,1,0:T(8,128)S(1)}, f32[2,64,256]{2,1,0:T(8,128)S(1)}, u32[]{:S(2)}, u32[]{:S(2)}) collective-permute-start(f32[2,64,256]{2,1,0:T(8,128)S(1)} %fusion.4), channel_id=1, source_target_pairs={{0,19},{1,30},{2,17},{3,20},{4,23},{5,18},{6,21},{7,24},{8,27},{9,... | collective-permute-start | bytes 393224 | tf_op jit(solution)/shard_map/ppermute | solution.py:278
  31.5 0.0 collective-permute-done.7
  31.5 1.6 %collective-permute-start.8 = (f32[2,64,256]{2,1,0:T(8,128)S(1)}, f32[2,64,256]{2,1,0:T(8,128)S(1)}, u32[]{:S(2)}, u32[]{:S(2)}) collective-permute-start(f32[2,64,256]{2,1,0:T(8,128)S(1)} %fusion.5), channel_id=1, source_target_pairs={{0,19},{1,30},{2,17},{3,20},{4,23},{5,18},{6,21},{7,24},{8,27},{9,... | collective-permute-start | bytes 393224 | tf_op jit(solution)/shard_map/ppermute | solution.py:278
  33.1 3.0 %collective-permute-done.14.moving = f32[2,64,256]{2,1,0:T(8,128)S(1)} collective-permute-done((f32[2,64,256]{2,1,0:T(8,128)S(1)}, f32[2,64,256]{2,1,0:T(8,128)S(1)}, u32[]{:S(2)}, u32[]{:S(2)}) %collective-permute-start.14) | collective-permute-done | bytes 131104 | tf_op jit(solution)/shard_map/ppermute | solution.py:278
  36.1 1.5 %collective-permute-start.15 = (f32[64,256]{1,0:T(8,128)S(1)}, f32[64,256]{1,0:T(8,128)S(1)}, u32[]{:S(2)}, u32[]{:S(2)}) collective-permute-start(f32[64,256]{1,0:T(8,128)S(1)} %slice_bitcast_fusion.8), channel_id=1, source_target_pairs={{0,1},{1,0},{2,3},{3,2},{4,5},{5,4},{6,7},{7,6},{8,9},{9,8},{10,11... | collective-permute-start | bytes 196616 | tf_op jit(solution)/shard_map/ppermute | solution.py:230
  37.6 2.6 %collective-permute-done.8.moving = f32[2,64,256]{2,1,0:T(8,128)S(1)} collective-permute-done((f32[2,64,256]{2,1,0:T(8,128)S(1)}, f32[2,64,256]{2,1,0:T(8,128)S(1)}, u32[]{:S(2)}, u32[]{:S(2)}) %collective-permute-start.8) | collective-permute-done | bytes 131104 | tf_op jit(solution)/shard_map/ppermute | solution.py:278
  40.2 0.0 collective-permute-start.9
  40.2 0.0 collective-permute-done.15.crossed
  40.2 1.1 %shard_map.80 = (f32[64,256]{1,0:T(8,128)S(1)}, bf16[128,256]{1,0:T(8,128)(2,1)S(1)}, f32[2,64,256]{2,1,0:T(8,128)S(1)}, f32[2,64,256]{2,1,0:T(8,128)S(1)}, f32[...) custom-call(s32[2,16]{1,0:T(2,128)S(1)} %get-tuple-element.41.table, f32[2,128,256]{2,1,0:T(8,128)S(1)} %copy-done, ...), custom_call_target="tpu_custom_call" | custom-call | flops 201326592 | bytes 786432 | tf_op jit(solution)/shard_map/pallas_call | solution.py:185
  41.3 0.6 collective-permute-start.18
  41.9 0.1 collective-permute-start.26
  42.0 0.0 collective-permute-done.9.crossed
  42.0 1.1 %shard_map.79 = (f32[64,256]{1,0:T(8,128)S(1)}, bf16[128,256]{1,0:T(8,128)(2,1)S(1)}, f32[2,64,256]{2,1,0:T(8,128)S(1)}, f32[2,64,256]{2,1,0:T(8,128)S(1)}, f32[...) custom-call(s32[2,16]{1,0:T(2,128)S(1)} %get-tuple-element.41.table, f32[2,128,256]{2,1,0:T(8,128)S(1)} %copy-done, ...), custom_call_target="tpu_custom_call" | custom-call | flops 201326592 | bytes 786432 | tf_op jit(solution)/shard_map/pallas_call | solution.py:185
  43.0 0.5 collective-permute-start.17
  43.5 0.1 collective-permute-start.21
  43.6 1.0 %shard_map.81 = (f32[4,64,256]{2,1,0:T(8,128)S(1)}, f32[4,64,256]{2,1,0:T(8,128)S(1)}, f32[4,64,256]{2,1,0:T(8,128)S(1)}, f32[4,64,256]{2,1,0:T(8,128)S(1)}) custom-call(s32[2,16]{1,0:T(2,128)S(1)} %get-tuple-element.41.table, bf16[256,4096]{1,0:T(8,128)(2,1)S(1)} %get-tuple-element.42.factor, bf16[128,256]{1,0:T(8,128)(2,1)S(1)} %get-tuple-element.62.rest_0_, ...), custom_call_target="tpu_custom_call" | custom-call | flops 536870912 | bytes 2097152 | tf_op jit(solution)/shard_map/pallas_call | solution.py:195
  44.7 0.5 collective-permute-start.16
  45.2 0.0 collective-permute-done.18
  45.3 3.5 %collective-permute-start.19 = (f32[128,256]{1,0:T(8,128)S(1)}, f32[128,256]{1,0:T(8,128)S(1)}, u32[]{:S(2)}, u32[]{:S(2)}) collective-permute-start(f32[128,256]{1,0:T(8,128)S(1)} %pad_maximum_fusion.5), channel_id=1, source_target_pairs={{0,7},{1,10},{2,13},{3,8},{4,11},{5,14},{6,1},{7,12},{8,15},{9,2},... | collective-permute-start | bytes 393224 | tf_op jit(solution)/shard_map/ppermute | solution.py:230
  48.8 0.7 collective-permute-start.20
  49.5 0.0 collective-permute-done.21
  49.5 2.4 %collective-permute-start.22 = (f32[2,64,256]{2,1,0:T(8,128)S(1)}, f32[2,64,256]{2,1,0:T(8,128)S(1)}, u32[]{:S(2)}, u32[]{:S(2)}) collective-permute-start(f32[2,64,256]{2,1,0:T(8,128)S(1)} %add.91), channel_id=1, source_target_pairs={{0,3},{1,14},{2,1},{3,4},{4,7},{5,2},{6,5},{7,8},{8,11},{9,6},{10,... | collective-permute-start | bytes 393224 | tf_op jit(solution)/shard_map/ppermute | solution.py:230
  52.0 0.0 collective-permute-done.19
  52.0 5.4 %collective-permute-start.27 = (f32[2,64,256]{2,1,0:T(8,128)S(1)}, f32[2,64,256]{2,1,0:T(8,128)S(1)}, u32[]{:S(2)}, u32[]{:S(2)}) collective-permute-start(f32[2,64,256]{2,1,0:T(8,128)S(1)} %add.96), channel_id=1, source_target_pairs={{0,3},{1,14},{2,1},{3,4},{4,7},{5,2},{6,5},{7,8},{8,11},{9,6},{10,... | collective-permute-start | bytes 393224 | tf_op jit(solution)/shard_map/ppermute | solution.py:230
  57.4 0.0 collective-permute-done.20
  57.4 0.0 collective-permute-done.16
  57.5 2.6 %collective-permute-start.23 = (f32[2,64,256]{2,1,0:T(8,128)S(1)}, f32[2,64,256]{2,1,0:T(8,128)S(1)}, u32[]{:S(2)}, u32[]{:S(2)}) collective-permute-start(f32[2,64,256]{2,1,0:T(8,128)S(1)} %slice_add_fusion.2), channel_id=1, source_target_pairs={{0,3},{1,14},{2,1},{3,4},{4,7},{5,2},{6,5},{7,8},{8,11},{9,6},{10,... | collective-permute-start | bytes 393224 | tf_op jit(solution)/shard_map/ppermute | solution.py:230
  60.2 0.0 collective-permute-done.27
  60.2 2.9 %collective-permute-start.28 = (f32[2,64,256]{2,1,0:T(8,128)S(1)}, f32[2,64,256]{2,1,0:T(8,128)S(1)}, u32[]{:S(2)}, u32[]{:S(2)}) collective-permute-start(f32[2,64,256]{2,1,0:T(8,128)S(1)} %slice_add_fusion), channel_id=1, source_target_pairs={{0,3},{1,14},{2,1},{3,4},{4,7},{5,2},{6,5},{7,8},{8,11},{9,6},{10,... | collective-permute-start | bytes 393224 | tf_op jit(solution)/shard_map/ppermute | solution.py:230
  63.2 0.3 collective-permute-start.24
  63.5 1.6 %collective-permute-done.28 = f32[2,64,256]{2,1,0:T(8,128)S(1)} collective-permute-done((f32[2,64,256]{2,1,0:T(8,128)S(1)}, f32[2,64,256]{2,1,0:T(8,128)S(1)}, u32[]{:S(2)}, u32[]{:S(2)}) %collective-permute-start.28) | collective-permute-done | bytes 131104 | tf_op jit(solution)/shard_map/ppermute | solution.py:230
  65.1 1.2 %collective-permute-start.29 = (f32[2,64,256]{2,1,0:T(8,128)S(1)}, f32[2,64,256]{2,1,0:T(8,128)S(1)}, u32[]{:S(2)}, u32[]{:S(2)}) collective-permute-start(f32[2,64,256]{2,1,0:T(8,128)S(1)} %fusion.2), channel_id=1, source_target_pairs={{0,19},{1,30},{2,17},{3,20},{4,23},{5,18},{6,21},{7,24},{8,27},{9,... | collective-permute-start | bytes 393224 | tf_op jit(solution)/shard_map/ppermute | solution.py:278
  66.3 6.5 %collective-permute-done.24 = f32[2,64,256]{2,1,0:T(8,128)S(1)} collective-permute-done((f32[2,64,256]{2,1,0:T(8,128)S(1)}, f32[2,64,256]{2,1,0:T(8,128)S(1)}, u32[]{:S(2)}, u32[]{:S(2)}) %collective-permute-start.24) | collective-permute-done | bytes 131104 | tf_op jit(solution)/shard_map/ppermute | solution.py:278
  72.8 1.3 %collective-permute-start.30 = (f32[64,256]{1,0:T(8,128)S(1)}, f32[64,256]{1,0:T(8,128)S(1)}, u32[]{:S(2)}, u32[]{:S(2)}) collective-permute-start(f32[64,256]{1,0:T(8,128)S(1)} %get-tuple-element.82), channel_id=1, source_target_pairs={{0,1},{1,0},{2,3},{3,2},{4,5},{5,4},{6,7},{7,6},{8,9},{9,8},{10,11... | collective-permute-start | bytes 196616 | tf_op jit(solution)/shard_map/ppermute | solution.py:230
  74.0 0.9 %collective-permute-done.29 = f32[2,64,256]{2,1,0:T(8,128)S(1)} collective-permute-done((f32[2,64,256]{2,1,0:T(8,128)S(1)}, f32[2,64,256]{2,1,0:T(8,128)S(1)}, u32[]{:S(2)}, u32[]{:S(2)}) %collective-permute-start.29) | collective-permute-done | bytes 131104 | tf_op jit(solution)/shard_map/ppermute | solution.py:278
  74.9 1.9 %collective-permute-start.31 = (f32[64,256]{1,0:T(8,128)S(1)}, f32[64,256]{1,0:T(8,128)S(1)}, u32[]{:S(2)}, u32[]{:S(2)}) collective-permute-start(f32[64,256]{1,0:T(8,128)S(1)} %get-tuple-element.84), channel_id=1, source_target_pairs={{0,1},{1,0},{2,3},{3,2},{4,5},{5,4},{6,7},{7,6},{8,9},{9,8},{10,11... | collective-permute-start | bytes 196616 | tf_op jit(solution)/shard_map/ppermute | solution.py:230
  76.9 0.7 pad_maximum_fusion
  77.6 0.2 collective-permute-done.31
  77.8 0.7 fusion.6
  (43 shorter events, 0.7 us)
Async XLA Ops:
  3.3 5.4 %collective-permute-start.1 = (f32[2,64,256]{2,1,0:T(8,128)S(1)}, f32[2,64,256]{2,1,0:T(8,128)S(1)}, u32[]{:S(2)}, u32[]{:S(2)}) collective-permute-start(f32[2,64,256]{2,1,0:T(8,128)S(1)} %get-tuple-element.47), channel_id=1, source_target_pairs={{0,1},{1,0},{2,3},{3,2},{4,5},{5,4},{6,7},{7,6},{8,9},{9,8},{10,11... | collective-permute-start | bytes 393224 | tf_op jit(solution)/shard_map/ppermute | solution.py:230
  6.6 2.2 %collective-permute-start.2 = (f32[2,64,256]{2,1,0:T(8,128)S(1)}, f32[2,64,256]{2,1,0:T(8,128)S(1)}, u32[]{:S(2)}, u32[]{:S(2)}) collective-permute-start(f32[2,64,256]{2,1,0:T(8,128)S(1)} %get-tuple-element.49), channel_id=1, source_target_pairs={{0,1},{1,0},{2,3},{3,2},{4,5},{5,4},{6,7},{7,6},{8,9},{9,8},{10,11... | collective-permute-start | bytes 393224 | tf_op jit(solution)/shard_map/ppermute | solution.py:230
  6.7 10.1 %collective-permute-start.5 = (f32[2,64,256]{2,1,0:T(8,128)S(1)}, f32[2,64,256]{2,1,0:T(8,128)S(1)}, u32[]{:S(2)}, u32[]{:S(2)}) collective-permute-start(f32[2,64,256]{2,1,0:T(8,128)S(1)} %get-tuple-element.52), channel_id=1, source_target_pairs={{0,1},{1,0},{2,3},{3,2},{4,5},{5,4},{6,7},{7,6},{8,9},{9,8},{10,11... | collective-permute-start | bytes 393224 | tf_op jit(solution)/shard_map/ppermute | solution.py:230
  7.1 7.7 %collective-permute-start.11 = (f32[2,64,256]{2,1,0:T(8,128)S(1)}, f32[2,64,256]{2,1,0:T(8,128)S(1)}, u32[]{:S(2)}, u32[]{:S(2)}) collective-permute-start(f32[2,64,256]{2,1,0:T(8,128)S(1)} %get-tuple-element.60), channel_id=1, source_target_pairs={{0,1},{1,0},{2,3},{3,2},{4,5},{5,4},{6,7},{7,6},{8,9},{9,8},{10,11... | collective-permute-start | bytes 393224 | tf_op jit(solution)/shard_map/ppermute | solution.py:230
  8.3 12.7 %collective-permute-start.10 = (f32[4,64,256]{2,1,0:T(8,128)S(1)}, f32[4,64,256]{2,1,0:T(8,128)S(1)}, u32[]{:S(2)}, u32[]{:S(2)}) collective-permute-start(f32[4,64,256]{2,1,0:T(8,128)S(1)} %get-tuple-element.57), channel_id=1, source_target_pairs={{0,1},{1,0},{2,3},{3,2},{4,5},{5,4},{6,7},{7,6},{8,9},{9,8},{10,11... | collective-permute-start | bytes 786440 | tf_op jit(solution)/shard_map/ppermute | solution.py:230
  8.9 10.8 %collective-permute-start.3 = (f32[128,256]{1,0:T(8,128)S(1)}, f32[128,256]{1,0:T(8,128)S(1)}, u32[]{:S(2)}, u32[]{:S(2)}) collective-permute-start(f32[128,256]{1,0:T(8,128)S(1)} %pad_maximum_fusion.3), channel_id=1, source_target_pairs={{0,7},{1,10},{2,13},{3,8},{4,11},{5,14},{6,1},{7,12},{8,15},{9,2},... | collective-permute-start | bytes 393224 | tf_op jit(solution)/shard_map/ppermute | solution.py:230
  13.7 7.3 %collective-permute-start.4 = (f32[128,256]{1,0:T(8,128)S(1)}, f32[128,256]{1,0:T(8,128)S(1)}, u32[]{:S(2)}, u32[]{:S(2)}) collective-permute-start(f32[128,256]{1,0:T(8,128)S(1)} %pad_maximum_fusion.4), channel_id=1, source_target_pairs={{0,15},{1,2},{2,5},{3,0},{4,3},{5,6},{6,9},{7,4},{8,7},{9,10},{10,... | collective-permute-start | bytes 393224 | tf_op jit(solution)/shard_map/ppermute | solution.py:230
  14.9 6.5 %collective-permute-start.12 = (f32[2,64,256]{2,1,0:T(8,128)S(1)}, f32[2,64,256]{2,1,0:T(8,128)S(1)}, u32[]{:S(2)}, u32[]{:S(2)}) collective-permute-start(f32[2,64,256]{2,1,0:T(8,128)S(1)} %add.84), channel_id=1, source_target_pairs={{0,3},{1,14},{2,1},{3,4},{4,7},{5,2},{6,5},{7,8},{8,11},{9,6},{10,... | collective-permute-start | bytes 393224 | tf_op jit(solution)/shard_map/ppermute | solution.py:230
  16.8 8.0 %collective-permute-start = (f32[4,64,256]{2,1,0:T(8,128)S(1)}, f32[4,64,256]{2,1,0:T(8,128)S(1)}, u32[]{:S(2)}, u32[]{:S(2)}) collective-permute-start(f32[4,64,256]{2,1,0:T(8,128)S(1)} %get-tuple-element.45), channel_id=1, source_target_pairs={{0,1},{1,0},{2,3},{3,2},{4,5},{5,4},{6,7},{7,6},{8,9},{9,8},{10,11... | collective-permute-start | bytes 786440 | tf_op jit(solution)/shard_map/ppermute | solution.py:230
  19.7 5.2 %collective-permute-start.6 = (f32[2,64,256]{2,1,0:T(8,128)S(1)}, f32[2,64,256]{2,1,0:T(8,128)S(1)}, u32[]{:S(2)}, u32[]{:S(2)}) collective-permute-start(f32[2,64,256]{2,1,0:T(8,128)S(1)} %add.79), channel_id=1, source_target_pairs={{0,3},{1,14},{2,1},{3,4},{4,7},{5,2},{6,5},{7,8},{8,11},{9,6},{10,... | collective-permute-start | bytes 393224 | tf_op jit(solution)/shard_map/ppermute | solution.py:230
  21.0 19.3 %copy-start = (f32[2,128,256]{2,1,0:T(8,128)S(1)}, f32[2,128,256]{2,1,0:T(8,128)}, u32[]{:S(2)}) copy-start(f32[2,128,256]{2,1,0:T(8,128)} %right_sides.5) | copy-start | bytes 786436
  21.4 5.4 %collective-permute-start.13 = (f32[2,64,256]{2,1,0:T(8,128)S(1)}, f32[2,64,256]{2,1,0:T(8,128)S(1)}, u32[]{:S(2)}, u32[]{:S(2)}) collective-permute-start(f32[2,64,256]{2,1,0:T(8,128)S(1)} %slice_add_fusion.4), channel_id=1, source_target_pairs={{0,3},{1,14},{2,1},{3,4},{4,7},{5,2},{6,5},{7,8},{8,11},{9,6},{10,... | collective-permute-start | bytes 393224 | tf_op jit(solution)/shard_map/ppermute | solution.py:230
  24.9 6.6 %collective-permute-start.7 = (f32[2,64,256]{2,1,0:T(8,128)S(1)}, f32[2,64,256]{2,1,0:T(8,128)S(1)}, u32[]{:S(2)}, u32[]{:S(2)}) collective-permute-start(f32[2,64,256]{2,1,0:T(8,128)S(1)} %slice_add_fusion.6), channel_id=1, source_target_pairs={{0,3},{1,14},{2,1},{3,4},{4,7},{5,2},{6,5},{7,8},{8,11},{9,6},{10,... | collective-permute-start | bytes 393224 | tf_op jit(solution)/shard_map/ppermute | solution.py:230
  26.8 9.3 %collective-permute-start.14 = (f32[2,64,256]{2,1,0:T(8,128)S(1)}, f32[2,64,256]{2,1,0:T(8,128)S(1)}, u32[]{:S(2)}, u32[]{:S(2)}) collective-permute-start(f32[2,64,256]{2,1,0:T(8,128)S(1)} %fusion.4), channel_id=1, source_target_pairs={{0,19},{1,30},{2,17},{3,20},{4,23},{5,18},{6,21},{7,24},{8,27},{9,... | collective-permute-start | bytes 393224 | tf_op jit(solution)/shard_map/ppermute | solution.py:278
  31.5 8.7 %collective-permute-start.8 = (f32[2,64,256]{2,1,0:T(8,128)S(1)}, f32[2,64,256]{2,1,0:T(8,128)S(1)}, u32[]{:S(2)}, u32[]{:S(2)}) collective-permute-start(f32[2,64,256]{2,1,0:T(8,128)S(1)} %fusion.5), channel_id=1, source_target_pairs={{0,19},{1,30},{2,17},{3,20},{4,23},{5,18},{6,21},{7,24},{8,27},{9,... | collective-permute-start | bytes 393224 | tf_op jit(solution)/shard_map/ppermute | solution.py:278
  36.1 4.1 %collective-permute-start.15 = (f32[64,256]{1,0:T(8,128)S(1)}, f32[64,256]{1,0:T(8,128)S(1)}, u32[]{:S(2)}, u32[]{:S(2)}) collective-permute-start(f32[64,256]{1,0:T(8,128)S(1)} %slice_bitcast_fusion.8), channel_id=1, source_target_pairs={{0,1},{1,0},{2,3},{3,2},{4,5},{5,4},{6,7},{7,6},{8,9},{9,8},{10,11... | collective-permute-start | bytes 196616 | tf_op jit(solution)/shard_map/ppermute | solution.py:230
  40.2 1.8 %collective-permute-start.9 = (f32[64,256]{1,0:T(8,128)S(1)}, f32[64,256]{1,0:T(8,128)S(1)}, u32[]{:S(2)}, u32[]{:S(2)}) collective-permute-start(f32[64,256]{1,0:T(8,128)S(1)} %slice_bitcast_fusion.9), channel_id=1, source_target_pairs={{0,1},{1,0},{2,3},{3,2},{4,5},{5,4},{6,7},{7,6},{8,9},{9,8},{10,11... | collective-permute-start | bytes 196616 | tf_op jit(solution)/shard_map/ppermute | solution.py:230
  41.3 3.9 %collective-permute-start.18 = (f32[2,64,256]{2,1,0:T(8,128)S(1)}, f32[2,64,256]{2,1,0:T(8,128)S(1)}, u32[]{:S(2)}, u32[]{:S(2)}) collective-permute-start(f32[2,64,256]{2,1,0:T(8,128)S(1)} %get-tuple-element.69), channel_id=1, source_target_pairs={{0,1},{1,0},{2,3},{3,2},{4,5},{5,4},{6,7},{7,6},{8,9},{9,8},{10,11... | collective-permute-start | bytes 393224 | tf_op jit(solution)/shard_map/ppermute | solution.py:230
  41.9 10.1 %collective-permute-start.26 = (f32[2,64,256]{2,1,0:T(8,128)S(1)}, f32[2,64,256]{2,1,0:T(8,128)S(1)}, u32[]{:S(2)}, u32[]{:S(2)}) collective-permute-start(f32[2,64,256]{2,1,0:T(8,128)S(1)} %get-tuple-element.77), channel_id=1, source_target_pairs={{0,1},{1,0},{2,3},{3,2},{4,5},{5,4},{6,7},{7,6},{8,9},{9,8},{10,11... | collective-permute-start | bytes 393224 | tf_op jit(solution)/shard_map/ppermute | solution.py:230
  43.0 2.2 %collective-permute-start.17 = (f32[2,64,256]{2,1,0:T(8,128)S(1)}, f32[2,64,256]{2,1,0:T(8,128)S(1)}, u32[]{:S(2)}, u32[]{:S(2)}) collective-permute-start(f32[2,64,256]{2,1,0:T(8,128)S(1)} %get-tuple-element.67), channel_id=1, source_target_pairs={{0,1},{1,0},{2,3},{3,2},{4,5},{5,4},{6,7},{7,6},{8,9},{9,8},{10,11... | collective-permute-start | bytes 393224 | tf_op jit(solution)/shard_map/ppermute | solution.py:230
  43.5 6.0 %collective-permute-start.21 = (f32[2,64,256]{2,1,0:T(8,128)S(1)}, f32[2,64,256]{2,1,0:T(8,128)S(1)}, u32[]{:S(2)}, u32[]{:S(2)}) collective-permute-start(f32[2,64,256]{2,1,0:T(8,128)S(1)} %get-tuple-element.72), channel_id=1, source_target_pairs={{0,1},{1,0},{2,3},{3,2},{4,5},{5,4},{6,7},{7,6},{8,9},{9,8},{10,11... | collective-permute-start | bytes 393224 | tf_op jit(solution)/shard_map/ppermute | solution.py:230
  44.7 12.8 %collective-permute-start.16 = (f32[4,64,256]{2,1,0:T(8,128)S(1)}, f32[4,64,256]{2,1,0:T(8,128)S(1)}, u32[]{:S(2)}, u32[]{:S(2)}) collective-permute-start(f32[4,64,256]{2,1,0:T(8,128)S(1)} %get-tuple-element.65), channel_id=1, source_target_pairs={{0,1},{1,0},{2,3},{3,2},{4,5},{5,4},{6,7},{7,6},{8,9},{9,8},{10,11... | collective-permute-start | bytes 786440 | tf_op jit(solution)/shard_map/ppermute | solution.py:230
  45.3 6.7 %collective-permute-start.19 = (f32[128,256]{1,0:T(8,128)S(1)}, f32[128,256]{1,0:T(8,128)S(1)}, u32[]{:S(2)}, u32[]{:S(2)}) collective-permute-start(f32[128,256]{1,0:T(8,128)S(1)} %pad_maximum_fusion.5), channel_id=1, source_target_pairs={{0,7},{1,10},{2,13},{3,8},{4,11},{5,14},{6,1},{7,12},{8,15},{9,2},... | collective-permute-start | bytes 393224 | tf_op jit(solution)/shard_map/ppermute | solution.py:230
  48.8 8.6 %collective-permute-start.20 = (f32[128,256]{1,0:T(8,128)S(1)}, f32[128,256]{1,0:T(8,128)S(1)}, u32[]{:S(2)}, u32[]{:S(2)}) collective-permute-start(f32[128,256]{1,0:T(8,128)S(1)} %pad_maximum_fusion.6), channel_id=1, source_target_pairs={{0,15},{1,2},{2,5},{3,0},{4,3},{5,6},{6,9},{7,4},{8,7},{9,10},{10,... | collective-permute-start | bytes 393224 | tf_op jit(solution)/shard_map/ppermute | solution.py:230
  49.5 8.0 %collective-permute-start.22 = (f32[2,64,256]{2,1,0:T(8,128)S(1)}, f32[2,64,256]{2,1,0:T(8,128)S(1)}, u32[]{:S(2)}, u32[]{:S(2)}) collective-permute-start(f32[2,64,256]{2,1,0:T(8,128)S(1)} %add.91), channel_id=1, source_target_pairs={{0,3},{1,14},{2,1},{3,4},{4,7},{5,2},{6,5},{7,8},{8,11},{9,6},{10,... | collective-permute-start | bytes 393224 | tf_op jit(solution)/shard_map/ppermute | solution.py:230
  52.0 8.2 %collective-permute-start.25 = (f32[4,64,256]{2,1,0:T(8,128)S(1)}, f32[4,64,256]{2,1,0:T(8,128)S(1)}, u32[]{:S(2)}, u32[]{:S(2)}) collective-permute-start(f32[4,64,256]{2,1,0:T(8,128)S(1)} %get-tuple-element.74), channel_id=1, source_target_pairs={{0,1},{1,0},{2,3},{3,2},{4,5},{5,4},{6,7},{7,6},{8,9},{9,8},{10,11... | collective-permute-start | bytes 786440 | tf_op jit(solution)/shard_map/ppermute | solution.py:230
  52.0 8.2 %collective-permute-start.27 = (f32[2,64,256]{2,1,0:T(8,128)S(1)}, f32[2,64,256]{2,1,0:T(8,128)S(1)}, u32[]{:S(2)}, u32[]{:S(2)}) collective-permute-start(f32[2,64,256]{2,1,0:T(8,128)S(1)} %add.96), channel_id=1, source_target_pairs={{0,3},{1,14},{2,1},{3,4},{4,7},{5,2},{6,5},{7,8},{8,11},{9,6},{10,... | collective-permute-start | bytes 393224 | tf_op jit(solution)/shard_map/ppermute | solution.py:230
  57.5 5.6 %collective-permute-start.23 = (f32[2,64,256]{2,1,0:T(8,128)S(1)}, f32[2,64,256]{2,1,0:T(8,128)S(1)}, u32[]{:S(2)}, u32[]{:S(2)}) collective-permute-start(f32[2,64,256]{2,1,0:T(8,128)S(1)} %slice_add_fusion.2), channel_id=1, source_target_pairs={{0,3},{1,14},{2,1},{3,4},{4,7},{5,2},{6,5},{7,8},{8,11},{9,6},{10,... | collective-permute-start | bytes 393224 | tf_op jit(solution)/shard_map/ppermute | solution.py:230
  60.2 4.9 %collective-permute-start.28 = (f32[2,64,256]{2,1,0:T(8,128)S(1)}, f32[2,64,256]{2,1,0:T(8,128)S(1)}, u32[]{:S(2)}, u32[]{:S(2)}) collective-permute-start(f32[2,64,256]{2,1,0:T(8,128)S(1)} %slice_add_fusion), channel_id=1, source_target_pairs={{0,3},{1,14},{2,1},{3,4},{4,7},{5,2},{6,5},{7,8},{8,11},{9,6},{10,... | collective-permute-start | bytes 393224 | tf_op jit(solution)/shard_map/ppermute | solution.py:230
  63.2 9.6 %collective-permute-start.24 = (f32[2,64,256]{2,1,0:T(8,128)S(1)}, f32[2,64,256]{2,1,0:T(8,128)S(1)}, u32[]{:S(2)}, u32[]{:S(2)}) collective-permute-start(f32[2,64,256]{2,1,0:T(8,128)S(1)} %fusion.3), channel_id=1, source_target_pairs={{0,19},{1,30},{2,17},{3,20},{4,23},{5,18},{6,21},{7,24},{8,27},{9,... | collective-permute-start | bytes 393224 | tf_op jit(solution)/shard_map/ppermute | solution.py:278
  65.1 9.8 %collective-permute-start.29 = (f32[2,64,256]{2,1,0:T(8,128)S(1)}, f32[2,64,256]{2,1,0:T(8,128)S(1)}, u32[]{:S(2)}, u32[]{:S(2)}) collective-permute-start(f32[2,64,256]{2,1,0:T(8,128)S(1)} %fusion.2), channel_id=1, source_target_pairs={{0,19},{1,30},{2,17},{3,20},{4,23},{5,18},{6,21},{7,24},{8,27},{9,... | collective-permute-start | bytes 393224 | tf_op jit(solution)/shard_map/ppermute | solution.py:278
  72.8 4.8 %collective-permute-start.30 = (f32[64,256]{1,0:T(8,128)S(1)}, f32[64,256]{1,0:T(8,128)S(1)}, u32[]{:S(2)}, u32[]{:S(2)}) collective-permute-start(f32[64,256]{1,0:T(8,128)S(1)} %get-tuple-element.82), channel_id=1, source_target_pairs={{0,1},{1,0},{2,3},{3,2},{4,5},{5,4},{6,7},{7,6},{8,9},{9,8},{10,11... | collective-permute-start | bytes 196616 | tf_op jit(solution)/shard_map/ppermute | solution.py:230
  74.9 2.8 %collective-permute-start.31 = (f32[64,256]{1,0:T(8,128)S(1)}, f32[64,256]{1,0:T(8,128)S(1)}, u32[]{:S(2)}, u32[]{:S(2)}) collective-permute-start(f32[64,256]{1,0:T(8,128)S(1)} %get-tuple-element.84), channel_id=1, source_target_pairs={{0,1},{1,0},{2,3},{3,2},{4,5},{5,4},{6,7},{7,6},{8,9},{9,8},{10,11... | collective-permute-start | bytes 196616 | tf_op jit(solution)/shard_map/ppermute | solution.py:230

commit v4 on v0

--- a/solution.py
+++ b/solution.py
@@ -115,11 +115,17 @@
     put_step(table, lhs[...], factor, chips, 0, [early], [keep], 0)
 
 
-def late_kernel(chips, streams, table, lhs, factor, *outs):
-    give, keep = outs[:streams], outs[streams:]
-    value = lhs[...]
+def late_kernel(chips, streams, table, factor, *rest):
+    parts, outs = rest[: -2 * streams], rest[-2 * streams :]
+    halves = [part.shape[0] // 2 for part in parts]
+    highs = [part[:half] for part, half in zip(parts, halves)]
+    lows = [part[half:] for part, half in zip(parts, halves)]
+    lhs = jnp.concatenate(highs + lows, axis=0)
     for step in range(1, chips // 2):
-        put_step(table, value, factor, chips, step, give, keep, 2 * (step - 1))
+        put_step(
+            table, lhs, factor, chips, step,
+            outs[:streams], outs[streams:], 2 * (step - 1),
+        )
 
 
 VMEM = pl.BlockSpec(memory_space=pltpu.VMEM)
@@ -180,11 +186,14 @@
     )
 
 
-def late_step(chips, streams, fixed, lhs):
-    rows, block = lhs.shape[0] // 2 // streams, lhs.shape[1]
+def late_step(chips, streams, fixed, parts):
+    block = parts[0].shape[1]
+    rows = sum(part.shape[0] for part in parts) // 2 // streams
     outs = [F32((chips - 2, rows, block))] * (2 * streams)
     kernel = functools.partial(late_kernel, chips, streams)
-    out = call(kernel, 12, [SMEM, VMEM, VMEM], outs, 4)(fixed[0], lhs, fixed[1])
+    out = call(kernel, 16, [SMEM] + [VMEM] * (1 + len(parts)), outs, 4)(
+        fixed[0], fixed[1], *parts
+    )
     return out[:streams], out[streams:]
 
 
@@ -228,9 +237,9 @@
                 (ancestor, structure, right_sides, carried, inv_diag, factor_tiles),
             )
             solved_all.append(solved)
-            later_gives, later_keeps = late_step(chips, STREAMS, fixed, lhs)
+            parts = [lhs]
         else:
-            gives, keeps, later_gives, later_keeps = [], [], [], []
+            gives, keeps, parts = [], [], []
             for stream in streams:
                 solved, lhs, give, keep = next_step(
                     chips, tick, stream * rows, fixed, right_sides,
@@ -239,9 +248,8 @@
                 solved_all.append(solved)
                 gives.append(give)
                 keeps.append(keep)
-                give, keep = late_step(chips, 1, fixed, lhs)
-                later_gives += give
-                later_keeps += keep
+                parts.append(lhs)
+        later_gives, later_keeps = late_step(chips, STREAMS, fixed, parts)
         moving, crossed = [], []
         for stream in streams:
             taken = swap(gives[stream])

time: 76.8 us -> 76.3 us (level)
  waiting for transfers between devices: 16.7 us -> 21.4 us
  starting transfers between devices: 49.8 us -> 45.3 us
  Pallas kernels: 7.62 us -> 6.85 us
    ppermute x12, starting transfers between devices: 30.2 us -> 26.6 us  [shards(): pass_on = lambda value: lax.ppermute(value, 'own', chain)]
    ppermute x4, waiting for transfers between devices: 8.77 us -> 12 us  [shards(): leave = lambda value: lax.ppermute(value, ('sec', 'own'), onward)]
    ppermute x12, waiting for transfers between devices: 5.01 us -> 7.12 us  [shards(): pass_on = lambda value: lax.ppermute(value, 'own', chain)]
    ppermute x12, starting transfers between devices: 12.1 us -> 11.2 us  [shards(): swap = lambda value: lax.ppermute(value, 'own', partner)]
    pallas_call x3 -> x2, Pallas kernels: 3.11 us -> 2.34 us  [late_step(): call(kernel, 16, [SMEM] + [VMEM] * (1 + len(parts)), outs, 4)]
  transfers between devices with their start and end apart: 28 -> 28, of which waited for: 13 -> 15; matrix products, arithmetic and copies ran while one was open for 1% -> 1% of each run, Pallas kernels for 5% -> 1%
where the time goes in v4:
time: 76.3 us; the launch traced here: 76.2 us
  starting transfers between devices  45.3 us (59%)
  waiting for transfers between devices  21.4 us (28%)
  Pallas kernels  6.85 us (9%)
  other arithmetic  1.78 us (2%)
  between operations  0.8 us (1%)
    ppermute x12, starting transfers between devices, shards(): pass_on = lambda value: lax.ppermute(value, 'own', chain)  26.6 us
    ppermute x4, waiting for transfers between devices, shards(): leave = lambda value: lax.ppermute(value, ('sec', 'own'), onward)  12 us
    ppermute x12, starting transfers between devices, shards(): swap = lambda value: lax.ppermute(value, 'own', partner)  11.2 us
    ppermute x4, starting transfers between devices, shards(): leave = lambda value: lax.ppermute(value, ('sec', 'own'), onward)  7.47 us
    ppermute x12, waiting for transfers between devices, shards(): pass_on = lambda value: lax.ppermute(value, 'own', chain)  7.12 us
    pallas_call x1, Pallas kernels, first_step(): call(kernel, 6, [HBM] * 6, outs, 4, scratch)  2.58 us
    pallas_call x2, Pallas kernels, late_step(): call(kernel, 16, [SMEM] + [VMEM] * (1 + len(parts)), outs, 4)  2.34 us
    ppermute x12, waiting for transfers between devices, shards(): swap = lambda value: lax.ppermute(value, 'own', partner)  2.26 us
  transfers between devices with their start and end apart: 28, of which 15 were waited for; matrix products, arithmetic and copies ran while one was open for 1% of the time, Pallas kernels for 1%

profile of v4, /device:TPU:1, one launch (start us, length us, event | category | flops | bytes accessed | tf_op | source)
XLA Modules:
  0.0 76.2 jit_solution(3883960117444652208)
XLA Ops:
  0.6 2.6 %shard_map.77 = (s32[2,16]{1,0:T(2,128)S(1)}, bf16[256,4096]{1,0:T(8,128)(2,1)S(1)}, bf16[256,256]{1,0:T(8,128)(2,1)S(1)}, bf16[256,256]{1,0:T(8,128)(2,1)S(1)},...) custom-call(s32[1,16]{1,0:T(1,128)} %ancestor.1, ...), custom_call_target="tpu_custom_call" | custom-call | flops 201326592 | bytes 786432 | tf_op jit(solution)/shard_map/pallas_call | solution.py:171
  3.2 1.2 %shard_map.78 = (f32[6,64,256]{2,1,0:T(8,128)S(1)}, f32[6,64,256]{2,1,0:T(8,128)S(1)}, f32[6,64,256]{2,1,0:T(8,128)S(1)}, f32[6,64,256]{2,1,0:T(8,128)S(1)}) custom-call(s32[2,16]{1,0:T(2,128)S(1)} %get-tuple-element.29.table, bf16[256,4096]{1,0:T(8,128)(2,1)S(1)} %get-tuple-element.30.factor, bf16[256,256]{1,0:T(8,128)(2,1)S(1)} %get-tuple-element.31.rest_0_), custom_call_target="tpu_custom_call" | custom-call | flops 536870912 | bytes 2097152 | tf_op jit(solution)/shard_map/pallas_call | solution.py:194
  4.4 3.3 %collective-permute-start = (f32[6,64,256]{2,1,0:T(8,128)S(1)}, f32[6,64,256]{2,1,0:T(8,128)S(1)}, u32[]{:S(2)}, u32[]{:S(2)}) collective-permute-start(f32[6,64,256]{2,1,0:T(8,128)S(1)} %get-tuple-element.33), channel_id=1, source_target_pairs={{0,1},{1,0},{2,3},{3,2},{4,5},{5,4},{6,7},{7,6},{8,9},{9,8},{10,11... | collective-permute-start | bytes 1179656 | tf_op jit(solution)/shard_map/ppermute | solution.py:223
  7.7 0.1 collective-permute-start.1
  7.8 0.4 collective-permute-start.7
  8.2 0.1 collective-permute-start.8
  8.3 0.9 %collective-permute-done.1 = f32[2,64,256]{2,1,0:T(8,128)S(1)} collective-permute-done((f32[2,64,256]{2,1,0:T(8,128)S(1)}, f32[2,64,256]{2,1,0:T(8,128)S(1)}, u32[]{:S(2)}, u32[]{:S(2)}) %collective-permute-start.1) | collective-permute-done | bytes 131104 | tf_op jit(solution)/shard_map/ppermute | solution.py:223
  9.2 4.2 %collective-permute-start.2 = (f32[2,64,256]{2,1,0:T(8,128)S(1)}, f32[2,64,256]{2,1,0:T(8,128)S(1)}, u32[]{:S(2)}, u32[]{:S(2)}) collective-permute-start(f32[2,64,256]{2,1,0:T(8,128)S(1)} %add.90), channel_id=1, source_target_pairs={{0,3},{1,14},{2,1},{3,4},{4,7},{5,2},{6,5},{7,8},{8,11},{9,6},{10,... | collective-permute-start | bytes 393224 | tf_op jit(solution)/shard_map/ppermute | solution.py:224
  13.4 0.0 collective-permute-done.8
  13.5 0.8 %collective-permute-start.9 = (f32[2,64,256]{2,1,0:T(8,128)S(1)}, f32[2,64,256]{2,1,0:T(8,128)S(1)}, u32[]{:S(2)}, u32[]{:S(2)}) collective-permute-start(f32[2,64,256]{2,1,0:T(8,128)S(1)} %add.97), channel_id=1, source_target_pairs={{0,3},{1,14},{2,1},{3,4},{4,7},{5,2},{6,5},{7,8},{8,11},{9,6},{10,... | collective-permute-start | bytes 393224 | tf_op jit(solution)/shard_map/ppermute | solution.py:224
  14.3 1.1 %collective-permute-done.2 = f32[2,64,256]{2,1,0:T(8,128)S(1)} collective-permute-done((f32[2,64,256]{2,1,0:T(8,128)S(1)}, f32[2,64,256]{2,1,0:T(8,128)S(1)}, u32[]{:S(2)}, u32[]{:S(2)}) %collective-permute-start.2) | collective-permute-done | bytes 131104 | tf_op jit(solution)/shard_map/ppermute | solution.py:224
  15.4 0.0 collective-permute-done
  15.4 3.7 %collective-permute-start.3 = (f32[2,64,256]{2,1,0:T(8,128)S(1)}, f32[2,64,256]{2,1,0:T(8,128)S(1)}, u32[]{:S(2)}, u32[]{:S(2)}) collective-permute-start(f32[2,64,256]{2,1,0:T(8,128)S(1)} %fusion.9), channel_id=1, source_target_pairs={{0,3},{1,14},{2,1},{3,4},{4,7},{5,2},{6,5},{7,8},{8,11},{9,6},{10,... | collective-permute-start | bytes 393224 | tf_op jit(solution)/shard_map/ppermute | solution.py:224
  19.2 0.0 collective-permute-done.9
  19.2 0.0 collective-permute-done.7
  19.2 1.4 %collective-permute-start.10 = (f32[2,64,256]{2,1,0:T(8,128)S(1)}, f32[2,64,256]{2,1,0:T(8,128)S(1)}, u32[]{:S(2)}, u32[]{:S(2)}) collective-permute-start(f32[2,64,256]{2,1,0:T(8,128)S(1)} %fusion.6), channel_id=1, source_target_pairs={{0,3},{1,14},{2,1},{3,4},{4,7},{5,2},{6,5},{7,8},{8,11},{9,6},{10,... | collective-permute-start | bytes 393224 | tf_op jit(solution)/shard_map/ppermute | solution.py:224
  20.6 0.5 collective-permute-done.3
  21.1 3.7 %collective-permute-start.4 = (f32[2,64,256]{2,1,0:T(8,128)S(1)}, f32[2,64,256]{2,1,0:T(8,128)S(1)}, u32[]{:S(2)}, u32[]{:S(2)}) collective-permute-start(f32[2,64,256]{2,1,0:T(8,128)S(1)} %fusion.10), channel_id=1, source_target_pairs={{0,3},{1,14},{2,1},{3,4},{4,7},{5,2},{6,5},{7,8},{8,11},{9,6},{10,... | collective-permute-start | bytes 393224 | tf_op jit(solution)/shard_map/ppermute | solution.py:224
  24.9 0.0 collective-permute-done.10
  24.9 1.4 %collective-permute-start.11 = (f32[2,64,256]{2,1,0:T(8,128)S(1)}, f32[2,64,256]{2,1,0:T(8,128)S(1)}, u32[]{:S(2)}, u32[]{:S(2)}) collective-permute-start(f32[2,64,256]{2,1,0:T(8,128)S(1)} %fusion.7), channel_id=1, source_target_pairs={{0,3},{1,14},{2,1},{3,4},{4,7},{5,2},{6,5},{7,8},{8,11},{9,6},{10,... | collective-permute-start | bytes 393224 | tf_op jit(solution)/shard_map/ppermute | solution.py:224
  26.3 0.5 collective-permute-done.4
  26.9 4.7 %collective-permute-start.5 = (f32[2,64,256]{2,1,0:T(8,128)S(1)}, f32[2,64,256]{2,1,0:T(8,128)S(1)}, u32[]{:S(2)}, u32[]{:S(2)}) collective-permute-start(f32[2,64,256]{2,1,0:T(8,128)S(1)} %fusion.11), channel_id=1, source_target_pairs={{0,16},{1,30},{2,17},{3,19},{4,20},{5,18},{6,21},{7,23},{8,24},{9,... | collective-permute-start | bytes 393224 | tf_op jit(solution)/shard_map/ppermute | solution.py:225
  31.5 0.0 collective-permute-done.11
  31.6 1.4 %collective-permute-start.12 = (f32[2,64,256]{2,1,0:T(8,128)S(1)}, f32[2,64,256]{2,1,0:T(8,128)S(1)}, u32[]{:S(2)}, u32[]{:S(2)}) collective-permute-start(f32[2,64,256]{2,1,0:T(8,128)S(1)} %fusion.8), channel_id=1, source_target_pairs={{0,16},{1,30},{2,17},{3,19},{4,20},{5,18},{6,21},{7,23},{8,24},{9,... | collective-permute-start | bytes 393224 | tf_op jit(solution)/shard_map/ppermute | solution.py:225
  32.9 2.7 %collective-permute-done.5.moving = f32[2,64,256]{2,1,0:T(8,128)S(1)} collective-permute-done((f32[2,64,256]{2,1,0:T(8,128)S(1)}, f32[2,64,256]{2,1,0:T(8,128)S(1)}, u32[]{:S(2)}, u32[]{:S(2)}) %collective-permute-start.5) | collective-permute-done | bytes 131104 | tf_op jit(solution)/shard_map/ppermute | solution.py:225
  35.6 1.8 %collective-permute-start.6 = (f32[64,256]{1,0:T(8,128)S(1)}, f32[64,256]{1,0:T(8,128)S(1)}, u32[]{:S(2)}, u32[]{:S(2)}) collective-permute-start(f32[64,256]{1,0:T(8,128)S(1)} %slice_bitcast_fusion.5), channel_id=1, source_target_pairs={{0,1},{1,0},{2,3},{3,2},{4,5},{5,4},{6,7},{7,6},{8,9},{9,8},{10,11... | collective-permute-start | bytes 196616 | tf_op jit(solution)/shard_map/ppermute | solution.py:223
  37.5 2.8 %collective-permute-done.12.moving = f32[2,64,256]{2,1,0:T(8,128)S(1)} collective-permute-done((f32[2,64,256]{2,1,0:T(8,128)S(1)}, f32[2,64,256]{2,1,0:T(8,128)S(1)}, u32[]{:S(2)}, u32[]{:S(2)}) %collective-permute-start.12) | collective-permute-done | bytes 131104 | tf_op jit(solution)/shard_map/ppermute | solution.py:225
  40.2 0.0 collective-permute-start.13
  40.3 0.0 collective-permute-done.6.crossed
  40.3 0.0 copy-done
  40.3 1.0 %shard_map.79 = (f32[64,256]{1,0:T(8,128)S(1)}, bf16[128,256]{1,0:T(8,128)(2,1)S(1)}, f32[2,64,256]{2,1,0:T(8,128)S(1)}, f32[2,64,256]{2,1,0:T(8,128)S(1)}) custom-call(s32[2,16]{1,0:T(2,128)S(1)} %get-tuple-element.29.table, f32[2,128,256]{2,1,0:T(8,128)S(1)} %copy-done, f32[2,64,256]{2,1,0:T(8,128)S(1)} %collective-permute-done.5.moving, ...), custom_call_target="tpu_custom_call" | custom-call | flops 201326592 | bytes 786432 | tf_op jit(solution)/shard_map/pallas_call | solution.py:184
  41.3 0.2 collective-permute-done.13.crossed
  41.5 1.0 %shard_map.80 = (f32[64,256]{1,0:T(8,128)S(1)}, bf16[128,256]{1,0:T(8,128)(2,1)S(1)}, f32[2,64,256]{2,1,0:T(8,128)S(1)}, f32[2,64,256]{2,1,0:T(8,128)S(1)}) custom-call(s32[2,16]{1,0:T(2,128)S(1)} %get-tuple-element.29.table, f32[2,128,256]{2,1,0:T(8,128)S(1)} %copy-done, f32[2,64,256]{2,1,0:T(8,128)S(1)} %collective-permute-done.12.moving, ...), custom_call_target="tpu_custom_call" | custom-call | flops 201326592 | bytes 786432 | tf_op jit(solution)/shard_map/pallas_call | solution.py:184
  42.5 1.2 %shard_map.81 = (f32[6,64,256]{2,1,0:T(8,128)S(1)}, f32[6,64,256]{2,1,0:T(8,128)S(1)}, f32[6,64,256]{2,1,0:T(8,128)S(1)}, f32[6,64,256]{2,1,0:T(8,128)S(1)}) custom-call(s32[2,16]{1,0:T(2,128)S(1)} %get-tuple-element.29.table, bf16[256,4096]{1,0:T(8,128)(2,1)S(1)} %get-tuple-element.30.factor, bf16[128,256]{1,0:T(8,128)(2,1)S(1)} %get-tuple-element.44.rest_0_, ...), custom_call_target="tpu_custom_call" | custom-call | flops 536870912 | bytes 2097152 | tf_op jit(solution)/shard_map/pallas_call | solution.py:194
  43.7 0.5 collective-permute-start.14
  44.2 0.3 collective-permute-start.15
  44.4 0.3 collective-permute-start.20
  44.7 0.3 collective-permute-start.21
  44.9 0.9 %collective-permute-done.15 = f32[2,64,256]{2,1,0:T(8,128)S(1)} collective-permute-done((f32[2,64,256]{2,1,0:T(8,128)S(1)}, f32[2,64,256]{2,1,0:T(8,128)S(1)}, u32[]{:S(2)}, u32[]{:S(2)}) %collective-permute-start.15) | collective-permute-done | bytes 131104 | tf_op jit(solution)/shard_map/ppermute | solution.py:223
  45.9 1.6 %collective-permute-start.16 = (f32[2,64,256]{2,1,0:T(8,128)S(1)}, f32[2,64,256]{2,1,0:T(8,128)S(1)}, u32[]{:S(2)}, u32[]{:S(2)}) collective-permute-start(f32[2,64,256]{2,1,0:T(8,128)S(1)} %add.104), channel_id=1, source_target_pairs={{0,3},{1,14},{2,1},{3,4},{4,7},{5,2},{6,5},{7,8},{8,11},{9,6},{10,... | collective-permute-start | bytes 393224 | tf_op jit(solution)/shard_map/ppermute | solution.py:224
  47.5 0.0 collective-permute-done.21
  47.5 0.7 collective-permute-start.22
  48.3 2.4 %collective-permute-done.16 = f32[2,64,256]{2,1,0:T(8,128)S(1)} collective-permute-done((f32[2,64,256]{2,1,0:T(8,128)S(1)}, f32[2,64,256]{2,1,0:T(8,128)S(1)}, u32[]{:S(2)}, u32[]{:S(2)}) %collective-permute-start.16) | collective-permute-done | bytes 131104 | tf_op jit(solution)/shard_map/ppermute | solution.py:224
  50.6 0.0 collective-permute-done.14
  50.6 2.6 %collective-permute-start.17 = (f32[2,64,256]{2,1,0:T(8,128)S(1)}, f32[2,64,256]{2,1,0:T(8,128)S(1)}, u32[]{:S(2)}, u32[]{:S(2)}) collective-permute-start(f32[2,64,256]{2,1,0:T(8,128)S(1)} %fusion.3), channel_id=1, source_target_pairs={{0,3},{1,14},{2,1},{3,4},{4,7},{5,2},{6,5},{7,8},{8,11},{9,6},{10,... | collective-permute-start | bytes 393224 | tf_op jit(solution)/shard_map/ppermute | solution.py:224
  53.2 0.0 collective-permute-done.22
  53.2 0.0 collective-permute-done.20
  53.3 1.4 %collective-permute-start.23 = (f32[2,64,256]{2,1,0:T(8,128)S(1)}, f32[2,64,256]{2,1,0:T(8,128)S(1)}, u32[]{:S(2)}, u32[]{:S(2)}) collective-permute-start(f32[2,64,256]{2,1,0:T(8,128)S(1)} %fusion), channel_id=1, source_target_pairs={{0,3},{1,14},{2,1},{3,4},{4,7},{5,2},{6,5},{7,8},{8,11},{9,6},{10,... | collective-permute-start | bytes 393224 | tf_op jit(solution)/shard_map/ppermute | solution.py:224
  54.6 0.5 collective-permute-done.17
  55.2 3.7 %collective-permute-start.18 = (f32[2,64,256]{2,1,0:T(8,128)S(1)}, f32[2,64,256]{2,1,0:T(8,128)S(1)}, u32[]{:S(2)}, u32[]{:S(2)}) collective-permute-start(f32[2,64,256]{2,1,0:T(8,128)S(1)} %fusion.4), channel_id=1, source_target_pairs={{0,3},{1,14},{2,1},{3,4},{4,7},{5,2},{6,5},{7,8},{8,11},{9,6},{10,... | collective-permute-start | bytes 393224 | tf_op jit(solution)/shard_map/ppermute | solution.py:224
  58.9 0.0 collective-permute-done.23
  59.0 1.4 %collective-permute-start.24 = (f32[2,64,256]{2,1,0:T(8,128)S(1)}, f32[2,64,256]{2,1,0:T(8,128)S(1)}, u32[]{:S(2)}, u32[]{:S(2)}) collective-permute-start(f32[2,64,256]{2,1,0:T(8,128)S(1)} %fusion.1), channel_id=1, source_target_pairs={{0,3},{1,14},{2,1},{3,4},{4,7},{5,2},{6,5},{7,8},{8,11},{9,6},{10,... | collective-permute-start | bytes 393224 | tf_op jit(solution)/shard_map/ppermute | solution.py:224
  60.3 0.5 collective-permute-done.18
  60.9 1.3 %collective-permute-start.19 = (f32[2,64,256]{2,1,0:T(8,128)S(1)}, f32[2,64,256]{2,1,0:T(8,128)S(1)}, u32[]{:S(2)}, u32[]{:S(2)}) collective-permute-start(f32[2,64,256]{2,1,0:T(8,128)S(1)} %fusion.5), channel_id=1, source_target_pairs={{0,16},{1,30},{2,17},{3,19},{4,20},{5,18},{6,21},{7,23},{8,24},{9,... | collective-permute-start | bytes 393224 | tf_op jit(solution)/shard_map/ppermute | solution.py:225
  62.2 1.5 %collective-permute-done.24 = f32[2,64,256]{2,1,0:T(8,128)S(1)} collective-permute-done((f32[2,64,256]{2,1,0:T(8,128)S(1)}, f32[2,64,256]{2,1,0:T(8,128)S(1)}, u32[]{:S(2)}, u32[]{:S(2)}) %collective-permute-start.24) | collective-permute-done | bytes 131104 | tf_op jit(solution)/shard_map/ppermute | solution.py:224
  63.8 0.1 collective-permute-start.25
  63.8 5.8 %collective-permute-done.19 = f32[2,64,256]{2,1,0:T(8,128)S(1)} collective-permute-done((f32[2,64,256]{2,1,0:T(8,128)S(1)}, f32[2,64,256]{2,1,0:T(8,128)S(1)}, u32[]{:S(2)}, u32[]{:S(2)}) %collective-permute-start.19) | collective-permute-done | bytes 131104 | tf_op jit(solution)/shard_map/ppermute | solution.py:225
  69.6 2.2 %collective-permute-start.26 = (f32[64,256]{1,0:T(8,128)S(1)}, f32[64,256]{1,0:T(8,128)S(1)}, u32[]{:S(2)}, u32[]{:S(2)}) collective-permute-start(f32[64,256]{1,0:T(8,128)S(1)} %get-tuple-element.54), channel_id=1, source_target_pairs={{0,1},{1,0},{2,3},{3,2},{4,5},{5,4},{6,7},{7,6},{8,9},{9,8},{10,11... | collective-permute-start | bytes 196616 | tf_op jit(solution)/shard_map/ppermute | solution.py:223
  71.8 0.8 collective-permute-done.25
  72.6 2.0 %collective-permute-start.27 = (f32[64,256]{1,0:T(8,128)S(1)}, f32[64,256]{1,0:T(8,128)S(1)}, u32[]{:S(2)}, u32[]{:S(2)}) collective-permute-start(f32[64,256]{1,0:T(8,128)S(1)} %get-tuple-element.56), channel_id=1, source_target_pairs={{0,1},{1,0},{2,3},{3,2},{4,5},{5,4},{6,7},{7,6},{8,9},{9,8},{10,11... | collective-permute-start | bytes 196616 | tf_op jit(solution)/shard_map/ppermute | solution.py:223
  74.6 0.7 pad_maximum_fusion
  75.3 0.0 collective-permute-done.26
  75.3 0.2 collective-permute-done.27
  75.5 0.7 fusion.12
  (21 shorter events, 0.4 us)
Async XLA Ops:
  4.4 11.0 %collective-permute-start = (f32[6,64,256]{2,1,0:T(8,128)S(1)}, f32[6,64,256]{2,1,0:T(8,128)S(1)}, u32[]{:S(2)}, u32[]{:S(2)}) collective-permute-start(f32[6,64,256]{2,1,0:T(8,128)S(1)} %get-tuple-element.33), channel_id=1, source_target_pairs={{0,1},{1,0},{2,3},{3,2},{4,5},{5,4},{6,7},{7,6},{8,9},{9,8},{10,11... | collective-permute-start | bytes 1179656 | tf_op jit(solution)/shard_map/ppermute | solution.py:223
  7.7 1.5 %collective-permute-start.1 = (f32[2,64,256]{2,1,0:T(8,128)S(1)}, f32[2,64,256]{2,1,0:T(8,128)S(1)}, u32[]{:S(2)}, u32[]{:S(2)}) collective-permute-start(f32[2,64,256]{2,1,0:T(8,128)S(1)} %get-tuple-element.35), channel_id=1, source_target_pairs={{0,1},{1,0},{2,3},{3,2},{4,5},{5,4},{6,7},{7,6},{8,9},{9,8},{10,11... | collective-permute-start | bytes 393224 | tf_op jit(solution)/shard_map/ppermute | solution.py:223
  7.8 11.4 %collective-permute-start.7 = (f32[6,64,256]{2,1,0:T(8,128)S(1)}, f32[6,64,256]{2,1,0:T(8,128)S(1)}, u32[]{:S(2)}, u32[]{:S(2)}) collective-permute-start(f32[6,64,256]{2,1,0:T(8,128)S(1)} %get-tuple-element.40), channel_id=1, source_target_pairs={{0,1},{1,0},{2,3},{3,2},{4,5},{5,4},{6,7},{7,6},{8,9},{9,8},{10,11... | collective-permute-start | bytes 1179656 | tf_op jit(solution)/shard_map/ppermute | solution.py:223
  8.2 5.3 %collective-permute-start.8 = (f32[2,64,256]{2,1,0:T(8,128)S(1)}, f32[2,64,256]{2,1,0:T(8,128)S(1)}, u32[]{:S(2)}, u32[]{:S(2)}) collective-permute-start(f32[2,64,256]{2,1,0:T(8,128)S(1)} %get-tuple-element.42), channel_id=1, source_target_pairs={{0,1},{1,0},{2,3},{3,2},{4,5},{5,4},{6,7},{7,6},{8,9},{9,8},{10,11... | collective-permute-start | bytes 393224 | tf_op jit(solution)/shard_map/ppermute | solution.py:223
  9.2 31.1 %copy-start = (f32[2,128,256]{2,1,0:T(8,128)S(1)}, f32[2,128,256]{2,1,0:T(8,128)}, u32[]{:S(2)}) copy-start(f32[2,128,256]{2,1,0:T(8,128)} %right_sides.5) | copy-start | bytes 786436
  9.2 6.2 %collective-permute-start.2 = (f32[2,64,256]{2,1,0:T(8,128)S(1)}, f32[2,64,256]{2,1,0:T(8,128)S(1)}, u32[]{:S(2)}, u32[]{:S(2)}) collective-permute-start(f32[2,64,256]{2,1,0:T(8,128)S(1)} %add.90), channel_id=1, source_target_pairs={{0,3},{1,14},{2,1},{3,4},{4,7},{5,2},{6,5},{7,8},{8,11},{9,6},{10,... | collective-permute-start | bytes 393224 | tf_op jit(solution)/shard_map/ppermute | solution.py:224
  13.5 5.7 %collective-permute-start.9 = (f32[2,64,256]{2,1,0:T(8,128)S(1)}, f32[2,64,256]{2,1,0:T(8,128)S(1)}, u32[]{:S(2)}, u32[]{:S(2)}) collective-permute-start(f32[2,64,256]{2,1,0:T(8,128)S(1)} %add.97), channel_id=1, source_target_pairs={{0,3},{1,14},{2,1},{3,4},{4,7},{5,2},{6,5},{7,8},{8,11},{9,6},{10,... | collective-permute-start | bytes 393224 | tf_op jit(solution)/shard_map/ppermute | solution.py:224
  15.4 5.7 %collective-permute-start.3 = (f32[2,64,256]{2,1,0:T(8,128)S(1)}, f32[2,64,256]{2,1,0:T(8,128)S(1)}, u32[]{:S(2)}, u32[]{:S(2)}) collective-permute-start(f32[2,64,256]{2,1,0:T(8,128)S(1)} %fusion.9), channel_id=1, source_target_pairs={{0,3},{1,14},{2,1},{3,4},{4,7},{5,2},{6,5},{7,8},{8,11},{9,6},{10,... | collective-permute-start | bytes 393224 | tf_op jit(solution)/shard_map/ppermute | solution.py:224
  19.2 5.7 %collective-permute-start.10 = (f32[2,64,256]{2,1,0:T(8,128)S(1)}, f32[2,64,256]{2,1,0:T(8,128)S(1)}, u32[]{:S(2)}, u32[]{:S(2)}) collective-permute-start(f32[2,64,256]{2,1,0:T(8,128)S(1)} %fusion.6), channel_id=1, source_target_pairs={{0,3},{1,14},{2,1},{3,4},{4,7},{5,2},{6,5},{7,8},{8,11},{9,6},{10,... | collective-permute-start | bytes 393224 | tf_op jit(solution)/shard_map/ppermute | solution.py:224
  21.1 5.7 %collective-permute-start.4 = (f32[2,64,256]{2,1,0:T(8,128)S(1)}, f32[2,64,256]{2,1,0:T(8,128)S(1)}, u32[]{:S(2)}, u32[]{:S(2)}) collective-permute-start(f32[2,64,256]{2,1,0:T(8,128)S(1)} %fusion.10), channel_id=1, source_target_pairs={{0,3},{1,14},{2,1},{3,4},{4,7},{5,2},{6,5},{7,8},{8,11},{9,6},{10,... | collective-permute-start | bytes 393224 | tf_op jit(solution)/shard_map/ppermute | solution.py:224
  24.9 6.6 %collective-permute-start.11 = (f32[2,64,256]{2,1,0:T(8,128)S(1)}, f32[2,64,256]{2,1,0:T(8,128)S(1)}, u32[]{:S(2)}, u32[]{:S(2)}) collective-permute-start(f32[2,64,256]{2,1,0:T(8,128)S(1)} %fusion.7), channel_id=1, source_target_pairs={{0,3},{1,14},{2,1},{3,4},{4,7},{5,2},{6,5},{7,8},{8,11},{9,6},{10,... | collective-permute-start | bytes 393224 | tf_op jit(solution)/shard_map/ppermute | solution.py:224
  26.9 8.8 %collective-permute-start.5 = (f32[2,64,256]{2,1,0:T(8,128)S(1)}, f32[2,64,256]{2,1,0:T(8,128)S(1)}, u32[]{:S(2)}, u32[]{:S(2)}) collective-permute-start(f32[2,64,256]{2,1,0:T(8,128)S(1)} %fusion.11), channel_id=1, source_target_pairs={{0,16},{1,30},{2,17},{3,19},{4,20},{5,18},{6,21},{7,23},{8,24},{9,... | collective-permute-start | bytes 393224 | tf_op jit(solution)/shard_map/ppermute | solution.py:225
  31.6 8.7 %collective-permute-start.12 = (f32[2,64,256]{2,1,0:T(8,128)S(1)}, f32[2,64,256]{2,1,0:T(8,128)S(1)}, u32[]{:S(2)}, u32[]{:S(2)}) collective-permute-start(f32[2,64,256]{2,1,0:T(8,128)S(1)} %fusion.8), channel_id=1, source_target_pairs={{0,16},{1,30},{2,17},{3,19},{4,20},{5,18},{6,21},{7,23},{8,24},{9,... | collective-permute-start | bytes 393224 | tf_op jit(solution)/shard_map/ppermute | solution.py:225
  35.6 4.6 %collective-permute-start.6 = (f32[64,256]{1,0:T(8,128)S(1)}, f32[64,256]{1,0:T(8,128)S(1)}, u32[]{:S(2)}, u32[]{:S(2)}) collective-permute-start(f32[64,256]{1,0:T(8,128)S(1)} %slice_bitcast_fusion.5), channel_id=1, source_target_pairs={{0,1},{1,0},{2,3},{3,2},{4,5},{5,4},{6,7},{7,6},{8,9},{9,8},{10,11... | collective-permute-start | bytes 196616 | tf_op jit(solution)/shard_map/ppermute | solution.py:223
  40.2 1.3 %collective-permute-start.13 = (f32[64,256]{1,0:T(8,128)S(1)}, f32[64,256]{1,0:T(8,128)S(1)}, u32[]{:S(2)}, u32[]{:S(2)}) collective-permute-start(f32[64,256]{1,0:T(8,128)S(1)} %slice_bitcast_fusion.4), channel_id=1, source_target_pairs={{0,1},{1,0},{2,3},{3,2},{4,5},{5,4},{6,7},{7,6},{8,9},{9,8},{10,11... | collective-permute-start | bytes 196616 | tf_op jit(solution)/shard_map/ppermute | solution.py:223
  43.7 7.0 %collective-permute-start.14 = (f32[6,64,256]{2,1,0:T(8,128)S(1)}, f32[6,64,256]{2,1,0:T(8,128)S(1)}, u32[]{:S(2)}, u32[]{:S(2)}) collective-permute-start(f32[6,64,256]{2,1,0:T(8,128)S(1)} %get-tuple-element.47), channel_id=1, source_target_pairs={{0,1},{1,0},{2,3},{3,2},{4,5},{5,4},{6,7},{7,6},{8,9},{9,8},{10,11... | collective-permute-start | bytes 1179656 | tf_op jit(solution)/shard_map/ppermute | solution.py:223
  44.2 1.7 %collective-permute-start.15 = (f32[2,64,256]{2,1,0:T(8,128)S(1)}, f32[2,64,256]{2,1,0:T(8,128)S(1)}, u32[]{:S(2)}, u32[]{:S(2)}) collective-permute-start(f32[2,64,256]{2,1,0:T(8,128)S(1)} %get-tuple-element.49), channel_id=1, source_target_pairs={{0,1},{1,0},{2,3},{3,2},{4,5},{5,4},{6,7},{7,6},{8,9},{9,8},{10,11... | collective-permute-start | bytes 393224 | tf_op jit(solution)/shard_map/ppermute | solution.py:223
  44.4 8.8 %collective-permute-start.20 = (f32[6,64,256]{2,1,0:T(8,128)S(1)}, f32[6,64,256]{2,1,0:T(8,128)S(1)}, u32[]{:S(2)}, u32[]{:S(2)}) collective-permute-start(f32[6,64,256]{2,1,0:T(8,128)S(1)} %get-tuple-element.51), channel_id=1, source_target_pairs={{0,1},{1,0},{2,3},{3,2},{4,5},{5,4},{6,7},{7,6},{8,9},{9,8},{10,11... | collective-permute-start | bytes 1179656 | tf_op jit(solution)/shard_map/ppermute | solution.py:223
  44.7 2.8 %collective-permute-start.21 = (f32[2,64,256]{2,1,0:T(8,128)S(1)}, f32[2,64,256]{2,1,0:T(8,128)S(1)}, u32[]{:S(2)}, u32[]{:S(2)}) collective-permute-start(f32[2,64,256]{2,1,0:T(8,128)S(1)} %get-tuple-element.53), channel_id=1, source_target_pairs={{0,1},{1,0},{2,3},{3,2},{4,5},{5,4},{6,7},{7,6},{8,9},{9,8},{10,11... | collective-permute-start | bytes 393224 | tf_op jit(solution)/shard_map/ppermute | solution.py:223
  45.9 4.8 %collective-permute-start.16 = (f32[2,64,256]{2,1,0:T(8,128)S(1)}, f32[2,64,256]{2,1,0:T(8,128)S(1)}, u32[]{:S(2)}, u32[]{:S(2)}) collective-permute-start(f32[2,64,256]{2,1,0:T(8,128)S(1)} %add.104), channel_id=1, source_target_pairs={{0,3},{1,14},{2,1},{3,4},{4,7},{5,2},{6,5},{7,8},{8,11},{9,6},{10,... | collective-permute-start | bytes 393224 | tf_op jit(solution)/shard_map/ppermute | solution.py:224
  47.5 5.7 %collective-permute-start.22 = (f32[2,64,256]{2,1,0:T(8,128)S(1)}, f32[2,64,256]{2,1,0:T(8,128)S(1)}, u32[]{:S(2)}, u32[]{:S(2)}) collective-permute-start(f32[2,64,256]{2,1,0:T(8,128)S(1)} %add.111), channel_id=1, source_target_pairs={{0,3},{1,14},{2,1},{3,4},{4,7},{5,2},{6,5},{7,8},{8,11},{9,6},{10,... | collective-permute-start | bytes 393224 | tf_op jit(solution)/shard_map/ppermute | solution.py:224
  50.6 4.5 %collective-permute-start.17 = (f32[2,64,256]{2,1,0:T(8,128)S(1)}, f32[2,64,256]{2,1,0:T(8,128)S(1)}, u32[]{:S(2)}, u32[]{:S(2)}) collective-permute-start(f32[2,64,256]{2,1,0:T(8,128)S(1)} %fusion.3), channel_id=1, source_target_pairs={{0,3},{1,14},{2,1},{3,4},{4,7},{5,2},{6,5},{7,8},{8,11},{9,6},{10,... | collective-permute-start | bytes 393224 | tf_op jit(solution)/shard_map/ppermute | solution.py:224
  53.3 5.7 %collective-permute-start.23 = (f32[2,64,256]{2,1,0:T(8,128)S(1)}, f32[2,64,256]{2,1,0:T(8,128)S(1)}, u32[]{:S(2)}, u32[]{:S(2)}) collective-permute-start(f32[2,64,256]{2,1,0:T(8,128)S(1)} %fusion), channel_id=1, source_target_pairs={{0,3},{1,14},{2,1},{3,4},{4,7},{5,2},{6,5},{7,8},{8,11},{9,6},{10,... | collective-permute-start | bytes 393224 | tf_op jit(solution)/shard_map/ppermute | solution.py:224
  55.2 5.7 %collective-permute-start.18 = (f32[2,64,256]{2,1,0:T(8,128)S(1)}, f32[2,64,256]{2,1,0:T(8,128)S(1)}, u32[]{:S(2)}, u32[]{:S(2)}) collective-permute-start(f32[2,64,256]{2,1,0:T(8,128)S(1)} %fusion.4), channel_id=1, source_target_pairs={{0,3},{1,14},{2,1},{3,4},{4,7},{5,2},{6,5},{7,8},{8,11},{9,6},{10,... | collective-permute-start | bytes 393224 | tf_op jit(solution)/shard_map/ppermute | solution.py:224
  59.0 4.8 %collective-permute-start.24 = (f32[2,64,256]{2,1,0:T(8,128)S(1)}, f32[2,64,256]{2,1,0:T(8,128)S(1)}, u32[]{:S(2)}, u32[]{:S(2)}) collective-permute-start(f32[2,64,256]{2,1,0:T(8,128)S(1)} %fusion.1), channel_id=1, source_target_pairs={{0,3},{1,14},{2,1},{3,4},{4,7},{5,2},{6,5},{7,8},{8,11},{9,6},{10,... | collective-permute-start | bytes 393224 | tf_op jit(solution)/shard_map/ppermute | solution.py:224
  60.9 8.7 %collective-permute-start.19 = (f32[2,64,256]{2,1,0:T(8,128)S(1)}, f32[2,64,256]{2,1,0:T(8,128)S(1)}, u32[]{:S(2)}, u32[]{:S(2)}) collective-permute-start(f32[2,64,256]{2,1,0:T(8,128)S(1)} %fusion.5), channel_id=1, source_target_pairs={{0,16},{1,30},{2,17},{3,19},{4,20},{5,18},{6,21},{7,23},{8,24},{9,... | collective-permute-start | bytes 393224 | tf_op jit(solution)/shard_map/ppermute | solution.py:225
  63.8 8.8 %collective-permute-start.25 = (f32[2,64,256]{2,1,0:T(8,128)S(1)}, f32[2,64,256]{2,1,0:T(8,128)S(1)}, u32[]{:S(2)}, u32[]{:S(2)}) collective-permute-start(f32[2,64,256]{2,1,0:T(8,128)S(1)} %fusion.2), channel_id=1, source_target_pairs={{0,16},{1,30},{2,17},{3,19},{4,20},{5,18},{6,21},{7,23},{8,24},{9,... | collective-permute-start | bytes 393224 | tf_op jit(solution)/shard_map/ppermute | solution.py:225
  69.6 5.7 %collective-permute-start.26 = (f32[64,256]{1,0:T(8,128)S(1)}, f32[64,256]{1,0:T(8,128)S(1)}, u32[]{:S(2)}, u32[]{:S(2)}) collective-permute-start(f32[64,256]{1,0:T(8,128)S(1)} %get-tuple-element.54), channel_id=1, source_target_pairs={{0,1},{1,0},{2,3},{3,2},{4,5},{5,4},{6,7},{7,6},{8,9},{9,8},{10,11... | collective-permute-start | bytes 196616 | tf_op jit(solution)/shard_map/ppermute | solution.py:223
  72.6 2.9 %collective-permute-start.27 = (f32[64,256]{1,0:T(8,128)S(1)}, f32[64,256]{1,0:T(8,128)S(1)}, u32[]{:S(2)}, u32[]{:S(2)}) collective-permute-start(f32[64,256]{1,0:T(8,128)S(1)} %get-tuple-element.56), channel_id=1, source_target_pairs={{0,1},{1,0},{2,3},{3,2},{4,5},{5,4},{6,7},{7,6},{8,9},{9,8},{10,11... | collective-permute-start | bytes 196616 | tf_op jit(solution)/shard_map/ppermute | solution.py:223

commit v5 on v0

--- a/solution.py
+++ b/solution.py
@@ -200,11 +200,12 @@
         return ((chip + ahead) % chips) * 2 + 1 - core
 
     def to_next_section(place):
+        last = sections - 1
         return [
-            (s * owners + i, (s + 1) % sections * owners + place(i))
-            for s in range(sections)
+            (s * owners + i, (s + 1) * owners + place(i))
+            for s in range(last)
             for i in range(owners)
-        ]
+        ] + [(last * owners + i, i ^ 1) for i in range(owners)]
 
     chain = [(i, next_on_chain(i)) for i in range(owners)]
     upward = lambda i: (i // 2 + i) % 2 == 0

time: 76.8 us -> 75.6 us (0.984)
  starting transfers between devices: 49.8 us -> 45.7 us
  waiting for transfers between devices: 16.7 us -> 19.5 us
    ppermute x12, starting transfers between devices: 12.1 us -> 7.29 us  [shards(): swap = lambda value: lax.ppermute(value, 'own', partner)]
    ppermute x4, waiting for transfers between devices: 8.77 us -> 11.7 us  [shards(): leave = lambda value: lax.ppermute(value, ('sec', 'own'), onward)]
    ppermute x4, starting transfers between devices: 7.57 us -> 8.57 us  [shards(): leave = lambda value: lax.ppermute(value, ('sec', 'own'), onward)]
  transfers between devices with their start and end apart: 28 -> 28, of which waited for: 13 -> 14; matrix products, arithmetic and copies ran while one was open for 1% -> 2% of each run, Pallas kernels for 5% -> 5%
where the time goes in v5:
time: 75.6 us; the launch traced here: 75.5 us
  starting transfers between devices  45.7 us (60%)
  waiting for transfers between devices  19.5 us (26%)
  Pallas kernels  7.63 us (10%)
  other arithmetic  1.78 us (2%)
  between operations  0.79 us (1%)
    ppermute x12, starting transfers between devices, shards(): pass_on = lambda value: lax.ppermute(value, 'own', chain)  29.9 us
    ppermute x4, waiting for transfers between devices, shards(): leave = lambda value: lax.ppermute(value, ('sec', 'own'), onward)  11.7 us
    ppermute x4, starting transfers between devices, shards(): leave = lambda value: lax.ppermute(value, ('sec', 'own'), onward)  8.57 us
    ppermute x12, starting transfers between devices, shards(): swap = lambda value: lax.ppermute(value, 'own', partner)  7.29 us
    ppermute x12, waiting for transfers between devices, shards(): pass_on = lambda value: lax.ppermute(value, 'own', chain)  4.51 us
    ppermute x12, waiting for transfers between devices, shards(): swap = lambda value: lax.ppermute(value, 'own', partner)  3.3 us
    pallas_call x3, Pallas kernels, late_step(): out = call(kernel, 12, [SMEM, VMEM, VMEM], outs, 4)(fixed[0], lhs, fixed[1])  3.12 us
    pallas_call x1, Pallas kernels, first_step(): call(kernel, 6, [HBM] * 6, outs, 4, scratch)  2.58 us
  transfers between devices with their start and end apart: 28, of which 14 were waited for; matrix products, arithmetic and copies ran while one was open for 2% of the time, Pallas kernels for 5%

profile of v5, /device:TPU:1, one launch (start us, length us, event | category | flops | bytes accessed | tf_op | source)
XLA Modules:
  0.0 75.5 jit_solution(10976865719257455967)
XLA Ops:
  0.6 2.6 %shard_map.77 = (s32[2,16]{1,0:T(2,128)S(1)}, bf16[256,4096]{1,0:T(8,128)(2,1)S(1)}, bf16[256,256]{1,0:T(8,128)(2,1)S(1)}, bf16[256,256]{1,0:T(8,128)(2,1)S(1)},...) custom-call(s32[1,16]{1,0:T(1,128)} %ancestor.1, ...), custom_call_target="tpu_custom_call" | custom-call | flops 201326592 | bytes 786432 | tf_op jit(solution)/shard_map/pallas_call | solution.py:165
  3.2 1.2 %shard_map.78 = (f32[6,64,256]{2,1,0:T(8,128)S(1)}, f32[6,64,256]{2,1,0:T(8,128)S(1)}, f32[6,64,256]{2,1,0:T(8,128)S(1)}, f32[6,64,256]{2,1,0:T(8,128)S(1)}) custom-call(s32[2,16]{1,0:T(2,128)S(1)} %get-tuple-element.29.table, bf16[256,256]{1,0:T(8,128)(2,1)S(1)} %get-tuple-element.30.lhs, bf16[256,4096]{1,0:T(8,128)(2,1)S(1)} %get-tuple-element.31.factor), custom_call_target="tpu_custom_call" | custom-call | flops 402653184 | bytes 1572864 | tf_op jit(solution)/shard_map/pallas_call | solution.py:187
  4.4 0.0 copy-start
  4.4 3.3 %collective-permute-start.7 = (f32[6,64,256]{2,1,0:T(8,128)S(1)}, f32[6,64,256]{2,1,0:T(8,128)S(1)}, u32[]{:S(2)}, u32[]{:S(2)}) collective-permute-start(f32[6,64,256]{2,1,0:T(8,128)S(1)} %get-tuple-element.40), channel_id=1, source_target_pairs={{0,1},{1,0},{2,3},{3,2},{4,5},{5,4},{6,7},{7,6},{8,9},{9,8},{10,11... | collective-permute-start | bytes 1179656 | tf_op jit(solution)/shard_map/ppermute | solution.py:215
  7.7 0.1 collective-permute-start.8
  7.8 0.4 collective-permute-start
  8.2 0.1 collective-permute-start.1
  8.3 0.9 %collective-permute-done.8 = f32[2,64,256]{2,1,0:T(8,128)S(1)} collective-permute-done((f32[2,64,256]{2,1,0:T(8,128)S(1)}, f32[2,64,256]{2,1,0:T(8,128)S(1)}, u32[]{:S(2)}, u32[]{:S(2)}) %collective-permute-start.8) | collective-permute-done | bytes 131104 | tf_op jit(solution)/shard_map/ppermute | solution.py:215
  9.3 4.2 %collective-permute-start.9 = (f32[2,64,256]{2,1,0:T(8,128)S(1)}, f32[2,64,256]{2,1,0:T(8,128)S(1)}, u32[]{:S(2)}, u32[]{:S(2)}) collective-permute-start(f32[2,64,256]{2,1,0:T(8,128)S(1)} %add.97), channel_id=1, source_target_pairs={{0,3},{1,14},{2,1},{3,4},{4,7},{5,2},{6,5},{7,8},{8,11},{9,6},{10,... | collective-permute-start | bytes 393224 | tf_op jit(solution)/shard_map/ppermute | solution.py:216
  13.5 0.0 collective-permute-done.1
  13.5 0.8 %collective-permute-start.2 = (f32[2,64,256]{2,1,0:T(8,128)S(1)}, f32[2,64,256]{2,1,0:T(8,128)S(1)}, u32[]{:S(2)}, u32[]{:S(2)}) collective-permute-start(f32[2,64,256]{2,1,0:T(8,128)S(1)} %add.90), channel_id=1, source_target_pairs={{0,3},{1,14},{2,1},{3,4},{4,7},{5,2},{6,5},{7,8},{8,11},{9,6},{10,... | collective-permute-start | bytes 393224 | tf_op jit(solution)/shard_map/ppermute | solution.py:216
  14.3 1.1 %collective-permute-done.9 = f32[2,64,256]{2,1,0:T(8,128)S(1)} collective-permute-done((f32[2,64,256]{2,1,0:T(8,128)S(1)}, f32[2,64,256]{2,1,0:T(8,128)S(1)}, u32[]{:S(2)}, u32[]{:S(2)}) %collective-permute-start.9) | collective-permute-done | bytes 131104 | tf_op jit(solution)/shard_map/ppermute | solution.py:216
  15.4 0.0 collective-permute-done.7
  15.4 3.7 %collective-permute-start.10 = (f32[2,64,256]{2,1,0:T(8,128)S(1)}, f32[2,64,256]{2,1,0:T(8,128)S(1)}, u32[]{:S(2)}, u32[]{:S(2)}) collective-permute-start(f32[2,64,256]{2,1,0:T(8,128)S(1)} %fusion.6), channel_id=1, source_target_pairs={{0,3},{1,14},{2,1},{3,4},{4,7},{5,2},{6,5},{7,8},{8,11},{9,6},{10,... | collective-permute-start | bytes 393224 | tf_op jit(solution)/shard_map/ppermute | solution.py:216
  19.2 0.0 collective-permute-done.2
  19.2 0.0 collective-permute-done
  19.2 1.4 %collective-permute-start.3 = (f32[2,64,256]{2,1,0:T(8,128)S(1)}, f32[2,64,256]{2,1,0:T(8,128)S(1)}, u32[]{:S(2)}, u32[]{:S(2)}) collective-permute-start(f32[2,64,256]{2,1,0:T(8,128)S(1)} %fusion.9), channel_id=1, source_target_pairs={{0,3},{1,14},{2,1},{3,4},{4,7},{5,2},{6,5},{7,8},{8,11},{9,6},{10,... | collective-permute-start | bytes 393224 | tf_op jit(solution)/shard_map/ppermute | solution.py:216
  20.6 0.5 collective-permute-done.10
  21.2 3.7 %collective-permute-start.11 = (f32[2,64,256]{2,1,0:T(8,128)S(1)}, f32[2,64,256]{2,1,0:T(8,128)S(1)}, u32[]{:S(2)}, u32[]{:S(2)}) collective-permute-start(f32[2,64,256]{2,1,0:T(8,128)S(1)} %fusion.7), channel_id=1, source_target_pairs={{0,3},{1,14},{2,1},{3,4},{4,7},{5,2},{6,5},{7,8},{8,11},{9,6},{10,... | collective-permute-start | bytes 393224 | tf_op jit(solution)/shard_map/ppermute | solution.py:216
  24.9 0.0 collective-permute-done.3
  24.9 1.4 %collective-permute-start.4 = (f32[2,64,256]{2,1,0:T(8,128)S(1)}, f32[2,64,256]{2,1,0:T(8,128)S(1)}, u32[]{:S(2)}, u32[]{:S(2)}) collective-permute-start(f32[2,64,256]{2,1,0:T(8,128)S(1)} %fusion.10), channel_id=1, source_target_pairs={{0,3},{1,14},{2,1},{3,4},{4,7},{5,2},{6,5},{7,8},{8,11},{9,6},{10,... | collective-permute-start | bytes 393224 | tf_op jit(solution)/shard_map/ppermute | solution.py:216
  26.3 0.5 collective-permute-done.11
  26.9 4.7 %collective-permute-start.12 = (f32[2,64,256]{2,1,0:T(8,128)S(1)}, f32[2,64,256]{2,1,0:T(8,128)S(1)}, u32[]{:S(2)}, u32[]{:S(2)}) collective-permute-start(f32[2,64,256]{2,1,0:T(8,128)S(1)} %fusion.8), channel_id=1, source_target_pairs={{0,16},{1,30},{2,17},{3,19},{4,20},{5,18},{6,21},{7,23},{8,24},{9,... | collective-permute-start | bytes 393224 | tf_op jit(solution)/shard_map/ppermute | solution.py:217
  31.5 0.0 collective-permute-done.4
  31.6 1.4 %collective-permute-start.5 = (f32[2,64,256]{2,1,0:T(8,128)S(1)}, f32[2,64,256]{2,1,0:T(8,128)S(1)}, u32[]{:S(2)}, u32[]{:S(2)}) collective-permute-start(f32[2,64,256]{2,1,0:T(8,128)S(1)} %fusion.11), channel_id=1, source_target_pairs={{0,16},{1,30},{2,17},{3,19},{4,20},{5,18},{6,21},{7,23},{8,24},{9,... | collective-permute-start | bytes 393224 | tf_op jit(solution)/shard_map/ppermute | solution.py:217
  32.9 4.0 %collective-permute-done.12.moving = f32[2,64,256]{2,1,0:T(8,128)S(1)} collective-permute-done((f32[2,64,256]{2,1,0:T(8,128)S(1)}, f32[2,64,256]{2,1,0:T(8,128)S(1)}, u32[]{:S(2)}, u32[]{:S(2)}) %collective-permute-start.12) | collective-permute-done | bytes 131104 | tf_op jit(solution)/shard_map/ppermute | solution.py:217
  37.0 0.0 collective-permute-start.13
  37.0 1.2 %collective-permute-done.13.crossed = f32[64,256]{1,0:T(8,128)S(1)} collective-permute-done((f32[64,256]{1,0:T(8,128)S(1)}, f32[64,256]{1,0:T(8,128)S(1)}, u32[]{:S(2)}, u32[]{:S(2)}) %collective-permute-start.13) | collective-permute-done | bytes 65568 | tf_op jit(solution)/shard_map/ppermute | solution.py:215
  38.2 1.0 %shard_map.80 = (f32[64,256]{1,0:T(8,128)S(1)}, bf16[128,256]{1,0:T(8,128)(2,1)S(1)}, f32[2,64,256]{2,1,0:T(8,128)S(1)}, f32[2,64,256]{2,1,0:T(8,128)S(1)}) custom-call(s32[2,16]{1,0:T(2,128)S(1)} %get-tuple-element.29.table, f32[2,128,256]{2,1,0:T(8,128)S(1)} %copy-done, f32[2,64,256]{2,1,0:T(8,128)S(1)} %collective-permute-done.12.moving, ...), custom_call_target="tpu_custom_call" | custom-call | flops 201326592 | bytes 786432 | tf_op jit(solution)/shard_map/pallas_call | solution.py:178
  39.2 1.0 %shard_map.82 = (f32[6,64,256]{2,1,0:T(8,128)S(1)}, f32[6,64,256]{2,1,0:T(8,128)S(1)}) custom-call(s32[2,16]{1,0:T(2,128)S(1)} %get-tuple-element.29.table, bf16[128,256]{1,0:T(8,128)(2,1)S(1)} %get-tuple-element.49.lhs, bf16[256,4096]{1,0:T(8,128)(2,1)S(1)} %get-tuple-element.31.factor), custom_call_target="tpu_custom_call" | custom-call | flops 402653184 | bytes 1572864 | tf_op jit(solution)/shard_map/pallas_call | solution.py:187
  40.2 0.2 collective-permute-start.20
  40.4 0.0 collective-permute-done.5.moving
  40.4 0.4 collective-permute-start.6
  40.9 0.3 collective-permute-start.21
  41.1 0.9 %collective-permute-done.6.crossed = f32[64,256]{1,0:T(8,128)S(1)} collective-permute-done((f32[64,256]{1,0:T(8,128)S(1)}, f32[64,256]{1,0:T(8,128)S(1)}, u32[]{:S(2)}, u32[]{:S(2)}) %collective-permute-start.6) | collective-permute-done | bytes 65568 | tf_op jit(solution)/shard_map/ppermute | solution.py:215
  42.1 1.0 %shard_map.79 = (f32[64,256]{1,0:T(8,128)S(1)}, bf16[128,256]{1,0:T(8,128)(2,1)S(1)}, f32[2,64,256]{2,1,0:T(8,128)S(1)}, f32[2,64,256]{2,1,0:T(8,128)S(1)}) custom-call(s32[2,16]{1,0:T(2,128)S(1)} %get-tuple-element.29.table, f32[2,128,256]{2,1,0:T(8,128)S(1)} %copy-done, f32[2,64,256]{2,1,0:T(8,128)S(1)} %collective-permute-done.5.moving, ...), custom_call_target="tpu_custom_call" | custom-call | flops 201326592 | bytes 786432 | tf_op jit(solution)/shard_map/pallas_call | solution.py:178
  43.0 1.0 %shard_map.81 = (f32[6,64,256]{2,1,0:T(8,128)S(1)}, f32[6,64,256]{2,1,0:T(8,128)S(1)}) custom-call(s32[2,16]{1,0:T(2,128)S(1)} %get-tuple-element.29.table, bf16[128,256]{1,0:T(8,128)(2,1)S(1)} %get-tuple-element.44.lhs, bf16[256,4096]{1,0:T(8,128)(2,1)S(1)} %get-tuple-element.31.factor), custom_call_target="tpu_custom_call" | custom-call | flops 402653184 | bytes 1572864 | tf_op jit(solution)/shard_map/pallas_call | solution.py:187
  44.0 0.2 collective-permute-start.14
  44.3 0.4 collective-permute-start.15
  44.6 0.0 collective-permute-done.21
  44.7 3.1 %collective-permute-start.22 = (f32[2,64,256]{2,1,0:T(8,128)S(1)}, f32[2,64,256]{2,1,0:T(8,128)S(1)}, u32[]{:S(2)}, u32[]{:S(2)}) collective-permute-start(f32[2,64,256]{2,1,0:T(8,128)S(1)} %add.111), channel_id=1, source_target_pairs={{0,3},{1,14},{2,1},{3,4},{4,7},{5,2},{6,5},{7,8},{8,11},{9,6},{10,... | collective-permute-start | bytes 393224 | tf_op jit(solution)/shard_map/ppermute | solution.py:216
  47.7 0.0 collective-permute-done.15
  47.7 1.4 %collective-permute-start.16 = (f32[2,64,256]{2,1,0:T(8,128)S(1)}, f32[2,64,256]{2,1,0:T(8,128)S(1)}, u32[]{:S(2)}, u32[]{:S(2)}) collective-permute-start(f32[2,64,256]{2,1,0:T(8,128)S(1)} %add.104), channel_id=1, source_target_pairs={{0,3},{1,14},{2,1},{3,4},{4,7},{5,2},{6,5},{7,8},{8,11},{9,6},{10,... | collective-permute-start | bytes 393224 | tf_op jit(solution)/shard_map/ppermute | solution.py:216
  49.1 0.6 collective-permute-done.22
  49.7 0.0 collective-permute-done.20
  49.7 3.7 %collective-permute-start.23 = (f32[2,64,256]{2,1,0:T(8,128)S(1)}, f32[2,64,256]{2,1,0:T(8,128)S(1)}, u32[]{:S(2)}, u32[]{:S(2)}) collective-permute-start(f32[2,64,256]{2,1,0:T(8,128)S(1)} %fusion), channel_id=1, source_target_pairs={{0,3},{1,14},{2,1},{3,4},{4,7},{5,2},{6,5},{7,8},{8,11},{9,6},{10,... | collective-permute-start | bytes 393224 | tf_op jit(solution)/shard_map/ppermute | solution.py:216
  53.4 0.0 collective-permute-done.16
  53.4 0.0 collective-permute-done.14
  53.5 1.4 %collective-permute-start.17 = (f32[2,64,256]{2,1,0:T(8,128)S(1)}, f32[2,64,256]{2,1,0:T(8,128)S(1)}, u32[]{:S(2)}, u32[]{:S(2)}) collective-permute-start(f32[2,64,256]{2,1,0:T(8,128)S(1)} %fusion.3), channel_id=1, source_target_pairs={{0,3},{1,14},{2,1},{3,4},{4,7},{5,2},{6,5},{7,8},{8,11},{9,6},{10,... | collective-permute-start | bytes 393224 | tf_op jit(solution)/shard_map/ppermute | solution.py:216
  54.8 0.5 collective-permute-done.23
  55.4 3.7 %collective-permute-start.24 = (f32[2,64,256]{2,1,0:T(8,128)S(1)}, f32[2,64,256]{2,1,0:T(8,128)S(1)}, u32[]{:S(2)}, u32[]{:S(2)}) collective-permute-start(f32[2,64,256]{2,1,0:T(8,128)S(1)} %fusion.1), channel_id=1, source_target_pairs={{0,3},{1,14},{2,1},{3,4},{4,7},{5,2},{6,5},{7,8},{8,11},{9,6},{10,... | collective-permute-start | bytes 393224 | tf_op jit(solution)/shard_map/ppermute | solution.py:216
  59.2 1.4 %collective-permute-start.18 = (f32[2,64,256]{2,1,0:T(8,128)S(1)}, f32[2,64,256]{2,1,0:T(8,128)S(1)}, u32[]{:S(2)}, u32[]{:S(2)}) collective-permute-start(f32[2,64,256]{2,1,0:T(8,128)S(1)} %fusion.4), channel_id=1, source_target_pairs={{0,3},{1,14},{2,1},{3,4},{4,7},{5,2},{6,5},{7,8},{8,11},{9,6},{10,... | collective-permute-start | bytes 393224 | tf_op jit(solution)/shard_map/ppermute | solution.py:216
  60.5 0.5 collective-permute-done.24
  61.1 1.8 %collective-permute-start.25 = (f32[2,64,256]{2,1,0:T(8,128)S(1)}, f32[2,64,256]{2,1,0:T(8,128)S(1)}, u32[]{:S(2)}, u32[]{:S(2)}) collective-permute-start(f32[2,64,256]{2,1,0:T(8,128)S(1)} %fusion.2), channel_id=1, source_target_pairs={{0,16},{1,30},{2,17},{3,19},{4,20},{5,18},{6,21},{7,23},{8,24},{9,... | collective-permute-start | bytes 393224 | tf_op jit(solution)/shard_map/ppermute | solution.py:217
  63.0 0.7 collective-permute-done.18
  63.7 0.7 collective-permute-start.19
  64.4 5.9 %collective-permute-done.25 = f32[2,64,256]{2,1,0:T(8,128)S(1)} collective-permute-done((f32[2,64,256]{2,1,0:T(8,128)S(1)}, f32[2,64,256]{2,1,0:T(8,128)S(1)}, u32[]{:S(2)}, u32[]{:S(2)}) %collective-permute-start.25) | collective-permute-done | bytes 131104 | tf_op jit(solution)/shard_map/ppermute | solution.py:217
  70.3 1.1 %collective-permute-start.27 = (f32[64,256]{1,0:T(8,128)S(1)}, f32[64,256]{1,0:T(8,128)S(1)}, u32[]{:S(2)}, u32[]{:S(2)}) collective-permute-start(f32[64,256]{1,0:T(8,128)S(1)} %get-tuple-element.56), channel_id=1, source_target_pairs={{0,1},{1,0},{2,3},{3,2},{4,5},{5,4},{6,7},{7,6},{8,9},{9,8},{10,11... | collective-permute-start | bytes 196616 | tf_op jit(solution)/shard_map/ppermute | solution.py:215
  71.4 1.8 %collective-permute-done.19 = f32[2,64,256]{2,1,0:T(8,128)S(1)} collective-permute-done((f32[2,64,256]{2,1,0:T(8,128)S(1)}, f32[2,64,256]{2,1,0:T(8,128)S(1)}, u32[]{:S(2)}, u32[]{:S(2)}) %collective-permute-start.19) | collective-permute-done | bytes 131104 | tf_op jit(solution)/shard_map/ppermute | solution.py:217
  73.2 0.7 collective-permute-start.26
  73.9 0.7 pad_maximum_fusion
  74.6 0.0 collective-permute-done.27
  74.6 0.2 collective-permute-done.26
  74.8 0.7 fusion.12
  (22 shorter events, 0.4 us)
Async XLA Ops:
  4.4 33.8 %copy-start = (f32[2,128,256]{2,1,0:T(8,128)S(1)}, f32[2,128,256]{2,1,0:T(8,128)}, u32[]{:S(2)}) copy-start(f32[2,128,256]{2,1,0:T(8,128)} %right_sides.5) | copy-start | bytes 786436
  4.4 11.0 %collective-permute-start.7 = (f32[6,64,256]{2,1,0:T(8,128)S(1)}, f32[6,64,256]{2,1,0:T(8,128)S(1)}, u32[]{:S(2)}, u32[]{:S(2)}) collective-permute-start(f32[6,64,256]{2,1,0:T(8,128)S(1)} %get-tuple-element.40), channel_id=1, source_target_pairs={{0,1},{1,0},{2,3},{3,2},{4,5},{5,4},{6,7},{7,6},{8,9},{9,8},{10,11... | collective-permute-start | bytes 1179656 | tf_op jit(solution)/shard_map/ppermute | solution.py:215
  7.7 1.5 %collective-permute-start.8 = (f32[2,64,256]{2,1,0:T(8,128)S(1)}, f32[2,64,256]{2,1,0:T(8,128)S(1)}, u32[]{:S(2)}, u32[]{:S(2)}) collective-permute-start(f32[2,64,256]{2,1,0:T(8,128)S(1)} %get-tuple-element.42), channel_id=1, source_target_pairs={{0,1},{1,0},{2,3},{3,2},{4,5},{5,4},{6,7},{7,6},{8,9},{9,8},{10,11... | collective-permute-start | bytes 393224 | tf_op jit(solution)/shard_map/ppermute | solution.py:215
  7.8 11.4 %collective-permute-start = (f32[6,64,256]{2,1,0:T(8,128)S(1)}, f32[6,64,256]{2,1,0:T(8,128)S(1)}, u32[]{:S(2)}, u32[]{:S(2)}) collective-permute-start(f32[6,64,256]{2,1,0:T(8,128)S(1)} %get-tuple-element.33), channel_id=1, source_target_pairs={{0,1},{1,0},{2,3},{3,2},{4,5},{5,4},{6,7},{7,6},{8,9},{9,8},{10,11... | collective-permute-start | bytes 1179656 | tf_op jit(solution)/shard_map/ppermute | solution.py:215
  8.2 5.3 %collective-permute-start.1 = (f32[2,64,256]{2,1,0:T(8,128)S(1)}, f32[2,64,256]{2,1,0:T(8,128)S(1)}, u32[]{:S(2)}, u32[]{:S(2)}) collective-permute-start(f32[2,64,256]{2,1,0:T(8,128)S(1)} %get-tuple-element.35), channel_id=1, source_target_pairs={{0,1},{1,0},{2,3},{3,2},{4,5},{5,4},{6,7},{7,6},{8,9},{9,8},{10,11... | collective-permute-start | bytes 393224 | tf_op jit(solution)/shard_map/ppermute | solution.py:215
  9.3 6.2 %collective-permute-start.9 = (f32[2,64,256]{2,1,0:T(8,128)S(1)}, f32[2,64,256]{2,1,0:T(8,128)S(1)}, u32[]{:S(2)}, u32[]{:S(2)}) collective-permute-start(f32[2,64,256]{2,1,0:T(8,128)S(1)} %add.97), channel_id=1, source_target_pairs={{0,3},{1,14},{2,1},{3,4},{4,7},{5,2},{6,5},{7,8},{8,11},{9,6},{10,... | collective-permute-start | bytes 393224 | tf_op jit(solution)/shard_map/ppermute | solution.py:216
  13.5 5.7 %collective-permute-start.2 = (f32[2,64,256]{2,1,0:T(8,128)S(1)}, f32[2,64,256]{2,1,0:T(8,128)S(1)}, u32[]{:S(2)}, u32[]{:S(2)}) collective-permute-start(f32[2,64,256]{2,1,0:T(8,128)S(1)} %add.90), channel_id=1, source_target_pairs={{0,3},{1,14},{2,1},{3,4},{4,7},{5,2},{6,5},{7,8},{8,11},{9,6},{10,... | collective-permute-start | bytes 393224 | tf_op jit(solution)/shard_map/ppermute | solution.py:216
  15.4 5.7 %collective-permute-start.10 = (f32[2,64,256]{2,1,0:T(8,128)S(1)}, f32[2,64,256]{2,1,0:T(8,128)S(1)}, u32[]{:S(2)}, u32[]{:S(2)}) collective-permute-start(f32[2,64,256]{2,1,0:T(8,128)S(1)} %fusion.6), channel_id=1, source_target_pairs={{0,3},{1,14},{2,1},{3,4},{4,7},{5,2},{6,5},{7,8},{8,11},{9,6},{10,... | collective-permute-start | bytes 393224 | tf_op jit(solution)/shard_map/ppermute | solution.py:216
  19.2 5.7 %collective-permute-start.3 = (f32[2,64,256]{2,1,0:T(8,128)S(1)}, f32[2,64,256]{2,1,0:T(8,128)S(1)}, u32[]{:S(2)}, u32[]{:S(2)}) collective-permute-start(f32[2,64,256]{2,1,0:T(8,128)S(1)} %fusion.9), channel_id=1, source_target_pairs={{0,3},{1,14},{2,1},{3,4},{4,7},{5,2},{6,5},{7,8},{8,11},{9,6},{10,... | collective-permute-start | bytes 393224 | tf_op jit(solution)/shard_map/ppermute | solution.py:216
  21.2 5.7 %collective-permute-start.11 = (f32[2,64,256]{2,1,0:T(8,128)S(1)}, f32[2,64,256]{2,1,0:T(8,128)S(1)}, u32[]{:S(2)}, u32[]{:S(2)}) collective-permute-start(f32[2,64,256]{2,1,0:T(8,128)S(1)} %fusion.7), channel_id=1, source_target_pairs={{0,3},{1,14},{2,1},{3,4},{4,7},{5,2},{6,5},{7,8},{8,11},{9,6},{10,... | collective-permute-start | bytes 393224 | tf_op jit(solution)/shard_map/ppermute | solution.py:216
  24.9 6.6 %collective-permute-start.4 = (f32[2,64,256]{2,1,0:T(8,128)S(1)}, f32[2,64,256]{2,1,0:T(8,128)S(1)}, u32[]{:S(2)}, u32[]{:S(2)}) collective-permute-start(f32[2,64,256]{2,1,0:T(8,128)S(1)} %fusion.10), channel_id=1, source_target_pairs={{0,3},{1,14},{2,1},{3,4},{4,7},{5,2},{6,5},{7,8},{8,11},{9,6},{10,... | collective-permute-start | bytes 393224 | tf_op jit(solution)/shard_map/ppermute | solution.py:216
  26.9 10.1 %collective-permute-start.12 = (f32[2,64,256]{2,1,0:T(8,128)S(1)}, f32[2,64,256]{2,1,0:T(8,128)S(1)}, u32[]{:S(2)}, u32[]{:S(2)}) collective-permute-start(f32[2,64,256]{2,1,0:T(8,128)S(1)} %fusion.8), channel_id=1, source_target_pairs={{0,16},{1,30},{2,17},{3,19},{4,20},{5,18},{6,21},{7,23},{8,24},{9,... | collective-permute-start | bytes 393224 | tf_op jit(solution)/shard_map/ppermute | solution.py:217
  31.6 8.8 %collective-permute-start.5 = (f32[2,64,256]{2,1,0:T(8,128)S(1)}, f32[2,64,256]{2,1,0:T(8,128)S(1)}, u32[]{:S(2)}, u32[]{:S(2)}) collective-permute-start(f32[2,64,256]{2,1,0:T(8,128)S(1)} %fusion.11), channel_id=1, source_target_pairs={{0,16},{1,30},{2,17},{3,19},{4,20},{5,18},{6,21},{7,23},{8,24},{9,... | collective-permute-start | bytes 393224 | tf_op jit(solution)/shard_map/ppermute | solution.py:217
  37.0 1.3 %collective-permute-start.13 = (f32[64,256]{1,0:T(8,128)S(1)}, f32[64,256]{1,0:T(8,128)S(1)}, u32[]{:S(2)}, u32[]{:S(2)}) collective-permute-start(f32[64,256]{1,0:T(8,128)S(1)} %slice_bitcast_fusion.4), channel_id=1, source_target_pairs={{0,1},{1,0},{2,3},{3,2},{4,5},{5,4},{6,7},{7,6},{8,9},{9,8},{10,11... | collective-permute-start | bytes 196616 | tf_op jit(solution)/shard_map/ppermute | solution.py:215
  40.2 9.5 %collective-permute-start.20 = (f32[6,64,256]{2,1,0:T(8,128)S(1)}, f32[6,64,256]{2,1,0:T(8,128)S(1)}, u32[]{:S(2)}, u32[]{:S(2)}) collective-permute-start(f32[6,64,256]{2,1,0:T(8,128)S(1)} %get-tuple-element.51), channel_id=1, source_target_pairs={{0,1},{1,0},{2,3},{3,2},{4,5},{5,4},{6,7},{7,6},{8,9},{9,8},{10,11... | collective-permute-start | bytes 1179656 | tf_op jit(solution)/shard_map/ppermute | solution.py:215
  40.4 1.6 %collective-permute-start.6 = (f32[64,256]{1,0:T(8,128)S(1)}, f32[64,256]{1,0:T(8,128)S(1)}, u32[]{:S(2)}, u32[]{:S(2)}) collective-permute-start(f32[64,256]{1,0:T(8,128)S(1)} %slice_bitcast_fusion.5), channel_id=1, source_target_pairs={{0,1},{1,0},{2,3},{3,2},{4,5},{5,4},{6,7},{7,6},{8,9},{9,8},{10,11... | collective-permute-start | bytes 196616 | tf_op jit(solution)/shard_map/ppermute | solution.py:215
  40.9 3.8 %collective-permute-start.21 = (f32[2,64,256]{2,1,0:T(8,128)S(1)}, f32[2,64,256]{2,1,0:T(8,128)S(1)}, u32[]{:S(2)}, u32[]{:S(2)}) collective-permute-start(f32[2,64,256]{2,1,0:T(8,128)S(1)} %get-tuple-element.53), channel_id=1, source_target_pairs={{0,1},{1,0},{2,3},{3,2},{4,5},{5,4},{6,7},{7,6},{8,9},{9,8},{10,11... | collective-permute-start | bytes 393224 | tf_op jit(solution)/shard_map/ppermute | solution.py:215
  44.0 9.4 %collective-permute-start.14 = (f32[6,64,256]{2,1,0:T(8,128)S(1)}, f32[6,64,256]{2,1,0:T(8,128)S(1)}, u32[]{:S(2)}, u32[]{:S(2)}) collective-permute-start(f32[6,64,256]{2,1,0:T(8,128)S(1)} %get-tuple-element.46), channel_id=1, source_target_pairs={{0,1},{1,0},{2,3},{3,2},{4,5},{5,4},{6,7},{7,6},{8,9},{9,8},{10,11... | collective-permute-start | bytes 1179656 | tf_op jit(solution)/shard_map/ppermute | solution.py:215
  44.3 3.4 %collective-permute-start.15 = (f32[2,64,256]{2,1,0:T(8,128)S(1)}, f32[2,64,256]{2,1,0:T(8,128)S(1)}, u32[]{:S(2)}, u32[]{:S(2)}) collective-permute-start(f32[2,64,256]{2,1,0:T(8,128)S(1)} %get-tuple-element.48), channel_id=1, source_target_pairs={{0,1},{1,0},{2,3},{3,2},{4,5},{5,4},{6,7},{7,6},{8,9},{9,8},{10,11... | collective-permute-start | bytes 393224 | tf_op jit(solution)/shard_map/ppermute | solution.py:215
  44.7 5.0 %collective-permute-start.22 = (f32[2,64,256]{2,1,0:T(8,128)S(1)}, f32[2,64,256]{2,1,0:T(8,128)S(1)}, u32[]{:S(2)}, u32[]{:S(2)}) collective-permute-start(f32[2,64,256]{2,1,0:T(8,128)S(1)} %add.111), channel_id=1, source_target_pairs={{0,3},{1,14},{2,1},{3,4},{4,7},{5,2},{6,5},{7,8},{8,11},{9,6},{10,... | collective-permute-start | bytes 393224 | tf_op jit(solution)/shard_map/ppermute | solution.py:216
  47.7 5.7 %collective-permute-start.16 = (f32[2,64,256]{2,1,0:T(8,128)S(1)}, f32[2,64,256]{2,1,0:T(8,128)S(1)}, u32[]{:S(2)}, u32[]{:S(2)}) collective-permute-start(f32[2,64,256]{2,1,0:T(8,128)S(1)} %add.104), channel_id=1, source_target_pairs={{0,3},{1,14},{2,1},{3,4},{4,7},{5,2},{6,5},{7,8},{8,11},{9,6},{10,... | collective-permute-start | bytes 393224 | tf_op jit(solution)/shard_map/ppermute | solution.py:216
  49.7 5.7 %collective-permute-start.23 = (f32[2,64,256]{2,1,0:T(8,128)S(1)}, f32[2,64,256]{2,1,0:T(8,128)S(1)}, u32[]{:S(2)}, u32[]{:S(2)}) collective-permute-start(f32[2,64,256]{2,1,0:T(8,128)S(1)} %fusion), channel_id=1, source_target_pairs={{0,3},{1,14},{2,1},{3,4},{4,7},{5,2},{6,5},{7,8},{8,11},{9,6},{10,... | collective-permute-start | bytes 393224 | tf_op jit(solution)/shard_map/ppermute | solution.py:216
  53.5 5.7 %collective-permute-start.17 = (f32[2,64,256]{2,1,0:T(8,128)S(1)}, f32[2,64,256]{2,1,0:T(8,128)S(1)}, u32[]{:S(2)}, u32[]{:S(2)}) collective-permute-start(f32[2,64,256]{2,1,0:T(8,128)S(1)} %fusion.3), channel_id=1, source_target_pairs={{0,3},{1,14},{2,1},{3,4},{4,7},{5,2},{6,5},{7,8},{8,11},{9,6},{10,... | collective-permute-start | bytes 393224 | tf_op jit(solution)/shard_map/ppermute | solution.py:216
  55.4 5.7 %collective-permute-start.24 = (f32[2,64,256]{2,1,0:T(8,128)S(1)}, f32[2,64,256]{2,1,0:T(8,128)S(1)}, u32[]{:S(2)}, u32[]{:S(2)}) collective-permute-start(f32[2,64,256]{2,1,0:T(8,128)S(1)} %fusion.1), channel_id=1, source_target_pairs={{0,3},{1,14},{2,1},{3,4},{4,7},{5,2},{6,5},{7,8},{8,11},{9,6},{10,... | collective-permute-start | bytes 393224 | tf_op jit(solution)/shard_map/ppermute | solution.py:216
  59.2 4.5 %collective-permute-start.18 = (f32[2,64,256]{2,1,0:T(8,128)S(1)}, f32[2,64,256]{2,1,0:T(8,128)S(1)}, u32[]{:S(2)}, u32[]{:S(2)}) collective-permute-start(f32[2,64,256]{2,1,0:T(8,128)S(1)} %fusion.4), channel_id=1, source_target_pairs={{0,3},{1,14},{2,1},{3,4},{4,7},{5,2},{6,5},{7,8},{8,11},{9,6},{10,... | collective-permute-start | bytes 393224 | tf_op jit(solution)/shard_map/ppermute | solution.py:216
  61.1 9.1 %collective-permute-start.25 = (f32[2,64,256]{2,1,0:T(8,128)S(1)}, f32[2,64,256]{2,1,0:T(8,128)S(1)}, u32[]{:S(2)}, u32[]{:S(2)}) collective-permute-start(f32[2,64,256]{2,1,0:T(8,128)S(1)} %fusion.2), channel_id=1, source_target_pairs={{0,16},{1,30},{2,17},{3,19},{4,20},{5,18},{6,21},{7,23},{8,24},{9,... | collective-permute-start | bytes 393224 | tf_op jit(solution)/shard_map/ppermute | solution.py:217
  63.7 9.5 %collective-permute-start.19 = (f32[2,64,256]{2,1,0:T(8,128)S(1)}, f32[2,64,256]{2,1,0:T(8,128)S(1)}, u32[]{:S(2)}, u32[]{:S(2)}) collective-permute-start(f32[2,64,256]{2,1,0:T(8,128)S(1)} %fusion.5), channel_id=1, source_target_pairs={{0,16},{1,30},{2,17},{3,19},{4,20},{5,18},{6,21},{7,23},{8,24},{9,... | collective-permute-start | bytes 393224 | tf_op jit(solution)/shard_map/ppermute | solution.py:217
  70.3 4.4 %collective-permute-start.27 = (f32[64,256]{1,0:T(8,128)S(1)}, f32[64,256]{1,0:T(8,128)S(1)}, u32[]{:S(2)}, u32[]{:S(2)}) collective-permute-start(f32[64,256]{1,0:T(8,128)S(1)} %get-tuple-element.56), channel_id=1, source_target_pairs={{0,1},{1,0},{2,3},{3,2},{4,5},{5,4},{6,7},{7,6},{8,9},{9,8},{10,11... | collective-permute-start | bytes 196616 | tf_op jit(solution)/shard_map/ppermute | solution.py:215
  73.2 1.6 %collective-permute-start.26 = (f32[64,256]{1,0:T(8,128)S(1)}, f32[64,256]{1,0:T(8,128)S(1)}, u32[]{:S(2)}, u32[]{:S(2)}) collective-permute-start(f32[64,256]{1,0:T(8,128)S(1)} %get-tuple-element.54), channel_id=1, source_target_pairs={{0,1},{1,0},{2,3},{3,2},{4,5},{5,4},{6,7},{7,6},{8,9},{9,8},{10,11... | collective-permute-start | bytes 196616 | tf_op jit(solution)/shard_map/ppermute | solution.py:215

commit v6 on v4

--- a/solution.py
+++ b/solution.py
@@ -209,11 +209,12 @@
         return ((chip + ahead) % chips) * 2 + 1 - core
 
     def to_next_section(place):
+        last = sections - 1
         return [
-            (s * owners + i, (s + 1) % sections * owners + place(i))
-            for s in range(sections)
+            (s * owners + i, (s + 1) * owners + place(i))
+            for s in range(last)
             for i in range(owners)
-        ]
+        ] + [(last * owners + i, i ^ 1) for i in range(owners)]
 
     chain = [(i, next_on_chain(i)) for i in range(owners)]
     upward = lambda i: (i // 2 + i) % 2 == 0

time: 76.3 us -> 75.7 us (level)
  starting transfers between devices: 45.3 us -> 43.3 us
  waiting for transfers between devices: 21.4 us -> 22.7 us
    ppermute x12, starting transfers between devices: 11.2 us -> 7.16 us  [shards(): swap = lambda value: lax.ppermute(value, 'own', partner)]
    ppermute x4, waiting for transfers between devices: 12 us -> 14.6 us  [shards(): leave = lambda value: lax.ppermute(value, ('sec', 'own'), onward)]
    ppermute x12, starting transfers between devices: 26.6 us -> 28.9 us  [shards(): pass_on = lambda value: lax.ppermute(value, 'own', chain)]
    ppermute x12, waiting for transfers between devices: 7.12 us -> 5.92 us  [shards(): pass_on = lambda value: lax.ppermute(value, 'own', chain)]
  transfers between devices with their start and end apart: 28 -> 28, of which waited for: 15 -> 15; matrix products, arithmetic and copies ran while one was open for 1% -> 2% of each run, Pallas kernels for 1% -> 1%
where the time goes in v6:
time: 75.7 us; the launch traced here: 75.5 us
  starting transfers between devices  43.3 us (57%)
  waiting for transfers between devices  22.7 us (30%)
  Pallas kernels  6.85 us (9%)
  other arithmetic  1.78 us (2%)
  between operations  0.81 us (1%)
    ppermute x12, starting transfers between devices, shards(): pass_on = lambda value: lax.ppermute(value, 'own', chain)  28.9 us
    ppermute x4, waiting for transfers between devices, shards(): leave = lambda value: lax.ppermute(value, ('sec', 'own'), onward)  14.6 us
    ppermute x4, starting transfers between devices, shards(): leave = lambda value: lax.ppermute(value, ('sec', 'own'), onward)  7.22 us
    ppermute x12, starting transfers between devices, shards(): swap = lambda value: lax.ppermute(value, 'own', partner)  7.16 us
    ppermute x12, waiting for transfers between devices, shards(): pass_on = lambda value: lax.ppermute(value, 'own', chain)  5.92 us
    pallas_call x1, Pallas kernels, first_step(): call(kernel, 6, [HBM] * 6, outs, 4, scratch)  2.58 us
    pallas_call x2, Pallas kernels, late_step(): call(kernel, 16, [SMEM] + [VMEM] * (1 + len(parts)), outs, 4)  2.34 us
    ppermute x12, waiting for transfers between devices, shards(): swap = lambda value: lax.ppermute(value, 'own', partner)  2.26 us
  transfers between devices with their start and end apart: 28, of which 15 were waited for; matrix products, arithmetic and copies ran while one was open for 2% of the time, Pallas kernels for 1%

profile of v6, /device:TPU:1, one launch (start us, length us, event | category | flops | bytes accessed | tf_op | source)
XLA Modules:
  0.0 75.5 jit_solution(11319399483128723951)
XLA Ops:
  0.6 2.6 %shard_map.77 = (s32[2,16]{1,0:T(2,128)S(1)}, bf16[256,4096]{1,0:T(8,128)(2,1)S(1)}, bf16[256,256]{1,0:T(8,128)(2,1)S(1)}, bf16[256,256]{1,0:T(8,128)(2,1)S(1)},...) custom-call(s32[1,16]{1,0:T(1,128)} %ancestor.1, ...), custom_call_target="tpu_custom_call" | custom-call | flops 201326592 | bytes 786432 | tf_op jit(solution)/shard_map/pallas_call | solution.py:171
  3.2 1.2 %shard_map.78 = (f32[6,64,256]{2,1,0:T(8,128)S(1)}, f32[6,64,256]{2,1,0:T(8,128)S(1)}, f32[6,64,256]{2,1,0:T(8,128)S(1)}, f32[6,64,256]{2,1,0:T(8,128)S(1)}) custom-call(s32[2,16]{1,0:T(2,128)S(1)} %get-tuple-element.29.table, bf16[256,4096]{1,0:T(8,128)(2,1)S(1)} %get-tuple-element.30.factor, bf16[256,256]{1,0:T(8,128)(2,1)S(1)} %get-tuple-element.31.rest_0_), custom_call_target="tpu_custom_call" | custom-call | flops 536870912 | bytes 2097152 | tf_op jit(solution)/shard_map/pallas_call | solution.py:194
  4.4 3.3 %collective-permute-start = (f32[6,64,256]{2,1,0:T(8,128)S(1)}, f32[6,64,256]{2,1,0:T(8,128)S(1)}, u32[]{:S(2)}, u32[]{:S(2)}) collective-permute-start(f32[6,64,256]{2,1,0:T(8,128)S(1)} %get-tuple-element.33), channel_id=1, source_target_pairs={{0,1},{1,0},{2,3},{3,2},{4,5},{5,4},{6,7},{7,6},{8,9},{9,8},{10,11... | collective-permute-start | bytes 1179656 | tf_op jit(solution)/shard_map/ppermute | solution.py:224
  7.7 0.1 collective-permute-start.1
  7.8 0.4 collective-permute-start.7
  8.2 0.1 collective-permute-start.8
  8.3 0.9 %collective-permute-done.1 = f32[2,64,256]{2,1,0:T(8,128)S(1)} collective-permute-done((f32[2,64,256]{2,1,0:T(8,128)S(1)}, f32[2,64,256]{2,1,0:T(8,128)S(1)}, u32[]{:S(2)}, u32[]{:S(2)}) %collective-permute-start.1) | collective-permute-done | bytes 131104 | tf_op jit(solution)/shard_map/ppermute | solution.py:224
  9.2 4.2 %collective-permute-start.2 = (f32[2,64,256]{2,1,0:T(8,128)S(1)}, f32[2,64,256]{2,1,0:T(8,128)S(1)}, u32[]{:S(2)}, u32[]{:S(2)}) collective-permute-start(f32[2,64,256]{2,1,0:T(8,128)S(1)} %add.90), channel_id=1, source_target_pairs={{0,3},{1,14},{2,1},{3,4},{4,7},{5,2},{6,5},{7,8},{8,11},{9,6},{10,... | collective-permute-start | bytes 393224 | tf_op jit(solution)/shard_map/ppermute | solution.py:225
  13.4 0.0 collective-permute-done.8
  13.5 0.8 %collective-permute-start.9 = (f32[2,64,256]{2,1,0:T(8,128)S(1)}, f32[2,64,256]{2,1,0:T(8,128)S(1)}, u32[]{:S(2)}, u32[]{:S(2)}) collective-permute-start(f32[2,64,256]{2,1,0:T(8,128)S(1)} %add.97), channel_id=1, source_target_pairs={{0,3},{1,14},{2,1},{3,4},{4,7},{5,2},{6,5},{7,8},{8,11},{9,6},{10,... | collective-permute-start | bytes 393224 | tf_op jit(solution)/shard_map/ppermute | solution.py:225
  14.3 1.1 %collective-permute-done.2 = f32[2,64,256]{2,1,0:T(8,128)S(1)} collective-permute-done((f32[2,64,256]{2,1,0:T(8,128)S(1)}, f32[2,64,256]{2,1,0:T(8,128)S(1)}, u32[]{:S(2)}, u32[]{:S(2)}) %collective-permute-start.2) | collective-permute-done | bytes 131104 | tf_op jit(solution)/shard_map/ppermute | solution.py:225
  15.4 0.0 collective-permute-done
  15.4 3.7 %collective-permute-start.3 = (f32[2,64,256]{2,1,0:T(8,128)S(1)}, f32[2,64,256]{2,1,0:T(8,128)S(1)}, u32[]{:S(2)}, u32[]{:S(2)}) collective-permute-start(f32[2,64,256]{2,1,0:T(8,128)S(1)} %fusion.9), channel_id=1, source_target_pairs={{0,3},{1,14},{2,1},{3,4},{4,7},{5,2},{6,5},{7,8},{8,11},{9,6},{10,... | collective-permute-start | bytes 393224 | tf_op jit(solution)/shard_map/ppermute | solution.py:225
  19.2 0.0 collective-permute-done.9
  19.2 0.0 collective-permute-done.7
  19.2 1.4 %collective-permute-start.10 = (f32[2,64,256]{2,1,0:T(8,128)S(1)}, f32[2,64,256]{2,1,0:T(8,128)S(1)}, u32[]{:S(2)}, u32[]{:S(2)}) collective-permute-start(f32[2,64,256]{2,1,0:T(8,128)S(1)} %fusion.6), channel_id=1, source_target_pairs={{0,3},{1,14},{2,1},{3,4},{4,7},{5,2},{6,5},{7,8},{8,11},{9,6},{10,... | collective-permute-start | bytes 393224 | tf_op jit(solution)/shard_map/ppermute | solution.py:225
  20.6 0.5 collective-permute-done.3
  21.1 3.7 %collective-permute-start.4 = (f32[2,64,256]{2,1,0:T(8,128)S(1)}, f32[2,64,256]{2,1,0:T(8,128)S(1)}, u32[]{:S(2)}, u32[]{:S(2)}) collective-permute-start(f32[2,64,256]{2,1,0:T(8,128)S(1)} %fusion.10), channel_id=1, source_target_pairs={{0,3},{1,14},{2,1},{3,4},{4,7},{5,2},{6,5},{7,8},{8,11},{9,6},{10,... | collective-permute-start | bytes 393224 | tf_op jit(solution)/shard_map/ppermute | solution.py:225
  24.9 0.0 collective-permute-done.10
  24.9 1.4 %collective-permute-start.11 = (f32[2,64,256]{2,1,0:T(8,128)S(1)}, f32[2,64,256]{2,1,0:T(8,128)S(1)}, u32[]{:S(2)}, u32[]{:S(2)}) collective-permute-start(f32[2,64,256]{2,1,0:T(8,128)S(1)} %fusion.7), channel_id=1, source_target_pairs={{0,3},{1,14},{2,1},{3,4},{4,7},{5,2},{6,5},{7,8},{8,11},{9,6},{10,... | collective-permute-start | bytes 393224 | tf_op jit(solution)/shard_map/ppermute | solution.py:225
  26.3 0.5 collective-permute-done.4
  26.9 4.7 %collective-permute-start.5 = (f32[2,64,256]{2,1,0:T(8,128)S(1)}, f32[2,64,256]{2,1,0:T(8,128)S(1)}, u32[]{:S(2)}, u32[]{:S(2)}) collective-permute-start(f32[2,64,256]{2,1,0:T(8,128)S(1)} %fusion.11), channel_id=1, source_target_pairs={{0,16},{1,30},{2,17},{3,19},{4,20},{5,18},{6,21},{7,23},{8,24},{9,... | collective-permute-start | bytes 393224 | tf_op jit(solution)/shard_map/ppermute | solution.py:226
  31.5 0.0 collective-permute-done.11
  31.6 1.4 %collective-permute-start.12 = (f32[2,64,256]{2,1,0:T(8,128)S(1)}, f32[2,64,256]{2,1,0:T(8,128)S(1)}, u32[]{:S(2)}, u32[]{:S(2)}) collective-permute-start(f32[2,64,256]{2,1,0:T(8,128)S(1)} %fusion.8), channel_id=1, source_target_pairs={{0,16},{1,30},{2,17},{3,19},{4,20},{5,18},{6,21},{7,23},{8,24},{9,... | collective-permute-start | bytes 393224 | tf_op jit(solution)/shard_map/ppermute | solution.py:226
  32.9 4.0 %collective-permute-done.5.moving = f32[2,64,256]{2,1,0:T(8,128)S(1)} collective-permute-done((f32[2,64,256]{2,1,0:T(8,128)S(1)}, f32[2,64,256]{2,1,0:T(8,128)S(1)}, u32[]{:S(2)}, u32[]{:S(2)}) %collective-permute-start.5) | collective-permute-done | bytes 131104 | tf_op jit(solution)/shard_map/ppermute | solution.py:226
  36.9 0.0 collective-permute-start.6
  37.0 2.4 %collective-permute-done.12.moving = f32[2,64,256]{2,1,0:T(8,128)S(1)} collective-permute-done((f32[2,64,256]{2,1,0:T(8,128)S(1)}, f32[2,64,256]{2,1,0:T(8,128)S(1)}, u32[]{:S(2)}, u32[]{:S(2)}) %collective-permute-start.12) | collective-permute-done | bytes 131104 | tf_op jit(solution)/shard_map/ppermute | solution.py:226
  39.4 0.0 collective-permute-start.13
  39.4 0.0 collective-permute-done.6.crossed
  39.4 0.0 copy-done
  39.4 1.0 %shard_map.79 = (f32[64,256]{1,0:T(8,128)S(1)}, bf16[128,256]{1,0:T(8,128)(2,1)S(1)}, f32[2,64,256]{2,1,0:T(8,128)S(1)}, f32[2,64,256]{2,1,0:T(8,128)S(1)}) custom-call(s32[2,16]{1,0:T(2,128)S(1)} %get-tuple-element.29.table, f32[2,128,256]{2,1,0:T(8,128)S(1)} %copy-done, f32[2,64,256]{2,1,0:T(8,128)S(1)} %collective-permute-done.5.moving, ...), custom_call_target="tpu_custom_call" | custom-call | flops 201326592 | bytes 786432 | tf_op jit(solution)/shard_map/pallas_call | solution.py:184
  40.4 0.2 collective-permute-done.13.crossed
  40.6 1.0 %shard_map.80 = (f32[64,256]{1,0:T(8,128)S(1)}, bf16[128,256]{1,0:T(8,128)(2,1)S(1)}, f32[2,64,256]{2,1,0:T(8,128)S(1)}, f32[2,64,256]{2,1,0:T(8,128)S(1)}) custom-call(s32[2,16]{1,0:T(2,128)S(1)} %get-tuple-element.29.table, f32[2,128,256]{2,1,0:T(8,128)S(1)} %copy-done, f32[2,64,256]{2,1,0:T(8,128)S(1)} %collective-permute-done.12.moving, ...), custom_call_target="tpu_custom_call" | custom-call | flops 201326592 | bytes 786432 | tf_op jit(solution)/shard_map/pallas_call | solution.py:184
  41.6 1.2 %shard_map.81 = (f32[6,64,256]{2,1,0:T(8,128)S(1)}, f32[6,64,256]{2,1,0:T(8,128)S(1)}, f32[6,64,256]{2,1,0:T(8,128)S(1)}, f32[6,64,256]{2,1,0:T(8,128)S(1)}) custom-call(s32[2,16]{1,0:T(2,128)S(1)} %get-tuple-element.29.table, bf16[256,4096]{1,0:T(8,128)(2,1)S(1)} %get-tuple-element.30.factor, bf16[128,256]{1,0:T(8,128)(2,1)S(1)} %get-tuple-element.44.rest_0_, ...), custom_call_target="tpu_custom_call" | custom-call | flops 536870912 | bytes 2097152 | tf_op jit(solution)/shard_map/pallas_call | solution.py:194
  42.8 0.5 collective-permute-start.14
  43.3 0.3 collective-permute-start.15
  43.5 0.2 collective-permute-start.20
  43.8 0.3 collective-permute-start.21
  44.1 0.9 %collective-permute-done.15 = f32[2,64,256]{2,1,0:T(8,128)S(1)} collective-permute-done((f32[2,64,256]{2,1,0:T(8,128)S(1)}, f32[2,64,256]{2,1,0:T(8,128)S(1)}, u32[]{:S(2)}, u32[]{:S(2)}) %collective-permute-start.15) | collective-permute-done | bytes 131104 | tf_op jit(solution)/shard_map/ppermute | solution.py:224
  45.0 2.8 %collective-permute-start.16 = (f32[2,64,256]{2,1,0:T(8,128)S(1)}, f32[2,64,256]{2,1,0:T(8,128)S(1)}, u32[]{:S(2)}, u32[]{:S(2)}) collective-permute-start(f32[2,64,256]{2,1,0:T(8,128)S(1)} %add.104), channel_id=1, source_target_pairs={{0,3},{1,14},{2,1},{3,4},{4,7},{5,2},{6,5},{7,8},{8,11},{9,6},{10,... | collective-permute-start | bytes 393224 | tf_op jit(solution)/shard_map/ppermute | solution.py:225
  47.8 0.0 collective-permute-done.21
  47.8 0.7 collective-permute-start.22
  48.5 1.2 %collective-permute-done.16 = f32[2,64,256]{2,1,0:T(8,128)S(1)} collective-permute-done((f32[2,64,256]{2,1,0:T(8,128)S(1)}, f32[2,64,256]{2,1,0:T(8,128)S(1)}, u32[]{:S(2)}, u32[]{:S(2)}) %collective-permute-start.16) | collective-permute-done | bytes 131104 | tf_op jit(solution)/shard_map/ppermute | solution.py:225
  49.7 0.0 collective-permute-done.14
  49.8 3.7 %collective-permute-start.17 = (f32[2,64,256]{2,1,0:T(8,128)S(1)}, f32[2,64,256]{2,1,0:T(8,128)S(1)}, u32[]{:S(2)}, u32[]{:S(2)}) collective-permute-start(f32[2,64,256]{2,1,0:T(8,128)S(1)} %fusion.3), channel_id=1, source_target_pairs={{0,3},{1,14},{2,1},{3,4},{4,7},{5,2},{6,5},{7,8},{8,11},{9,6},{10,... | collective-permute-start | bytes 393224 | tf_op jit(solution)/shard_map/ppermute | solution.py:225
  53.5 0.0 collective-permute-done.22
  53.5 0.0 collective-permute-done.20
  53.5 1.4 %collective-permute-start.23 = (f32[2,64,256]{2,1,0:T(8,128)S(1)}, f32[2,64,256]{2,1,0:T(8,128)S(1)}, u32[]{:S(2)}, u32[]{:S(2)}) collective-permute-start(f32[2,64,256]{2,1,0:T(8,128)S(1)} %fusion), channel_id=1, source_target_pairs={{0,3},{1,14},{2,1},{3,4},{4,7},{5,2},{6,5},{7,8},{8,11},{9,6},{10,... | collective-permute-start | bytes 393224 | tf_op jit(solution)/shard_map/ppermute | solution.py:225
  54.9 0.5 collective-permute-done.17
  55.5 3.7 %collective-permute-start.18 = (f32[2,64,256]{2,1,0:T(8,128)S(1)}, f32[2,64,256]{2,1,0:T(8,128)S(1)}, u32[]{:S(2)}, u32[]{:S(2)}) collective-permute-start(f32[2,64,256]{2,1,0:T(8,128)S(1)} %fusion.4), channel_id=1, source_target_pairs={{0,3},{1,14},{2,1},{3,4},{4,7},{5,2},{6,5},{7,8},{8,11},{9,6},{10,... | collective-permute-start | bytes 393224 | tf_op jit(solution)/shard_map/ppermute | solution.py:225
  59.2 0.0 collective-permute-done.23
  59.2 1.4 %collective-permute-start.24 = (f32[2,64,256]{2,1,0:T(8,128)S(1)}, f32[2,64,256]{2,1,0:T(8,128)S(1)}, u32[]{:S(2)}, u32[]{:S(2)}) collective-permute-start(f32[2,64,256]{2,1,0:T(8,128)S(1)} %fusion.1), channel_id=1, source_target_pairs={{0,3},{1,14},{2,1},{3,4},{4,7},{5,2},{6,5},{7,8},{8,11},{9,6},{10,... | collective-permute-start | bytes 393224 | tf_op jit(solution)/shard_map/ppermute | solution.py:225
  60.6 0.5 collective-permute-done.18
  61.2 1.1 %collective-permute-start.19 = (f32[2,64,256]{2,1,0:T(8,128)S(1)}, f32[2,64,256]{2,1,0:T(8,128)S(1)}, u32[]{:S(2)}, u32[]{:S(2)}) collective-permute-start(f32[2,64,256]{2,1,0:T(8,128)S(1)} %fusion.5), channel_id=1, source_target_pairs={{0,16},{1,30},{2,17},{3,19},{4,20},{5,18},{6,21},{7,23},{8,24},{9,... | collective-permute-start | bytes 393224 | tf_op jit(solution)/shard_map/ppermute | solution.py:226
  62.3 1.4 %collective-permute-done.24 = f32[2,64,256]{2,1,0:T(8,128)S(1)} collective-permute-done((f32[2,64,256]{2,1,0:T(8,128)S(1)}, f32[2,64,256]{2,1,0:T(8,128)S(1)}, u32[]{:S(2)}, u32[]{:S(2)}) %collective-permute-start.24) | collective-permute-done | bytes 131104 | tf_op jit(solution)/shard_map/ppermute | solution.py:225
  63.7 0.1 collective-permute-start.25
  63.8 6.3 %collective-permute-done.19 = f32[2,64,256]{2,1,0:T(8,128)S(1)} collective-permute-done((f32[2,64,256]{2,1,0:T(8,128)S(1)}, f32[2,64,256]{2,1,0:T(8,128)S(1)}, u32[]{:S(2)}, u32[]{:S(2)}) %collective-permute-start.19) | collective-permute-done | bytes 131104 | tf_op jit(solution)/shard_map/ppermute | solution.py:226
  70.2 1.2 %collective-permute-start.26 = (f32[64,256]{1,0:T(8,128)S(1)}, f32[64,256]{1,0:T(8,128)S(1)}, u32[]{:S(2)}, u32[]{:S(2)}) collective-permute-start(f32[64,256]{1,0:T(8,128)S(1)} %get-tuple-element.54), channel_id=1, source_target_pairs={{0,1},{1,0},{2,3},{3,2},{4,5},{5,4},{6,7},{7,6},{8,9},{9,8},{10,11... | collective-permute-start | bytes 196616 | tf_op jit(solution)/shard_map/ppermute | solution.py:224
  71.4 1.8 %collective-permute-done.25 = f32[2,64,256]{2,1,0:T(8,128)S(1)} collective-permute-done((f32[2,64,256]{2,1,0:T(8,128)S(1)}, f32[2,64,256]{2,1,0:T(8,128)S(1)}, u32[]{:S(2)}, u32[]{:S(2)}) %collective-permute-start.25) | collective-permute-done | bytes 131104 | tf_op jit(solution)/shard_map/ppermute | solution.py:226
  73.2 0.7 collective-permute-start.27
  74.0 0.7 pad_maximum_fusion
  74.7 0.0 collective-permute-done.26
  74.7 0.2 collective-permute-done.27
  74.9 0.7 fusion.12
  (21 shorter events, 0.4 us)
Async XLA Ops:
  4.4 11.0 %collective-permute-start = (f32[6,64,256]{2,1,0:T(8,128)S(1)}, f32[6,64,256]{2,1,0:T(8,128)S(1)}, u32[]{:S(2)}, u32[]{:S(2)}) collective-permute-start(f32[6,64,256]{2,1,0:T(8,128)S(1)} %get-tuple-element.33), channel_id=1, source_target_pairs={{0,1},{1,0},{2,3},{3,2},{4,5},{5,4},{6,7},{7,6},{8,9},{9,8},{10,11... | collective-permute-start | bytes 1179656 | tf_op jit(solution)/shard_map/ppermute | solution.py:224
  7.7 1.5 %collective-permute-start.1 = (f32[2,64,256]{2,1,0:T(8,128)S(1)}, f32[2,64,256]{2,1,0:T(8,128)S(1)}, u32[]{:S(2)}, u32[]{:S(2)}) collective-permute-start(f32[2,64,256]{2,1,0:T(8,128)S(1)} %get-tuple-element.35), channel_id=1, source_target_pairs={{0,1},{1,0},{2,3},{3,2},{4,5},{5,4},{6,7},{7,6},{8,9},{9,8},{10,11... | collective-permute-start | bytes 393224 | tf_op jit(solution)/shard_map/ppermute | solution.py:224
  7.8 11.4 %collective-permute-start.7 = (f32[6,64,256]{2,1,0:T(8,128)S(1)}, f32[6,64,256]{2,1,0:T(8,128)S(1)}, u32[]{:S(2)}, u32[]{:S(2)}) collective-permute-start(f32[6,64,256]{2,1,0:T(8,128)S(1)} %get-tuple-element.40), channel_id=1, source_target_pairs={{0,1},{1,0},{2,3},{3,2},{4,5},{5,4},{6,7},{7,6},{8,9},{9,8},{10,11... | collective-permute-start | bytes 1179656 | tf_op jit(solution)/shard_map/ppermute | solution.py:224
  8.2 5.3 %collective-permute-start.8 = (f32[2,64,256]{2,1,0:T(8,128)S(1)}, f32[2,64,256]{2,1,0:T(8,128)S(1)}, u32[]{:S(2)}, u32[]{:S(2)}) collective-permute-start(f32[2,64,256]{2,1,0:T(8,128)S(1)} %get-tuple-element.42), channel_id=1, source_target_pairs={{0,1},{1,0},{2,3},{3,2},{4,5},{5,4},{6,7},{7,6},{8,9},{9,8},{10,11... | collective-permute-start | bytes 393224 | tf_op jit(solution)/shard_map/ppermute | solution.py:224
  9.2 30.2 %copy-start = (f32[2,128,256]{2,1,0:T(8,128)S(1)}, f32[2,128,256]{2,1,0:T(8,128)}, u32[]{:S(2)}) copy-start(f32[2,128,256]{2,1,0:T(8,128)} %right_sides.5) | copy-start | bytes 786436
  9.2 6.2 %collective-permute-start.2 = (f32[2,64,256]{2,1,0:T(8,128)S(1)}, f32[2,64,256]{2,1,0:T(8,128)S(1)}, u32[]{:S(2)}, u32[]{:S(2)}) collective-permute-start(f32[2,64,256]{2,1,0:T(8,128)S(1)} %add.90), channel_id=1, source_target_pairs={{0,3},{1,14},{2,1},{3,4},{4,7},{5,2},{6,5},{7,8},{8,11},{9,6},{10,... | collective-permute-start | bytes 393224 | tf_op jit(solution)/shard_map/ppermute | solution.py:225
  13.5 5.7 %collective-permute-start.9 = (f32[2,64,256]{2,1,0:T(8,128)S(1)}, f32[2,64,256]{2,1,0:T(8,128)S(1)}, u32[]{:S(2)}, u32[]{:S(2)}) collective-permute-start(f32[2,64,256]{2,1,0:T(8,128)S(1)} %add.97), channel_id=1, source_target_pairs={{0,3},{1,14},{2,1},{3,4},{4,7},{5,2},{6,5},{7,8},{8,11},{9,6},{10,... | collective-permute-start | bytes 393224 | tf_op jit(solution)/shard_map/ppermute | solution.py:225
  15.4 5.7 %collective-permute-start.3 = (f32[2,64,256]{2,1,0:T(8,128)S(1)}, f32[2,64,256]{2,1,0:T(8,128)S(1)}, u32[]{:S(2)}, u32[]{:S(2)}) collective-permute-start(f32[2,64,256]{2,1,0:T(8,128)S(1)} %fusion.9), channel_id=1, source_target_pairs={{0,3},{1,14},{2,1},{3,4},{4,7},{5,2},{6,5},{7,8},{8,11},{9,6},{10,... | collective-permute-start | bytes 393224 | tf_op jit(solution)/shard_map/ppermute | solution.py:225
  19.2 5.7 %collective-permute-start.10 = (f32[2,64,256]{2,1,0:T(8,128)S(1)}, f32[2,64,256]{2,1,0:T(8,128)S(1)}, u32[]{:S(2)}, u32[]{:S(2)}) collective-permute-start(f32[2,64,256]{2,1,0:T(8,128)S(1)} %fusion.6), channel_id=1, source_target_pairs={{0,3},{1,14},{2,1},{3,4},{4,7},{5,2},{6,5},{7,8},{8,11},{9,6},{10,... | collective-permute-start | bytes 393224 | tf_op jit(solution)/shard_map/ppermute | solution.py:225
  21.1 5.7 %collective-permute-start.4 = (f32[2,64,256]{2,1,0:T(8,128)S(1)}, f32[2,64,256]{2,1,0:T(8,128)S(1)}, u32[]{:S(2)}, u32[]{:S(2)}) collective-permute-start(f32[2,64,256]{2,1,0:T(8,128)S(1)} %fusion.10), channel_id=1, source_target_pairs={{0,3},{1,14},{2,1},{3,4},{4,7},{5,2},{6,5},{7,8},{8,11},{9,6},{10,... | collective-permute-start | bytes 393224 | tf_op jit(solution)/shard_map/ppermute | solution.py:225
  24.9 6.6 %collective-permute-start.11 = (f32[2,64,256]{2,1,0:T(8,128)S(1)}, f32[2,64,256]{2,1,0:T(8,128)S(1)}, u32[]{:S(2)}, u32[]{:S(2)}) collective-permute-start(f32[2,64,256]{2,1,0:T(8,128)S(1)} %fusion.7), channel_id=1, source_target_pairs={{0,3},{1,14},{2,1},{3,4},{4,7},{5,2},{6,5},{7,8},{8,11},{9,6},{10,... | collective-permute-start | bytes 393224 | tf_op jit(solution)/shard_map/ppermute | solution.py:225
  26.9 10.1 %collective-permute-start.5 = (f32[2,64,256]{2,1,0:T(8,128)S(1)}, f32[2,64,256]{2,1,0:T(8,128)S(1)}, u32[]{:S(2)}, u32[]{:S(2)}) collective-permute-start(f32[2,64,256]{2,1,0:T(8,128)S(1)} %fusion.11), channel_id=1, source_target_pairs={{0,16},{1,30},{2,17},{3,19},{4,20},{5,18},{6,21},{7,23},{8,24},{9,... | collective-permute-start | bytes 393224 | tf_op jit(solution)/shard_map/ppermute | solution.py:226
  31.6 7.8 %collective-permute-start.12 = (f32[2,64,256]{2,1,0:T(8,128)S(1)}, f32[2,64,256]{2,1,0:T(8,128)S(1)}, u32[]{:S(2)}, u32[]{:S(2)}) collective-permute-start(f32[2,64,256]{2,1,0:T(8,128)S(1)} %fusion.8), channel_id=1, source_target_pairs={{0,16},{1,30},{2,17},{3,19},{4,20},{5,18},{6,21},{7,23},{8,24},{9,... | collective-permute-start | bytes 393224 | tf_op jit(solution)/shard_map/ppermute | solution.py:226
  36.9 2.4 %collective-permute-start.6 = (f32[64,256]{1,0:T(8,128)S(1)}, f32[64,256]{1,0:T(8,128)S(1)}, u32[]{:S(2)}, u32[]{:S(2)}) collective-permute-start(f32[64,256]{1,0:T(8,128)S(1)} %slice_bitcast_fusion.5), channel_id=1, source_target_pairs={{0,1},{1,0},{2,3},{3,2},{4,5},{5,4},{6,7},{7,6},{8,9},{9,8},{10,11... | collective-permute-start | bytes 196616 | tf_op jit(solution)/shard_map/ppermute | solution.py:224
  39.4 1.3 %collective-permute-start.13 = (f32[64,256]{1,0:T(8,128)S(1)}, f32[64,256]{1,0:T(8,128)S(1)}, u32[]{:S(2)}, u32[]{:S(2)}) collective-permute-start(f32[64,256]{1,0:T(8,128)S(1)} %slice_bitcast_fusion.4), channel_id=1, source_target_pairs={{0,1},{1,0},{2,3},{3,2},{4,5},{5,4},{6,7},{7,6},{8,9},{9,8},{10,11... | collective-permute-start | bytes 196616 | tf_op jit(solution)/shard_map/ppermute | solution.py:224
  42.8 7.0 %collective-permute-start.14 = (f32[6,64,256]{2,1,0:T(8,128)S(1)}, f32[6,64,256]{2,1,0:T(8,128)S(1)}, u32[]{:S(2)}, u32[]{:S(2)}) collective-permute-start(f32[6,64,256]{2,1,0:T(8,128)S(1)} %get-tuple-element.47), channel_id=1, source_target_pairs={{0,1},{1,0},{2,3},{3,2},{4,5},{5,4},{6,7},{7,6},{8,9},{9,8},{10,11... | collective-permute-start | bytes 1179656 | tf_op jit(solution)/shard_map/ppermute | solution.py:224
  43.3 1.7 %collective-permute-start.15 = (f32[2,64,256]{2,1,0:T(8,128)S(1)}, f32[2,64,256]{2,1,0:T(8,128)S(1)}, u32[]{:S(2)}, u32[]{:S(2)}) collective-permute-start(f32[2,64,256]{2,1,0:T(8,128)S(1)} %get-tuple-element.49), channel_id=1, source_target_pairs={{0,1},{1,0},{2,3},{3,2},{4,5},{5,4},{6,7},{7,6},{8,9},{9,8},{10,11... | collective-permute-start | bytes 393224 | tf_op jit(solution)/shard_map/ppermute | solution.py:224
  43.5 9.9 %collective-permute-start.20 = (f32[6,64,256]{2,1,0:T(8,128)S(1)}, f32[6,64,256]{2,1,0:T(8,128)S(1)}, u32[]{:S(2)}, u32[]{:S(2)}) collective-permute-start(f32[6,64,256]{2,1,0:T(8,128)S(1)} %get-tuple-element.51), channel_id=1, source_target_pairs={{0,1},{1,0},{2,3},{3,2},{4,5},{5,4},{6,7},{7,6},{8,9},{9,8},{10,11... | collective-permute-start | bytes 1179656 | tf_op jit(solution)/shard_map/ppermute | solution.py:224
  43.8 4.0 %collective-permute-start.21 = (f32[2,64,256]{2,1,0:T(8,128)S(1)}, f32[2,64,256]{2,1,0:T(8,128)S(1)}, u32[]{:S(2)}, u32[]{:S(2)}) collective-permute-start(f32[2,64,256]{2,1,0:T(8,128)S(1)} %get-tuple-element.53), channel_id=1, source_target_pairs={{0,1},{1,0},{2,3},{3,2},{4,5},{5,4},{6,7},{7,6},{8,9},{9,8},{10,11... | collective-permute-start | bytes 393224 | tf_op jit(solution)/shard_map/ppermute | solution.py:224
  45.0 4.8 %collective-permute-start.16 = (f32[2,64,256]{2,1,0:T(8,128)S(1)}, f32[2,64,256]{2,1,0:T(8,128)S(1)}, u32[]{:S(2)}, u32[]{:S(2)}) collective-permute-start(f32[2,64,256]{2,1,0:T(8,128)S(1)} %add.104), channel_id=1, source_target_pairs={{0,3},{1,14},{2,1},{3,4},{4,7},{5,2},{6,5},{7,8},{8,11},{9,6},{10,... | collective-permute-start | bytes 393224 | tf_op jit(solution)/shard_map/ppermute | solution.py:225
  47.8 5.7 %collective-permute-start.22 = (f32[2,64,256]{2,1,0:T(8,128)S(1)}, f32[2,64,256]{2,1,0:T(8,128)S(1)}, u32[]{:S(2)}, u32[]{:S(2)}) collective-permute-start(f32[2,64,256]{2,1,0:T(8,128)S(1)} %add.111), channel_id=1, source_target_pairs={{0,3},{1,14},{2,1},{3,4},{4,7},{5,2},{6,5},{7,8},{8,11},{9,6},{10,... | collective-permute-start | bytes 393224 | tf_op jit(solution)/shard_map/ppermute | solution.py:225
  49.8 5.7 %collective-permute-start.17 = (f32[2,64,256]{2,1,0:T(8,128)S(1)}, f32[2,64,256]{2,1,0:T(8,128)S(1)}, u32[]{:S(2)}, u32[]{:S(2)}) collective-permute-start(f32[2,64,256]{2,1,0:T(8,128)S(1)} %fusion.3), channel_id=1, source_target_pairs={{0,3},{1,14},{2,1},{3,4},{4,7},{5,2},{6,5},{7,8},{8,11},{9,6},{10,... | collective-permute-start | bytes 393224 | tf_op jit(solution)/shard_map/ppermute | solution.py:225
  53.5 5.7 %collective-permute-start.23 = (f32[2,64,256]{2,1,0:T(8,128)S(1)}, f32[2,64,256]{2,1,0:T(8,128)S(1)}, u32[]{:S(2)}, u32[]{:S(2)}) collective-permute-start(f32[2,64,256]{2,1,0:T(8,128)S(1)} %fusion), channel_id=1, source_target_pairs={{0,3},{1,14},{2,1},{3,4},{4,7},{5,2},{6,5},{7,8},{8,11},{9,6},{10,... | collective-permute-start | bytes 393224 | tf_op jit(solution)/shard_map/ppermute | solution.py:225
  55.5 5.7 %collective-permute-start.18 = (f32[2,64,256]{2,1,0:T(8,128)S(1)}, f32[2,64,256]{2,1,0:T(8,128)S(1)}, u32[]{:S(2)}, u32[]{:S(2)}) collective-permute-start(f32[2,64,256]{2,1,0:T(8,128)S(1)} %fusion.4), channel_id=1, source_target_pairs={{0,3},{1,14},{2,1},{3,4},{4,7},{5,2},{6,5},{7,8},{8,11},{9,6},{10,... | collective-permute-start | bytes 393224 | tf_op jit(solution)/shard_map/ppermute | solution.py:225
  59.2 4.5 %collective-permute-start.24 = (f32[2,64,256]{2,1,0:T(8,128)S(1)}, f32[2,64,256]{2,1,0:T(8,128)S(1)}, u32[]{:S(2)}, u32[]{:S(2)}) collective-permute-start(f32[2,64,256]{2,1,0:T(8,128)S(1)} %fusion.1), channel_id=1, source_target_pairs={{0,3},{1,14},{2,1},{3,4},{4,7},{5,2},{6,5},{7,8},{8,11},{9,6},{10,... | collective-permute-start | bytes 393224 | tf_op jit(solution)/shard_map/ppermute | solution.py:225
  61.2 9.0 %collective-permute-start.19 = (f32[2,64,256]{2,1,0:T(8,128)S(1)}, f32[2,64,256]{2,1,0:T(8,128)S(1)}, u32[]{:S(2)}, u32[]{:S(2)}) collective-permute-start(f32[2,64,256]{2,1,0:T(8,128)S(1)} %fusion.5), channel_id=1, source_target_pairs={{0,16},{1,30},{2,17},{3,19},{4,20},{5,18},{6,21},{7,23},{8,24},{9,... | collective-permute-start | bytes 393224 | tf_op jit(solution)/shard_map/ppermute | solution.py:226
  63.7 9.5 %collective-permute-start.25 = (f32[2,64,256]{2,1,0:T(8,128)S(1)}, f32[2,64,256]{2,1,0:T(8,128)S(1)}, u32[]{:S(2)}, u32[]{:S(2)}) collective-permute-start(f32[2,64,256]{2,1,0:T(8,128)S(1)} %fusion.2), channel_id=1, source_target_pairs={{0,16},{1,30},{2,17},{3,19},{4,20},{5,18},{6,21},{7,23},{8,24},{9,... | collective-permute-start | bytes 393224 | tf_op jit(solution)/shard_map/ppermute | solution.py:226
  70.2 4.5 %collective-permute-start.26 = (f32[64,256]{1,0:T(8,128)S(1)}, f32[64,256]{1,0:T(8,128)S(1)}, u32[]{:S(2)}, u32[]{:S(2)}) collective-permute-start(f32[64,256]{1,0:T(8,128)S(1)} %get-tuple-element.54), channel_id=1, source_target_pairs={{0,1},{1,0},{2,3},{3,2},{4,5},{5,4},{6,7},{7,6},{8,9},{9,8},{10,11... | collective-permute-start | bytes 196616 | tf_op jit(solution)/shard_map/ppermute | solution.py:224
  73.2 1.6 %collective-permute-start.27 = (f32[64,256]{1,0:T(8,128)S(1)}, f32[64,256]{1,0:T(8,128)S(1)}, u32[]{:S(2)}, u32[]{:S(2)}) collective-permute-start(f32[64,256]{1,0:T(8,128)S(1)} %get-tuple-element.56), channel_id=1, source_target_pairs={{0,1},{1,0},{2,3},{3,2},{4,5},{5,4},{6,7},{7,6},{8,9},{9,8},{10,11... | collective-permute-start | bytes 196616 | tf_op jit(solution)/shard_map/ppermute | solution.py:224
